TPU v7x, 32 devices: a whole 2x2x4 slice. The times are simulated.
32 devices in a mesh: seq: 8 (over z, x), tp: 4 (over y, core).
Axes of the slice: x: 2, y: 2, z: 4, core: 2. Of those that a mesh axis runs over, the one named last changes fastest.
Arguments:
- inputs: bfloat16 [1024, 4, 2048], P(('seq', 'tp')), may hold values from -6 to 6
- documents: int32 [4, 1024], replicated, may hold values from 0 to 3, as said below
- query_weight: bfloat16 [2048, 2048], P(None, 'tp'), may hold values from -0.125 to 0.125
- key_weight: bfloat16 [2048, 2048], P(None, 'tp'), may hold values from -0.125 to 0.125
- value_weight: bfloat16 [2048, 2048], P(None, 'tp'), may hold values from -0.125 to 0.125
- output_weight: bfloat16 [2048, 2048], P('tp'), may hold values from -0.125 to 0.125
- query_gain: float32 [2048], P('tp'), may hold values from 0.25 to 1.75
- key_gain: float32 [2048], P('tp'), may hold values from 0.25 to 1.75
- attention_gain: float32 [2048], replicated, may hold values from 0.5 to 1.5
- gate_weight: bfloat16 [2048, 8192], P(None, 'tp'), may hold values from -0.125 to 0.125
- up_weight: bfloat16 [2048, 8192], P(None, 'tp'), may hold values from -0.125 to 0.125
- down_weight: bfloat16 [8192, 2048], P('tp'), may hold values from -0.0625 to 0.0625
- feed_gain: float32 [2048], replicated, may hold values from 0.5 to 1.5
- cotangent: bfloat16 [1024, 4, 2048], P(('seq', 'tp')), may hold values from -6 to 6
Outputs:
- layer_out: float32 [1024, 4, 2048], P(('seq', 'tp'))
- input_grad: float32 [1024, 4, 2048], P(('seq', 'tp'))
- grad_query: float32 [2048, 2048], P('seq', 'tp')
- grad_key: float32 [2048, 2048], P('seq', 'tp')
- grad_value: float32 [2048, 2048], P('seq', 'tp')
- grad_output: float32 [2048, 2048], P('tp', 'seq')
- grad_gate: float32 [2048, 8192], P('seq', 'tp')
- grad_up: float32 [2048, 8192], P('seq', 'tp')
- grad_down: float32 [8192, 2048], P('tp', 'seq')
- grad_query_gain: float32 [2048], P('seq')
- grad_key_gain: float32 [2048], P('seq')
- grad_attention_gain: float32 [2048], P('seq')
- grad_feed_gain: float32 [2048], P('seq')
Inputs may be any that keep to these rules, and one draw needn't show every extreme that they name: In each sequence the ids never fall and each of its documents covers consecutive tokens; one sequence, which one drawn from the seed, is a single document of all 1024 tokens.
All inputs are finite; a program needn't handle non-finite values.
Results may differ from a plain program's by a relative error of at most 0.025.
Values may be sent and summed in bfloat16 or wider, within the bound.
No kernel may reach another device: no remote copies, remote signals or barrier semaphores. Data moves between devices by JAX's collectives and lax.ppermute only.
A program may use at most 320 MiB of HBM per device.

v0:
```python
import jax
import jax.numpy as jnp
from jax import lax
from jax.sharding import PartitionSpec as P

HEAD = 128


EPS = 1e-06
THETA = 500000.0
NEGATIVE = -1e30


def rope_tables(positions, head_size):
    half_size = head_size // 2
    rates = jnp.exp(-jnp.log(THETA) * (2.0 * jnp.arange(half_size, dtype=jnp.float32) / head_size))
    angles = positions.astype(jnp.float32)[..., None] * rates
    cosine = jnp.cos(angles)
    sine_part = jnp.sin(angles)
    return (
        jnp.concatenate([cosine, cosine], axis=-1)[..., None, :],
        jnp.concatenate([sine_part, sine_part], axis=-1)[..., None, :],
    )


def rotate(tensor, cosine, sine_part):
    half_size = tensor.shape[-1] // 2
    turned = jnp.concatenate([-tensor[..., half_size:], tensor[..., :half_size]], axis=-1)
    return tensor * cosine + turned * sine_part


def unrotate(grad_in, cosine, sine_part):
    half_size = grad_in.shape[-1] // 2
    scaled = grad_in * sine_part
    return grad_in * cosine + jnp.concatenate(
        [scaled[..., half_size:], -scaled[..., :half_size]], axis=-1
    )


def rms_scale(tensor):
    return lax.rsqrt(jnp.mean(tensor * tensor, axis=-1, keepdims=True) + EPS)


def norm_back(tensor, inverse, gain, grad_in):
    weighted = grad_in * gain
    return inverse * weighted - tensor * inverse**3 * jnp.mean(
        weighted * tensor, axis=-1, keepdims=True
    )


def cycle_values(key_low, value_low):
    return (
        lax.all_gather(jnp.transpose(key_low, (1, 0, 2)), "seq", axis=1, tiled=True),
        lax.all_gather(jnp.transpose(value_low, (1, 0, 2)), "seq", axis=1, tiled=True),
    )


def allowed_mask(query_docs, key_docs, query_first, key_first):
    query_places = query_first + jnp.arange(query_docs.shape[0], dtype=jnp.int32)
    key_places = key_first + jnp.arange(key_docs.shape[0], dtype=jnp.int32)
    return (query_docs[:, None] == key_docs[None, :]) & (
        key_places[None, :] <= query_places[:, None]
    )


def local(
    inputs,
    documents,
    query_weight,
    key_weight,
    value_weight,
    output_weight,
    query_gain,
    key_gain,
    attention_gain,
    gate_weight,
    up_weight,
    down_weight,
    feed_gain,
    cotangent,
):
    row_count, seq_count, model_width = inputs.shape
    heads_width = query_weight.shape[1]
    local_heads = heads_width // HEAD
    score_scale = HEAD ** (-0.5)
    seq_index = lax.axis_index("seq")
    tp_index = lax.axis_index("tp")
    total_length = documents.shape[1]
    f32 = jnp.float32
    bf16 = jnp.bfloat16
    whole = lax.all_gather(inputs, "tp", axis=0, tiled=True)
    here_length = whole.shape[0]
    queries = jnp.einsum("tsd,dh->tsh", whole, query_weight, preferred_element_type=f32)
    keys_proj = jnp.einsum("tsd,dh->tsh", whole, key_weight, preferred_element_type=f32)
    values_proj = jnp.einsum("tsd,dh->tsh", whole, value_weight, preferred_element_type=f32)
    query_sq, key_sq = lax.psum(
        (jnp.sum(queries * queries, axis=-1), jnp.sum(keys_proj * keys_proj, axis=-1)), "tp"
    )
    query_inv = lax.rsqrt(query_sq / model_width + EPS)[..., None]
    key_inv = lax.rsqrt(key_sq / model_width + EPS)[..., None]
    first_row = seq_index * here_length
    own_docs = lax.dynamic_slice_in_dim(documents, first_row, here_length, 1)
    starts = jnp.sum((documents[:, None, :] < own_docs[:, :, None]).astype(jnp.int32), axis=-1)
    positions = (first_row + jnp.arange(here_length, dtype=jnp.int32))[:, None] - starts.T
    cosine, sine_part = rope_tables(positions, HEAD)

    def heads_of(tensor):
        return tensor.reshape(here_length, seq_count, local_heads, HEAD)

    query_low = rotate(heads_of(queries * query_inv * query_gain), cosine, sine_part).astype(bf16)
    key_low = rotate(heads_of(keys_proj * key_inv * key_gain), cosine, sine_part).astype(bf16)
    key_low = key_low.reshape(here_length, seq_count, heads_width)
    value_low = values_proj.astype(bf16)
    key_cycle, value_cycle = cycle_values(key_low, value_low)
    query_seq = jnp.transpose(query_low, (1, 0, 2, 3))

    def keys_in_reach(key_part, value_part):
        return (
            key_part.reshape(total_length, local_heads, HEAD),
            value_part.reshape(total_length, local_heads, HEAD),
        )

    def scores_of(query_part, key_heads, query_docs, key_docs, first_query, first_key):
        scores = (
            jnp.einsum("qhd,khd->hqk", query_part, key_heads, preferred_element_type=f32)
            * score_scale
        )
        return jnp.where(
            allowed_mask(query_docs, key_docs, first_query, first_key)[None], scores, NEGATIVE
        )

    def attend(pieces):
        query_part, key_part, value_part, own_part, doc_row = pieces
        key_heads, value_heads = keys_in_reach(key_part, value_part)
        scores = scores_of(query_part, key_heads, own_part, doc_row, first_row, 0)
        top_score = jnp.max(scores, axis=-1, keepdims=True)
        spread = jnp.exp(scores - top_score)
        total_sum = jnp.sum(spread, axis=-1, keepdims=True)
        weights = (spread / total_sum).astype(bf16)
        mixed_part = jnp.einsum("hqk,khd->qhd", weights, value_heads, preferred_element_type=f32)
        return (mixed_part, (top_score + jnp.log(total_sum))[..., 0])

    attended, log_total = lax.map(attend, (query_seq, key_cycle, value_cycle, own_docs, documents))
    mixed_low = (
        jnp.transpose(attended, (1, 0, 2, 3))
        .reshape(here_length, seq_count, heads_width)
        .astype(bf16)
    )
    part = mixed_low
    branch = lax.psum_scatter(
        jnp.einsum("tsh,hd->tsd", part, output_weight, preferred_element_type=f32).astype(
            jnp.bfloat16
        ),
        "tp",
        scatter_dimension=0,
        tiled=True,
    ).astype(jnp.float32)
    attn_inv = rms_scale(branch)
    hidden = inputs.astype(f32) + branch * attn_inv * attention_gain
    hidden_whole = lax.all_gather(hidden.astype(bf16), "tp", axis=0, tiled=True)
    gate_value = jnp.einsum("tsd,df->tsf", hidden_whole, gate_weight, preferred_element_type=f32)
    up_value = jnp.einsum("tsd,df->tsf", hidden_whole, up_weight, preferred_element_type=f32)
    sigmoid_value = jax.nn.sigmoid(gate_value)
    act_low = (gate_value * sigmoid_value * up_value).astype(bf16)
    part = act_low
    down_value = lax.psum_scatter(
        jnp.einsum("tsf,fd->tsd", part, down_weight, preferred_element_type=f32).astype(
            jnp.bfloat16
        ),
        "tp",
        scatter_dimension=0,
        tiled=True,
    ).astype(jnp.float32)
    feed_inv = rms_scale(down_value)
    layer_out = hidden + down_value * feed_inv * feed_gain
    grad_top = cotangent.astype(f32)
    feed_gain_term = jnp.sum(grad_top * down_value * feed_inv, axis=(0, 1))
    down_grad_low = norm_back(down_value, feed_inv, feed_gain, grad_top).astype(bf16)
    down_whole = lax.all_gather(down_grad_low, "tp", axis=0, tiled=True)
    act_grad = jnp.einsum("tsd,fd->tsf", down_whole, down_weight, preferred_element_type=f32)
    down_term = jnp.einsum("tsd,tsf->df", down_whole, act_low, preferred_element_type=f32)
    up_grad_low = (act_grad * gate_value * sigmoid_value).astype(bf16)
    gate_grad_low = (
        act_grad * up_value * sigmoid_value * (1.0 + gate_value * (1.0 - sigmoid_value))
    ).astype(bf16)
    gate_term = jnp.einsum("tsd,tsf->df", hidden_whole, gate_grad_low, preferred_element_type=f32)
    up_term = jnp.einsum("tsd,tsf->df", hidden_whole, up_grad_low, preferred_element_type=f32)
    hidden_grad = grad_top + lax.psum_scatter(
        (
            jnp.einsum("tsf,df->tsd", gate_grad_low, gate_weight, preferred_element_type=f32)
            + jnp.einsum("tsf,df->tsd", up_grad_low, up_weight, preferred_element_type=f32)
        ).astype(jnp.bfloat16),
        "tp",
        scatter_dimension=0,
        tiled=True,
    ).astype(jnp.float32)
    attention_gain_term = jnp.sum(hidden_grad * branch * attn_inv, axis=(0, 1))
    branch_grad_low = norm_back(branch, attn_inv, attention_gain, hidden_grad).astype(bf16)
    branch_whole = lax.all_gather(branch_grad_low, "tp", axis=0, tiled=True)
    out_term = jnp.einsum("tsd,tsh->dh", branch_whole, mixed_low, preferred_element_type=f32)
    mixed_grad_low = jnp.einsum(
        "tsd,hd->tsh", branch_whole, output_weight, preferred_element_type=f32
    ).astype(bf16)
    grad_seq = jnp.transpose(
        mixed_grad_low.reshape(here_length, seq_count, local_heads, HEAD), (1, 0, 2, 3)
    )
    delta_own = jnp.transpose(jnp.sum(grad_seq.astype(f32) * attended, axis=-1), (0, 2, 1))
    key_cycle, value_cycle = cycle_values(key_low, value_low)

    def query_back(pieces):
        query_part, key_part, value_part, own_part, doc_row, grad_part, log_part, delta_part = (
            pieces
        )
        key_heads, value_heads = keys_in_reach(key_part, value_part)
        scores = scores_of(query_part, key_heads, own_part, doc_row, first_row, 0)
        weights = jnp.exp(scores - log_part[..., None])
        weight_grad = jnp.einsum("qhd,khd->hqk", grad_part, value_heads, preferred_element_type=f32)
        score_grad = (weights * (weight_grad - delta_part[:, :, None]) * score_scale).astype(bf16)
        query_grad = jnp.einsum("hqk,khd->qhd", score_grad, key_heads, preferred_element_type=f32)
        key_grad = jnp.einsum("hqk,qhd->khd", score_grad, query_part, preferred_element_type=f32)
        value_grad = jnp.einsum(
            "hqk,qhd->khd", weights.astype(bf16), grad_part, preferred_element_type=f32
        )
        return (
            query_grad,
            key_grad.reshape(total_length, heads_width),
            value_grad.reshape(total_length, heads_width),
        )

    query_grads, key_full, value_full = lax.map(
        query_back,
        (query_seq, key_cycle, value_cycle, own_docs, documents, grad_seq, log_total, delta_own),
    )
    key_own, value_own = (
        lax.psum_scatter(
            key_full.astype(jnp.bfloat16), "seq", scatter_dimension=1, tiled=True
        ).astype(jnp.float32),
        lax.psum_scatter(
            value_full.astype(jnp.bfloat16), "seq", scatter_dimension=1, tiled=True
        ).astype(jnp.float32),
    )
    value_grad_low = jnp.transpose(value_own, (1, 0, 2)).astype(bf16)
    query_rot = unrotate(jnp.transpose(query_grads, (1, 0, 2, 3)), cosine, sine_part)
    query_rot = query_rot.reshape(here_length, seq_count, heads_width)
    key_rot = unrotate(heads_of(jnp.transpose(key_own, (1, 0, 2))), cosine, sine_part)
    key_rot = key_rot.reshape(here_length, seq_count, heads_width)
    query_gain_term = jnp.sum(query_rot * queries * query_inv, axis=(0, 1))
    key_gain_term = jnp.sum(key_rot * keys_proj * key_inv, axis=(0, 1))

    def placed(term):
        return lax.dynamic_update_slice(
            jnp.zeros((model_width,), f32), term, (tp_index * heads_width,)
        )

    query_dot, key_dot, query_gain_sum, key_gain_sum, attention_gain_sum, feed_gain_sum = (
        lax.psum(
            jnp.sum(query_rot * query_gain * queries, axis=-1).astype(jnp.bfloat16), "tp"
        ).astype(jnp.float32),
        lax.psum(
            jnp.sum(key_rot * key_gain * keys_proj, axis=-1).astype(jnp.bfloat16), "tp"
        ).astype(jnp.float32),
        lax.psum(placed(query_gain_term).astype(jnp.bfloat16), "tp").astype(jnp.float32),
        lax.psum(placed(key_gain_term).astype(jnp.bfloat16), "tp").astype(jnp.float32),
        lax.psum(attention_gain_term.astype(jnp.bfloat16), "tp").astype(jnp.float32),
        lax.psum(feed_gain_term.astype(jnp.bfloat16), "tp").astype(jnp.float32),
    )
    query_grad_low = (
        query_inv * query_gain * query_rot
        - queries * query_inv**3 * (query_dot / model_width)[..., None]
    ).astype(bf16)
    key_grad_low = (
        key_inv * key_gain * key_rot - keys_proj * key_inv**3 * (key_dot / model_width)[..., None]
    ).astype(bf16)
    query_term = jnp.einsum("tsd,tsh->dh", whole, query_grad_low, preferred_element_type=f32)
    key_term = jnp.einsum("tsd,tsh->dh", whole, key_grad_low, preferred_element_type=f32)
    value_term = jnp.einsum("tsd,tsh->dh", whole, value_grad_low, preferred_element_type=f32)
    query_part = query_grad_low
    key_part = key_grad_low
    value_part = value_grad_low
    input_grad = hidden_grad + lax.psum_scatter(
        (
            jnp.einsum("tsh,dh->tsd", query_part, query_weight, preferred_element_type=f32)
            + jnp.einsum("tsh,dh->tsd", key_part, key_weight, preferred_element_type=f32)
            + jnp.einsum("tsh,dh->tsd", value_part, value_weight, preferred_element_type=f32)
        ).astype(jnp.bfloat16),
        "tp",
        scatter_dimension=0,
        tiled=True,
    ).astype(jnp.float32)
    summed = (
        lax.psum_scatter(
            query_term.astype(jnp.bfloat16), "seq", scatter_dimension=0, tiled=True
        ).astype(jnp.float32),
        lax.psum_scatter(
            key_term.astype(jnp.bfloat16), "seq", scatter_dimension=0, tiled=True
        ).astype(jnp.float32),
        lax.psum_scatter(
            value_term.astype(jnp.bfloat16), "seq", scatter_dimension=0, tiled=True
        ).astype(jnp.float32),
        lax.psum_scatter(
            out_term.astype(jnp.bfloat16), "seq", scatter_dimension=0, tiled=True
        ).astype(jnp.float32),
        lax.psum_scatter(
            gate_term.astype(jnp.bfloat16), "seq", scatter_dimension=0, tiled=True
        ).astype(jnp.float32),
        lax.psum_scatter(
            up_term.astype(jnp.bfloat16), "seq", scatter_dimension=0, tiled=True
        ).astype(jnp.float32),
        lax.psum_scatter(
            down_term.astype(jnp.bfloat16), "seq", scatter_dimension=0, tiled=True
        ).astype(jnp.float32),
        lax.psum_scatter(
            query_gain_sum.astype(jnp.bfloat16), "seq", scatter_dimension=0, tiled=True
        ).astype(jnp.float32),
        lax.psum_scatter(
            key_gain_sum.astype(jnp.bfloat16), "seq", scatter_dimension=0, tiled=True
        ).astype(jnp.float32),
        lax.psum_scatter(
            attention_gain_sum.astype(jnp.bfloat16), "seq", scatter_dimension=0, tiled=True
        ).astype(jnp.float32),
        lax.psum_scatter(
            feed_gain_sum.astype(jnp.bfloat16), "seq", scatter_dimension=0, tiled=True
        ).astype(jnp.float32),
    )
    return (
        layer_out,
        input_grad,
        summed[0],
        summed[1],
        summed[2],
        summed[3].T,
        summed[4],
        summed[5],
        summed[6].T,
        summed[7],
        summed[8],
        summed[9],
        summed[10],
    )


def solution(mesh):
    return jax.shard_map(
        local,
        mesh=mesh,
        in_specs=(
            P(("seq", "tp"), None, None),
            P(),
            P(None, "tp"),
            P(None, "tp"),
            P(None, "tp"),
            P("tp", None),
            P("tp"),
            P("tp"),
            P(),
            P(None, "tp"),
            P(None, "tp"),
            P("tp", None),
            P(),
            P(("seq", "tp"), None, None),
        ),
        out_specs=(
            P(("seq", "tp"), None, None),
            P(("seq", "tp"), None, None),
            P("seq", "tp"),
            P("seq", "tp"),
            P("seq", "tp"),
            P("tp", "seq"),
            P("seq", "tp"),
            P("seq", "tp"),
            P("tp", "seq"),
            P("seq"),
            P("seq"),
            P("seq"),
            P("seq"),
        ),
        check_vma=False,
    )
```

profile of v0, /device:TPU:0, one launch (start us, length us, event | category | flops | bytes accessed | tf_op | source)
XLA Modules:
  0.0 1492.3 jit_solution(13780305175537699631)
XLA Ops:
  9.6 25.9 %all-gather.7.cloned.1.call-done = bf16[128,4,2048]{2,0,1:T(8,128)(2,1)} async-done(((bf16[32,4,2048]{2,0,1:T(8,128)(2,1)}), bf16[128,4,2048]{2,0,1:T(8,128)(2,1)}) %all-gather.7.cloned.1.call-update) | async-done | bytes 2097168 | tf_op jit(solution)/shard_map/all_gather | solution.py:91
  35.5 4.3 fusion.76
  43.0 3.7 multiply_reduce_fusion.5
  49.0 6.3 all-reduce.4
  75.5 37.8 %all-gather.9.cloned.1.call-done = bf16[4,1024,512]{2,1,0:T(8,128)(2,1)} async-done(((bf16[4,128,512]{2,1,0:T(8,128)(2,1)}), bf16[4,1024,512]{2,1,0:T(8,128)(2,1)}) %all-gather.9.cloned.1.call-update) | async-done | bytes 4194320 | tf_op jit(solution)/shard_map/all_gather | solution.py:54
  113.3 6.3 copy.153
  119.6 68.2 %all-gather.11.cloned.1.call-done = bf16[4,1024,512]{2,1,0:T(8,128)(2,1)} async-done(((bf16[4,128,512]{2,1,0:T(8,128)(2,1)}), bf16[4,1024,512]{2,1,0:T(8,128)(2,1)}) %all-gather.11.cloned.1.call-update) | async-done | bytes 4194320 | tf_op jit(solution)/shard_map/all_gather | solution.py:53
  187.8 6.3 copy.155
  194.1 20.1 %while.26 = (s32[]{:T(128)}, f32[4,128,4,128]{1,3,2,0:T(8,128)S(1)}, f32[4,4,128]{2,1,0:T(4,128)S(1)}, bf16[4,1024,512]{1,2,0:T(8,128)(2,1)}, s32[4,128]{1,0:T(4...) while((s32[]{:T(128)}, ...), condition=%wide.region_8.9_spmd, body=%wide.region_5.8_spmd.sunk | while | flops 275119744 | bytes 13531785 | solution.py:143
  215.3 4.2 convolution_convert_fusion
  219.5 29.8 %reduce-scatter.16.cloned.1.call-done = bf16[32,4,2048]{2,0,1:T(8,128)(2,1)} async-done(((bf16[128,4,2048]{2,0,1:T(8,128)(2,1)}), bf16[32,4,2048]{2,0,1:T(8,128)(2,1)}) %reduce-scatter.16.cloned.1.call-update) | async-done | bytes 524304 | tf_op jit(solution)/shard_map/reduce_scatter | solution.py:150
  253.0 22.5 %all-gather.13.cloned.1.call-done = bf16[128,4,2048]{2,0,1:T(8,128)(2,1)} async-done(((bf16[32,4,2048]{2,0,1:T(8,128)(2,1)}), bf16[128,4,2048]{2,0,1:T(8,128)(2,1)}) %all-gather.13.cloned.1.call-update) | async-done | bytes 2097168 | tf_op jit(solution)/shard_map/all_gather | solution.py:160
  275.6 8.6 fusion.42
  284.2 11.7 multiply_convert_fusion.3
  297.2 5.7 fusion.46
  303.0 31.5 %reduce-scatter.18.cloned.1.call-done = bf16[32,4,2048]{2,0,1:T(8,128)(2,1)} async-done(((bf16[128,4,2048]{2,0,1:T(8,128)(2,1)}), bf16[32,4,2048]{2,0,1:T(8,128)(2,1)}) %reduce-scatter.18.cloned.1.call-update) | async-done | bytes 524304 | tf_op jit(solution)/shard_map/reduce_scatter | solution.py:166
  340.1 22.5 %all-gather.15.cloned.1.call-done = bf16[128,4,2048]{2,0,1:T(8,128)(2,1)} async-done(((bf16[32,4,2048]{2,0,1:T(8,128)(2,1)}), bf16[128,4,2048]{2,0,1:T(8,128)(2,1)}) %all-gather.15.cloned.1.call-update) | async-done | bytes 2097168 | tf_op jit(solution)/shard_map/all_gather | solution.py:179
  362.6 11.9 multiply_convert_fusion.2
  374.5 8.5 fusion.36
  383.0 9.2 add_convert_fusion.1
  392.3 31.5 %reduce-scatter.20.cloned.1.call-done = bf16[32,4,2048]{2,0,1:T(8,128)(2,1)} async-done(((bf16[128,4,2048]{2,0,1:T(8,128)(2,1)}), bf16[32,4,2048]{2,0,1:T(8,128)(2,1)}) %reduce-scatter.20.cloned.1.call-update) | async-done | bytes 524304 | tf_op jit(solution)/shard_map/reduce_scatter | solution.py:188
  425.5 3.5 fusion.86
  430.9 20.9 %all-gather.17.cloned.1.call-done = bf16[128,4,2048]{2,0,1:T(8,128)(2,1)} async-done(((bf16[32,4,2048]{2,0,1:T(8,128)(2,1)}), bf16[128,4,2048]{2,0,1:T(8,128)(2,1)}) %all-gather.17.cloned.1.call-update) | async-done | bytes 2097168 | tf_op jit(solution)/shard_map/all_gather | solution.py:199
  451.8 3.5 fusion.73
  457.7 57.7 %while.27 = (s32[]{:T(128)}, f32[4,128,4,128]{1,3,2,0:T(8,128)}, bf16[4,1024,512]{2,1,0:T(8,128)(2,1)}, bf16[4,1024,512]{1,2,0:T(8,128)(2,1)}, bf16[4,1024,512]{...) while((s32[]{:T(128)}, f32[4,128,4,128]{1,3,2,0:T(8,128)}, ...), condition=%wide.region_18.19_spmd, body=%wide.region_17.18_spmd.sunk | while | flops 675676288 | bytes 26241728 | solution.py:230
  515.4 7.8 copy.193
  523.3 5.6 copy.213
  530.0 4.2 bitcast_convert_fusion.3
  534.7 10.4 bitcast_convert_fusion
  545.2 10.1 bitcast_convert_fusion.2
  555.5 10.2 bitcast_convert_fusion.1
  567.6 49.5 %reduce-scatter.40.cloned.1.call-done = bf16[128,2048]{1,0:T(8,128)(2,1)} async-done(((bf16[1024,2048]{1,0:T(8,128)(2,1)}), bf16[128,2048]{1,0:T(8,128)(2,1)}) %reduce-scatter.40.cloned.1.call-update) | async-done | bytes 524304
  619.7 89.2 %reduce-scatter.22.cloned.1.call-done = bf16[4,128,512]{2,1,0:T(8,128)(2,1)} async-done(((bf16[4,1024,512]{2,1,0:T(8,128)(2,1)}), bf16[4,128,512]{2,1,0:T(8,128)(2,1)}) %reduce-scatter.22.cloned.1.call-update) | async-done | bytes 524304 | tf_op jit(solution)/shard_map/reduce_scatter | solution.py:235
  722.1 3.0 multiply_reduce_fusion
  727.6 36.0 %all-reduce.5 = (bf16[2048]{0:T(1024)(128)(2,1)S(1)}, bf16[2048]{0:T(1024)(128)(2,1)S(1)}, bf16[2048]{0:T(1024)(128)(2,1)S(1)}, bf16[2048]{0:T(1024)(128)(2,1)S(1)}) all-reduce(bf16[2048]{0:T(1024)(128)(2,1)S(1)} %dynamic_update_slice.24, ...), channel_id=15, replica_groups=mesh['seq'=8,'tp'=4] {'seq'}, use_global_device_ids=true, to_apply=%region_35.36.clone | all-reduce | flops 8192 | bytes 32768
  763.8 5.9 all-reduce.6
  779.2 4.2 fusion.50
  784.5 4.3 fusion.49
  788.8 4.2 fusion.51
  800.1 133.1 %reduce-scatter.38.cloned.1.call-done = bf16[256,2048]{1,0:T(8,128)(2,1)} async-done(((bf16[2048,2048]{1,0:T(8,128)(2,1)}), bf16[256,2048]{1,0:T(8,128)(2,1)}) %reduce-scatter.38.cloned.1.call-update) | async-done | bytes 1048592 | tf_op jit(solution)/shard_map/reduce_scatter | solution.py:309
  933.3 2.8 convert_bitcast_fusion
  936.0 2.9 copy.177
  938.9 145.9 %reduce-scatter.34.cloned.1.call-done = bf16[256,2048]{1,0:T(8,128)(2,1)} async-done(((bf16[2048,2048]{1,0:T(8,128)(2,1)}), bf16[256,2048]{1,0:T(8,128)(2,1)}) %reduce-scatter.34.cloned.1.call-update) | async-done | bytes 1048592 | tf_op jit(solution)/shard_map/reduce_scatter | solution.py:303
  1087.6 149.2 %reduce-scatter.36.cloned.1.call-done = bf16[256,2048]{1,0:T(8,128)(2,1)} async-done(((bf16[2048,2048]{1,0:T(8,128)(2,1)}), bf16[256,2048]{1,0:T(8,128)(2,1)}) %reduce-scatter.36.cloned.1.call-update) | async-done | bytes 1048592 | tf_op jit(solution)/shard_map/reduce_scatter | solution.py:306
  1239.6 30.1 %reduce-scatter.24.cloned.1.call-done = bf16[32,4,2048]{2,0,1:T(8,128)(2,1)} async-done(((bf16[128,4,2048]{2,0,1:T(8,128)(2,1)}), bf16[32,4,2048]{2,0,1:T(8,128)(2,1)}) %reduce-scatter.24.cloned.1.call-update) | async-done | bytes 524304 | tf_op jit(solution)/shard_map/reduce_scatter | solution.py:280
  1272.7 68.8 %reduce-scatter.28.cloned.1.call-done = bf16[256,512]{0,1:T(8,128)(2,1)} async-done(((bf16[2048,512]{0,1:T(8,128)(2,1)}), bf16[256,512]{0,1:T(8,128)(2,1)}) %reduce-scatter.28.cloned.1.call-update) | async-done | bytes 262160 | tf_op jit(solution)/shard_map/reduce_scatter | solution.py:294
  1343.4 69.0 %reduce-scatter.26.cloned.1.call-done = bf16[256,512]{0,1:T(8,128)(2,1)} async-done(((bf16[2048,512]{0,1:T(8,128)(2,1)}), bf16[256,512]{0,1:T(8,128)(2,1)}) %reduce-scatter.26.cloned.1.call-update) | async-done | bytes 262160 | tf_op jit(solution)/shard_map/reduce_scatter | solution.py:291
  1414.3 69.3 %reduce-scatter.30.cloned.1.call-done = bf16[256,512]{0,1:T(8,128)(2,1)} async-done(((bf16[2048,512]{0,1:T(8,128)(2,1)}), bf16[256,512]{0,1:T(8,128)(2,1)}) %reduce-scatter.30.cloned.1.call-update) | async-done | bytes 262160 | tf_op jit(solution)/shard_map/reduce_scatter | solution.py:297
  (313 shorter events, 176.6 us)
Async XLA Ops:
  7.2 39.5 %copy-start = (bf16[2048,512]{1,0:T(8,128)(2,1)S(1)}, bf16[2048,512]{1,0:T(8,128)(2,1)}, u32[]{:S(2)}) copy-start(bf16[2048,512]{1,0:T(8,128)(2,1)} %param.20) | copy-start | bytes 6291460
  7.2 28.3 %all-gather.7.cloned.1.call-start = ((), (), s32[]{:S(2)}) async-start(), calls=%async_computation.13 | async-start | bytes 2621440 | tf_op jit(solution)/shard_map/all_gather | solution.py:91
  9.5 30.3 %copy-start.25 = (s32[4,1024]{1,0:T(4,128)S(1)}, s32[4,1024]{1,0:T(4,128)}, u32[]{:S(2)}) copy-start(s32[4,1024]{1,0:T(4,128)} %param.19) | copy-start | bytes 49156
  9.5 103.8 %all-gather.9.cloned.1.call-start = ((), (), s32[]{:S(2)}) async-start(), calls=%async_computation.14 | async-start | bytes 4718592 | tf_op jit(solution)/shard_map/all_gather | solution.py:54
  39.8 148.0 %all-gather.11.cloned.1.call-start = ((), (), s32[]{:S(2)}) async-start(), calls=%async_computation.15 | async-start | bytes 4718592 | tf_op jit(solution)/shard_map/all_gather | solution.py:53
  41.6 25.1 %copy-start.11 = (f32[128,4,128]{0,2,1:T(8,128)}, f32[128,4,128]{0,2,1:T(8,128)S(1)}, u32[]{:S(2)}) copy-start(f32[128,4,128]{0,2,1:T(8,128)S(1)} %get-tuple-element.380) | copy-start | bytes 786436
  43.0 3.7 copy-start.38
  46.7 23.9 %copy-start.1 = (f32[128,4,512]{2,0,1:T(8,128)}, f32[128,4,512]{2,0,1:T(8,128)S(1)}, u32[]{:S(2)}) copy-start(f32[128,4,512]{2,0,1:T(8,128)S(1)} %get-tuple-element.373) | copy-start | bytes 3145732
  46.7 9.7 copy-start.34
  55.8 14.8 copy-start.28
  56.4 4.9 copy-start.30
  73.2 176.1 %reduce-scatter.16.cloned.1.call-start = ((), (), s32[]{:S(2)}) async-start(), calls=%async_computation.16 | async-start | bytes 2621440 | tf_op jit(solution)/shard_map/reduce_scatter | solution.py:150
  214.2 5.2 copy-start.6
  219.5 31.1 %copy-start.26 = (f32[2048]{0:T(1024)S(1)}, f32[2048]{0:T(1024)}, u32[]{:S(2)}) copy-start(f32[2048]{0:T(1024)} %param.26) | copy-start | bytes 24580
  219.5 31.1 %copy-start.9 = (bf16[32,4,2048]{2,1,0:T(4,128)(2,1)S(1)}, bf16[32,4,2048]{2,1,0:T(4,128)(2,1)}, u32[]{:S(2)}) copy-start(bf16[32,4,2048]{2,1,0:T(4,128)(2,1)} %param.18) | copy-start | bytes 1572868
  219.5 56.1 %all-gather.13.cloned.1.call-start = ((), (), s32[]{:S(2)}) async-start(), calls=%async_computation.17 | async-start | bytes 2621440 | tf_op jit(solution)/shard_map/all_gather | solution.py:160
  252.8 81.7 %reduce-scatter.18.cloned.1.call-start = ((), (), s32[]{:S(2)}) async-start(), calls=%async_computation.18 | async-start | bytes 2621440 | tf_op jit(solution)/shard_map/reduce_scatter | solution.py:166
  275.6 8.6 copy-start.39
  275.6 21.6 %slice-start = ((s8[8388608]{0:T(1024)(128)(4,1)}), s8[4194304]{0:T(1024)(128)(4,1)S(1)}, s32[]{:S(2)}) async-start(s8[8388608]{0:T(1024)(128)(4,1)} %bitcast.296), calls=%async_computation.32 | async-start | bytes 8388608
  284.1 11.7 copy-start.41
  284.1 13.0 slice-start.1
  302.9 32.8 %copy-start.3 = (bf16[32,4,2048]{2,1,0:T(4,128)(2,1)S(1)}, bf16[32,4,2048]{2,1,0:T(4,128)(2,1)}, u32[]{:S(2)}) copy-start(bf16[32,4,2048]{2,1,0:T(4,128)(2,1)} %param.31) | copy-start | bytes 1572868
  302.9 32.8 %copy-start.27 = (f32[2048]{0:T(1024)S(1)}, f32[2048]{0:T(1024)}, u32[]{:S(2)}) copy-start(f32[2048]{0:T(1024)} %param.30) | copy-start | bytes 24580
  302.9 59.6 %all-gather.15.cloned.1.call-start = ((), (), s32[]{:S(2)}) async-start(), calls=%async_computation.19 | async-start | bytes 2621440 | tf_op jit(solution)/shard_map/all_gather | solution.py:179
  339.8 84.0 %reduce-scatter.20.cloned.1.call-start = ((), (), s32[]{:S(2)}) async-start(), calls=%async_computation.20 | async-start | bytes 2621440 | tf_op jit(solution)/shard_map/reduce_scatter | solution.py:188
  374.5 8.5 copy-start.43
  374.5 8.5 copy-start.44
  392.2 31.6 %copy-start.7 = (bf16[32,4,2048]{2,0,1:T(8,128)(2,1)S(1)}, bf16[32,4,2048]{2,0,1:T(8,128)(2,1)}, u32[]{:S(2)}) copy-start(bf16[32,4,2048]{2,0,1:T(8,128)(2,1)} %reduce-scatter.16.cloned.1.call-done) | copy-start | bytes 1572868
  392.2 59.6 %all-gather.17.cloned.1.call-start = ((), (), s32[]{:S(2)}) async-start(), calls=%async_computation.21 | async-start | bytes 2621440 | tf_op jit(solution)/shard_map/all_gather | solution.py:199
  429.1 188.0 %reduce-scatter.40.cloned.1.call-start = ((), (), s32[]{:S(2)}) async-start(), calls=%async_computation.31 | async-start | bytes 4718592
  528.9 180.1 %reduce-scatter.22.cloned.1.call-start = ((), (), s32[]{:S(2)}) async-start(), calls=%async_computation.22 | async-start | bytes 4718592 | tf_op jit(solution)/shard_map/reduce_scatter | solution.py:235
  529.6 266.2 %reduce-scatter.32.cloned.1.call-start = ((), (), s32[]{:S(2)}) async-start(), calls=%async_computation.27 | async-start | bytes 2359296 | tf_op jit(solution)/shard_map/reduce_scatter | solution.py:300
  534.2 399.1 %reduce-scatter.38.cloned.1.call-start = ((), (), s32[]{:S(2)}) async-start(), calls=%async_computation.30 | async-start | bytes 9437184 | tf_op jit(solution)/shard_map/reduce_scatter | solution.py:309
  545.2 539.7 %reduce-scatter.34.cloned.1.call-start = ((), (), s32[]{:S(2)}) async-start(), calls=%async_computation.28 | async-start | bytes 9437184 | tf_op jit(solution)/shard_map/reduce_scatter | solution.py:303
  555.3 681.5 %reduce-scatter.36.cloned.1.call-start = ((), (), s32[]{:S(2)}) async-start(), calls=%async_computation.29 | async-start | bytes 9437184 | tf_op jit(solution)/shard_map/reduce_scatter | solution.py:306
  565.7 703.9 %reduce-scatter.24.cloned.1.call-start = ((), (), s32[]{:S(2)}) async-start(), calls=%async_computation.23 | async-start | bytes 2621440 | tf_op jit(solution)/shard_map/reduce_scatter | solution.py:280
  619.7 91.7 %copy-start.15 = (f32[128,4,128]{0,2,1:T(8,128)S(1)}, f32[128,4,128]{0,2,1:T(8,128)}, u32[]{:S(2)}) copy-start(f32[128,4,128]{0,2,1:T(8,128)} %get-tuple-element.381) | copy-start | bytes 786436
  717.0 5.1 copy-start.2
  717.0 5.1 copy-start.29
  717.0 5.1 copy-start.31
  722.1 3.3 copy-start.33
  725.1 44.6 %copy-start.37 = (f32[128,4]{0,1:T(4,128)S(1)}, f32[128,4]{0,1:T(4,128)}, u32[]{:S(2)}) copy-start(f32[128,4]{0,1:T(4,128)} %get-tuple-element.379) | copy-start | bytes 6148
  725.4 46.3 %copy-start.36 = (f32[128,4]{0,1:T(4,128)S(1)}, f32[128,4]{0,1:T(4,128)}, u32[]{:S(2)}) copy-start(f32[128,4]{0,1:T(4,128)} %get-tuple-element.364) | copy-start | bytes 6148
  778.2 563.4 %reduce-scatter.28.cloned.1.call-start = ((), (), s32[]{:S(2)}) async-start(), calls=%async_computation.25 | async-start | bytes 2359296 | tf_op jit(solution)/shard_map/reduce_scatter | solution.py:294
  783.5 629.0 %reduce-scatter.26.cloned.1.call-start = ((), (), s32[]{:S(2)}) async-start(), calls=%async_computation.24 | async-start | bytes 2359296 | tf_op jit(solution)/shard_map/reduce_scatter | solution.py:291
  788.8 694.9 %reduce-scatter.30.cloned.1.call-start = ((), (), s32[]{:S(2)}) async-start(), calls=%async_computation.26 | async-start | bytes 2359296 | tf_op jit(solution)/shard_map/reduce_scatter | solution.py:297
  1087.6 182.0 %copy-start.4 = (bf16[32,4,2048]{2,1,0:T(4,128)(2,1)S(1)}, bf16[32,4,2048]{2,1,0:T(4,128)(2,1)}, u32[]{:S(2)}) copy-start(bf16[32,4,2048]{2,1,0:T(4,128)(2,1)} %param.31) | copy-start | bytes 1572868
  1087.6 182.0 %copy-start.8 = (bf16[32,4,2048]{2,0,1:T(8,128)(2,1)S(1)}, bf16[32,4,2048]{2,0,1:T(8,128)(2,1)}, u32[]{:S(2)}) copy-start(bf16[32,4,2048]{2,0,1:T(8,128)(2,1)} %reduce-scatter.20.cloned.1.call-done) | copy-start | bytes 1572868
  (18 other events, 27.0 us)
Sparse Core Ops, SparseCore 0:
  10.2 25.2 all-gather.6
  39.9 73.3 all-gather.8
  116.1 71.6 all-gather.10
  219.6 29.6 reduce-scatter.15
  252.9 22.5 all-gather.12
  303.0 31.3 reduce-scatter.17
  339.9 22.5 all-gather.14
  392.3 31.4 reduce-scatter.19
  429.2 22.5 all-gather.16
  529.0 88.0 reduce-scatter.39
  620.7 88.1 reduce-scatter.21
  713.3 67.8 reduce-scatter.31
  785.2 147.9 reduce-scatter.37
  936.7 148.0 reduce-scatter.33
  1088.7 147.9 reduce-scatter.35
  1239.2 30.4 reduce-scatter.23
  1273.4 68.0 reduce-scatter.27
  1345.3 67.0 reduce-scatter.25
  1416.4 67.2 reduce-scatter.29
where the time goes:
time: 1500 us; the launch traced here: 1490 us
  waiting for transfers between devices  1100 us (73%)
  matrix products  167 us (11%)
  local copies, waits for them, and re-layouts  107 us (7%)
  other arithmetic  56.4 us (4%)
  blocking collectives  48.1 us (3%)
  between operations  15.5 us (1%)
    reduce_scatter x1, waiting for transfers between devices, local(): lax.psum_scatter(up_term.astype(jnp.bfloat16), 'seq', scatter_dimension=0...  149 us
    reduce_scatter x1, waiting for transfers between devices, local(): lax.psum_scatter(gate_term.astype(jnp.bfloat16), 'seq', scatter_dimension...  146 us
    reduce_scatter x1, waiting for transfers between devices, local(): lax.psum_scatter(down_term.astype(jnp.bfloat16), 'seq', scatter_dimension...  133 us
    reduce_scatter x1, waiting for transfers between devices, local(): lax.psum_scatter(key_full.astype(jnp.bfloat16), 'seq', scatter_dimension=...  89.2 us
    reduce_scatter x1, waiting for transfers between devices, local(): lax.psum_scatter(value_term.astype(jnp.bfloat16), 'seq', scatter_dimensio...  69.3 us
    reduce_scatter x1, waiting for transfers between devices, local(): lax.psum_scatter(query_term.astype(jnp.bfloat16), 'seq', scatter_dimensio...  69 us
    reduce_scatter x1, waiting for transfers between devices, local(): lax.psum_scatter(key_term.astype(jnp.bfloat16), 'seq', scatter_dimension=...  68.8 us
    all_gather x1, waiting for transfers between devices, cycle_values(): lax.all_gather(jnp.transpose(key_low, (1, 0, 2)), 'seq', axis=1, tiled=True)  68.2 us
  transfers between devices with their start and end apart: 19, of which 18 were waited for; matrix products, arithmetic and copies ran while one was open for 9% of the time, Pallas kernels for 0%

commit v1 on v0

--- a/solution.py
+++ b/solution.py
@@ -339,9 +339,300 @@
     )
 
 
+def xor_pairs(size, bit):
+    return [(index, index ^ bit) for index in range(size)]
+
+
+def grouped(
+    inputs,
+    documents,
+    query_weight,
+    key_weight,
+    value_weight,
+    output_weight,
+    query_gain,
+    key_gain,
+    attention_gain,
+    gate_weight,
+    up_weight,
+    down_weight,
+    feed_gain,
+    cotangent,
+):
+    f32 = jnp.float32
+    bf16 = jnp.bfloat16
+    row_count, seq_count, width = inputs.shape
+    own_count = row_count * seq_count
+    half_count = own_count // 2
+    all_count = 8 * own_count
+    block = width // 8
+    s = lax.axis_index("seq")
+    t = lax.axis_index("tp")
+    zh, zl, x = s // 4, (s // 2) % 2, s % 2
+    y, c = t // 2, t % 2
+    sequence = 2 * zh + x
+
+    def by_seq(v, bits):
+        return lax.ppermute(v, "seq", xor_pairs(8, bits))
+
+    def by_tp(v, bits):
+        return lax.ppermute(v, "tp", xor_pairs(4, bits))
+
+    swap_x = lambda v: by_seq(v, 1)
+    swap_zl = lambda v: by_seq(v, 2)
+    swap_zh = lambda v: by_seq(v, 4)
+    swap_c = lambda v: by_tp(v, 1)
+    swap_y = lambda v: by_tp(v, 2)
+
+    def to_sequence(v):
+        pieces = []
+        for k in range(4):
+            part = lax.dynamic_index_in_dim(v, sequence ^ k, 1, keepdims=False)
+            pieces.append(by_seq(part, (k // 2) * 4 + k % 2) if k else part)
+        return jnp.concatenate(pieces, axis=0)
+
+    def from_sequence(v):
+        parts = v.astype(bf16).reshape(4, row_count, width)
+        pieces = [parts[0]]
+        for k in range(1, 4):
+            pieces.append(by_seq(parts[k], (k // 2) * 4 + k % 2))
+        rows = jnp.stack(pieces, axis=1).reshape(row_count, 2, 2, width)
+        rows = jnp.where(zh == 1, rows[:, ::-1], rows)
+        rows = jnp.where(x == 1, rows[:, :, ::-1], rows)
+        return rows.reshape(row_count, 4, width).astype(f32)
+
+    def gather(a):
+        a0, b0 = a[:half_count], a[half_count:]
+        a1 = swap_y(a0)
+        b1 = swap_zl(b0)
+        a23 = swap_zl(jnp.concatenate([a0, a1]))
+        b13 = swap_y(jnp.concatenate([b0, b1]))
+        a_all = jnp.concatenate([a0, a1, a23])
+        b_all = jnp.concatenate(
+            [b0, b13[:half_count], b1, b13[half_count:]]
+        )
+        return jnp.concatenate([a_all, swap_c(a_all), b_all, swap_c(b_all)])
+
+    def scatter(p):
+        p = p.astype(bf16).reshape(2, 2, 4 * half_count, width)
+        p = (p[:, 0].astype(f32) + swap_c(p[:, 1]).astype(f32)).astype(bf16)
+        a = p[0].reshape(2, 2 * half_count, width)
+        a = (a[0].astype(f32) + swap_zl(a[1]).astype(f32)).astype(bf16)
+        a = a[:half_count].astype(f32) + swap_y(a[half_count:]).astype(f32)
+        b = p[1].reshape(2, 2, half_count, width)
+        b = (b[:, 0].astype(f32) + swap_y(b[:, 1]).astype(f32)).astype(bf16)
+        b = b[0].astype(f32) + swap_zl(b[1]).astype(f32)
+        return jnp.concatenate([a, b])
+
+    def group_sum(v):
+        v = v.reshape(-1, 2, 2, 2, 2, half_count)
+        v = v + swap_c(v)[:, :, ::-1]
+        v = v + swap_y(v)[:, :, :, :, ::-1]
+        v = v + swap_zl(v)[:, :, :, ::-1]
+        return v.reshape(-1, all_count)
+
+    def feature_blocks(v, bits):
+        v = v.reshape(all_count, 8, block)
+        return jnp.concatenate(
+            [lax.dynamic_index_in_dim(v, s ^ k, 1, keepdims=False) for k in bits], axis=1
+        )
+
+    def weight_sum(features, units, units_first):
+        def product(bits):
+            left = feature_blocks(features, bits)
+            if units_first:
+                return jnp.einsum("tu,tf->uf", units, left, preferred_element_type=f32)
+            return jnp.einsum("tf,tu->fu", left, units, preferred_element_type=f32)
+
+        axis = 1 if units_first else 0
+
+        def part(v, first, count):
+            return lax.slice_in_dim(v, first * block, (first + count) * block, axis=axis)
+
+        far = swap_x(product((5, 7, 1, 3)).astype(bf16))
+        sent = (product((4, 6)) + part(far, 0, 2).astype(f32)).astype(bf16)
+        sent = swap_zh(sent)
+        kept = product((0, 2)) + part(far, 2, 2).astype(f32) + sent.astype(f32)
+        other = swap_zl(part(kept, 1, 1).astype(bf16)).astype(f32)
+        mine = part(kept, 0, 1)
+        axis = 1 - axis
+        return jnp.where(
+            zl == 0,
+            jnp.concatenate([mine, other], axis=axis),
+            jnp.concatenate([other, mine], axis=axis),
+        )
+
+    def zl_half(w, axis):
+        size = w.shape[axis] // 2
+        return lax.dynamic_slice_in_dim(w, zl * size, size, axis)
+
+    wq, wk, wv = zl_half(query_weight, 1), zl_half(key_weight, 1), zl_half(value_weight, 1)
+    wo = zl_half(output_weight, 0)
+    wg, wu, wd = zl_half(gate_weight, 1), zl_half(up_weight, 1), zl_half(down_weight, 0)
+    gq, gk = zl_half(query_gain, 0), zl_half(key_gain, 0)
+    heads_width = wq.shape[1]
+    heads = heads_width // HEAD
+    score_scale = HEAD ** (-0.5)
+
+    rows_in = to_sequence(inputs)
+    grad_top = to_sequence(cotangent).astype(f32)
+    whole = gather(rows_in)
+
+    def relative(v):
+        v = v.reshape(2, 2, 2, 2, 2, row_count)
+        for axis, bit in enumerate((zh, zl, x, y, c)):
+            v = jnp.where(bit == 1, jnp.flip(v, axis), v)
+        return jnp.transpose(v, (0, 4, 1, 3, 2, 5)).reshape(all_count)
+
+    doc_row = lax.dynamic_index_in_dim(documents, sequence, 0, keepdims=False)
+    places = relative(jnp.arange(all_count, dtype=jnp.int32))
+    docs = relative(doc_row)
+    starts = jnp.sum((doc_row[None, :] < docs[:, None]).astype(jnp.int32), axis=-1)
+    cosine, sine_part = rope_tables(places - starts, HEAD)
+    allowed = (docs[:, None] == docs[None, :]) & (places[None, :] <= places[:, None])
+
+    def project(w):
+        return jnp.einsum("rd,dh->rh", whole, w, preferred_element_type=f32)
+
+    queries, keys_proj = project(wq), project(wk)
+    value_low = project(wv).astype(bf16)
+    sums = group_sum(
+        jnp.stack([jnp.sum(queries * queries, axis=-1), jnp.sum(keys_proj * keys_proj, axis=-1)])
+    )
+    query_inv = lax.rsqrt(sums[0] / width + EPS)[:, None]
+    key_inv = lax.rsqrt(sums[1] / width + EPS)[:, None]
+
+    def heads_of(v):
+        return v.reshape(all_count, heads, HEAD)
+
+    query_low = rotate(heads_of(queries * query_inv * gq), cosine, sine_part).astype(bf16)
+    key_low = rotate(heads_of(keys_proj * key_inv * gk), cosine, sine_part).astype(bf16)
+    value_heads = heads_of(value_low)
+
+    def scores_of():
+        scores = (
+            jnp.einsum("qhd,khd->hqk", query_low, key_low, preferred_element_type=f32)
+            * score_scale
+        )
+        return jnp.where(allowed[None], scores, NEGATIVE)
+
+    scores = scores_of()
+    top_score = jnp.max(scores, axis=-1, keepdims=True)
+    spread = jnp.exp(scores - top_score)
+    total = jnp.sum(spread, axis=-1, keepdims=True)
+    weights = (spread / total).astype(bf16)
+    attended = jnp.einsum("hqk,khd->qhd", weights, value_heads, preferred_element_type=f32)
+    log_total = top_score + jnp.log(total)
+    mixed_low = attended.reshape(all_count, heads_width).astype(bf16)
+
+    branch = scatter(jnp.einsum("rh,hd->rd", mixed_low, wo, preferred_element_type=f32))
+    attn_inv = rms_scale(branch)
+    hidden = rows_in.astype(f32) + branch * attn_inv * attention_gain
+    hidden_whole = gather(hidden.astype(bf16))
+    gate_value = jnp.einsum("rd,df->rf", hidden_whole, wg, preferred_element_type=f32)
+    up_value = jnp.einsum("rd,df->rf", hidden_whole, wu, preferred_element_type=f32)
+    sigmoid_value = jax.nn.sigmoid(gate_value)
+    act_low = (gate_value * sigmoid_value * up_value).astype(bf16)
+    down_value = scatter(jnp.einsum("rf,fd->rd", act_low, wd, preferred_element_type=f32))
+    feed_inv = rms_scale(down_value)
+    layer_out = from_sequence(hidden + down_value * feed_inv * feed_gain)
+    feed_gain_term = jnp.sum(grad_top * down_value * feed_inv, axis=0)
+    down_whole = gather(norm_back(down_value, feed_inv, feed_gain, grad_top).astype(bf16))
+
+    down_term = weight_sum(down_whole, act_low, True)
+    act_grad = jnp.einsum("rd,fd->rf", down_whole, wd, preferred_element_type=f32)
+    up_grad_low = (act_grad * gate_value * sigmoid_value).astype(bf16)
+    gate_grad_low = (
+        act_grad * up_value * sigmoid_value * (1.0 + gate_value * (1.0 - sigmoid_value))
+    ).astype(bf16)
+    hidden_grad = grad_top + scatter(
+        jnp.einsum("rf,df->rd", gate_grad_low, wg, preferred_element_type=f32)
+        + jnp.einsum("rf,df->rd", up_grad_low, wu, preferred_element_type=f32)
+    )
+    gate_term = weight_sum(hidden_whole, gate_grad_low, False)
+    up_term = weight_sum(hidden_whole, up_grad_low, False)
+    attention_gain_term = jnp.sum(hidden_grad * branch * attn_inv, axis=0)
+    branch_whole = gather(norm_back(branch, attn_inv, attention_gain, hidden_grad).astype(bf16))
+    mixed_grad_low = jnp.einsum(
+        "rd,hd->rh", branch_whole, wo, preferred_element_type=f32
+    ).astype(bf16)
+    out_term = weight_sum(branch_whole, mixed_low, True)
+
+    grad_heads = heads_of(mixed_grad_low)
+    delta = jnp.transpose(jnp.sum(grad_heads.astype(f32) * attended, axis=-1))
+    weights = jnp.exp(scores_of() - log_total)
+    weight_grad = jnp.einsum("qhd,khd->hqk", grad_heads, value_heads, preferred_element_type=f32)
+    score_grad = (weights * (weight_grad - delta[:, :, None]) * score_scale).astype(bf16)
+    query_back = jnp.einsum("hqk,khd->qhd", score_grad, key_low, preferred_element_type=f32)
+    key_back = jnp.einsum("hqk,qhd->khd", score_grad, query_low, preferred_element_type=f32)
+    value_grad_low = (
+        jnp.einsum("hqk,qhd->khd", weights.astype(bf16), grad_heads, preferred_element_type=f32)
+        .reshape(all_count, heads_width)
+        .astype(bf16)
+    )
+    query_rot = unrotate(query_back, cosine, sine_part).reshape(all_count, heads_width)
+    key_rot = unrotate(key_back, cosine, sine_part).reshape(all_count, heads_width)
+    query_gain_term = jnp.sum(query_rot * queries * query_inv, axis=0)
+    key_gain_term = jnp.sum(key_rot * keys_proj * key_inv, axis=0)
+    dots = group_sum(
+        jnp.stack(
+            [
+                jnp.sum(query_rot * gq * queries, axis=-1),
+                jnp.sum(key_rot * gk * keys_proj, axis=-1),
+            ]
+        )
+    )
+    query_grad_low = (
+        query_inv * gq * query_rot - queries * query_inv**3 * (dots[0] / width)[:, None]
+    ).astype(bf16)
+    key_grad_low = (
+        key_inv * gk * key_rot - keys_proj * key_inv**3 * (dots[1] / width)[:, None]
+    ).astype(bf16)
+    input_grad = from_sequence(
+        hidden_grad
+        + scatter(
+            jnp.einsum("rh,dh->rd", query_grad_low, wq, preferred_element_type=f32)
+            + jnp.einsum("rh,dh->rd", key_grad_low, wk, preferred_element_type=f32)
+            + jnp.einsum("rh,dh->rd", value_grad_low, wv, preferred_element_type=f32)
+        )
+    )
+    query_term = weight_sum(whole, query_grad_low, False)
+    key_term = weight_sum(whole, key_grad_low, False)
+    value_term = weight_sum(whole, value_grad_low, False)
+
+    place = (2 * t + zl) * heads_width
+
+    def placed(term):
+        return lax.dynamic_update_slice(jnp.zeros((width,), f32), term, (place,))
+
+    gains = lax.psum(
+        jnp.stack(
+            [placed(query_gain_term), placed(key_gain_term), attention_gain_term, feed_gain_term]
+        ),
+        ("seq", "tp"),
+    )
+    gains = lax.dynamic_slice_in_dim(gains, s * block, block, 1)
+    return (
+        layer_out,
+        input_grad,
+        query_term,
+        key_term,
+        value_term,
+        out_term,
+        gate_term,
+        up_term,
+        down_term,
+        gains[0],
+        gains[1],
+        gains[2],
+        gains[3],
+    )
+
+
 def solution(mesh):
+    step = grouped if mesh.shape["seq"] == 8 and mesh.shape["tp"] == 4 else local
     return jax.shard_map(
-        local,
+        step,
         mesh=mesh,
         in_specs=(
             P(("seq", "tp"), None, None),

time: 1500 us -> 778 us (0.52)
  waiting for transfers between devices: 1100 us -> 316 us
  starting transfers between devices: 2.06 us -> 79.6 us
  matrix products: 167 us -> 122 us
  local copies, waits for them, and re-layouts: 107 us -> 141 us
    reduce_scatter x12 -> x0, waiting for transfers between devices: 848 us -> none  [the longest x1 149 us: local(): lax.psum_scatter(up_term.astype(jnp.bfloat16), 'seq', scatter_dimension=0...]
    ppermute x0 -> x83, waiting for transfers between devices: none -> 316 us  [the longest x51 249 us: by_seq(): return lax.ppermute(v, 'seq', xor_pairs(8, bits))]
    all_gather x6 -> x0, waiting for transfers between devices: 198 us -> none  [the longest x1 68.2 us: cycle_values(): lax.all_gather(jnp.transpose(key_low, (1, 0, 2)), 'seq', axis=1, tiled=True)]
    ppermute x0 -> x83, starting transfers between devices: none -> 79.6 us  [the longest x51 60.9 us: by_seq(): return lax.ppermute(v, 'seq', xor_pairs(8, bits))]
    unnamed x20 -> x0, waiting for transfers between devices: 50.4 us -> none
    dot_general x49 -> x41, matrix products: 167 us -> 122 us  [the longest x15 30.2 us: product(): return jnp.einsum('tf,tu->fu', left, units, preferred_element_type=f32)]
    dynamic_slice x17 -> x8, local copies, waits for them, and re-layouts: 12.2 us -> 53.5 us  [the longest x3 43.4 us: feature_blocks(): lax.dynamic_index_in_dim(v, s ^ k, 1, keepdims=False)]
    unnamed x1 -> x0, blocking collectives: 36 us -> none
  transfers between devices with their start and end apart: 19 -> 83, of which waited for: 18 -> 46; matrix products, arithmetic and copies ran while one was open for 9% -> 30% of each run, Pallas kernels for 0% -> 0%
where the time goes in v1:
time: 778 us; the launch traced here: 772 us
  waiting for transfers between devices  316 us (41%)
  local copies, waits for them, and re-layouts  141 us (18%)
  matrix products  122 us (16%)
  starting transfers between devices  79.6 us (10%)
  other arithmetic  66.6 us (9%)
  blocking collectives  41.8 us (5%)
    ppermute x51, waiting for transfers between devices, by_seq(): return lax.ppermute(v, 'seq', xor_pairs(8, bits))  249 us
    ppermute x32, waiting for transfers between devices, by_tp(): return lax.ppermute(v, 'tp', xor_pairs(4, bits))  67.6 us
    unnamed x342, local copies, waits for them, and re-layouts  64.2 us
    ppermute x51, starting transfers between devices, by_seq(): return lax.ppermute(v, 'seq', xor_pairs(8, bits))  60.9 us
    dynamic_slice x3, local copies, waits for them, and re-layouts, feature_blocks(): lax.dynamic_index_in_dim(v, s ^ k, 1, keepdims=False)  43.4 us
    psum x1, blocking collectives, grouped(): lax.psum(jnp.stack([placed(query_gain_term), placed(key_gain_term), atten...  41.8 us
    dot_general x15, matrix products, product(): return jnp.einsum('tf,tu->fu', left, units, preferred_element_type=f32)  30.2 us
    ppermute x32, starting transfers between devices, by_tp(): return lax.ppermute(v, 'tp', xor_pairs(4, bits))  18.7 us
  transfers between devices with their start and end apart: 83, of which 46 were waited for; matrix products, arithmetic and copies ran while one was open for 30% of the time, Pallas kernels for 0%

profile of v1, /device:TPU:0, one launch (start us, length us, event | category | flops | bytes accessed | tf_op | source)
XLA Modules:
  0.0 771.8 jit_solution(2115351209806275873)
XLA Ops:
  0.7 5.6 constant_dynamic-slice_fusion.28
  7.0 5.0 collective-permute-start.2
  19.9 5.0 collective-permute-done.3
  29.4 12.1 %collective-permute-done.4 = bf16[128,2048]{1,0:T(8,128)(2,1)S(1)} collective-permute-done((bf16[128,2048]{1,0:T(8,128)(2,1)}, bf16[128,2048]{1,0:T(8,128)(2,1)S(1)}, u32[]{:S(2)}, u32[]{:S(2)}) %collective-permute-start.4) | collective-permute-done | bytes 524320 | tf_op jit(solution)/shard_map/ppermute | solution.py:376
  52.4 6.5 collective-permute-done.7
  68.8 3.6 multiply_reduce_fusion.5
  89.4 4.6 convolution_convert_fusion.8
  103.5 4.1 fusion.173
  109.2 4.1 collective-permute-done.12
  115.2 13.2 %collective-permute-done.13 = bf16[128,2048]{1,0:T(8,128)(2,1)S(1)} collective-permute-done((bf16[128,2048]{1,0:T(8,128)(2,1)S(1)}, bf16[128,2048]{1,0:T(8,128)(2,1)S(1)}, u32[]{:S(2)}, u32[]{:S(2)}) %collective-permute-start.13) | collective-permute-done | bytes 524320 | tf_op jit(solution)/shard_map/ppermute | solution.py:376
  130.6 5.5 collective-permute-done.14
  140.8 4.9 collective-permute-done.17
  158.5 7.6 collective-permute-done.18
  173.3 11.6 %collective-permute-done.21 = bf16[128,2048]{1,0:T(8,128)(2,1)S(1)} collective-permute-done((bf16[128,2048]{1,0:T(8,128)(2,1)S(1)}, bf16[128,2048]{1,0:T(8,128)(2,1)S(1)}, u32[]{:S(2)}, u32[]{:S(2)}) %collective-permute-start.21) | collective-permute-done | bytes 524320 | tf_op jit(solution)/shard_map/ppermute | solution.py:379
  187.9 6.4 fusion.19
  194.3 10.0 %multiply_convert_fusion.3 = (bf16[1024,1024]{1,0:T(8,128)(2,1)S(1)}, f32[1024,1024]{1,0:T(8,128)}) fusion(f32[1024,1024]{1,0:T(8,128)S(1)} %fusion.19, bf16[1024,2048]{1,0:T(8,128)(2,1)S(1)} %constant_dynamic-update-slice_fusion.18, bf16[2048,2048]{1,0:T(8,128)(2,1)} %param.24, s32[]{:T(128)S(6)} %select_n.289), kind=kOutput, calls=%fused_computation.20 | convolution fusion | flops 4301258752 | bytes 18874372 | tf_op jit(solution)/shard_map/rd,df->rf/dot_general | solution.py:533
  204.3 5.2 convolution_convert_fusion.1
  221.6 10.3 %constant_dynamic-slice_fusion.16 = (bf16[1024,1,256]{2,1,0:T(2,128)(2,1)}, bf16[1024,1,256]{2,1,0:T(2,128)(2,1)}, bf16[1024,1,256]{2,1,0:T(2,128)(2,1)}, bf16[1...) fusion(bf16[1024,8,256]{2,1,0:T(8,128)(2,1)S(1)} %bitcast.429, ...), kind=kLoop, calls=%fused_computation.427 | loop fusion | bytes 8388640 | tf_op jit(solution)/shard_map/jit(dynamic_index_in_dim)/dynamic_slice | solution.py:437
  244.1 5.2 collective-permute-done.25
  263.0 5.7 collective-permute-done.30
  271.4 12.3 %collective-permute-done.35 = bf16[128,2048]{1,0:T(8,128)(2,1)S(1)} collective-permute-done((bf16[128,2048]{1,0:T(8,128)(2,1)S(1)}, bf16[128,2048]{1,0:T(8,128)(2,1)S(1)}, u32[]{:S(2)}, u32[]{:S(2)}) %collective-permute-start.35) | collective-permute-done | bytes 524320 | tf_op jit(solution)/shard_map/ppermute | solution.py:376
  286.7 11.8 %collective-permute-done.38 = bf16[128,2048]{1,0:T(8,128)(2,1)S(1)} collective-permute-done((bf16[128,2048]{1,0:T(8,128)(2,1)S(1)}, bf16[128,2048]{1,0:T(8,128)(2,1)S(1)}, u32[]{:S(2)}, u32[]{:S(2)}) %collective-permute-start.38) | collective-permute-done | bytes 524320 | tf_op jit(solution)/shard_map/ppermute | solution.py:379
  301.5 8.8 %multiply_convert_fusion.1 = (bf16[1024,1024]{1,0:T(8,128)(2,1)S(1)}, bf16[1024,1024]{1,0:T(8,128)(2,1)S(1)}) fusion(f32[1024,1024]{1,0:T(8,128)S(1)} %copy-done.128, f32[1024,1024]{1,0:T(8,128)} %get-tuple-element.182, bf16[1024,2048]{1,0:T(8,128)(2,1)S(1)} %constant_dynamic-update-slice_fusion.27, bf16[2048,2048]{1,0:T(8,128)(2,1)} %param.25, ...), kind=kOutput, calls=%fused_computation.18 | convolution fusion | flops 4308598784 | bytes 20971524 | tf_op jit(solution)/shard_map/rd,fd->rf/dot_general | solution.py:543
  311.9 9.1 %fusion.17 = f32[1024,2048]{1,0:T(8,128)} fusion(bf16[1024,1024]{1,0:T(8,128)(2,1)S(1)} %get-tuple-element.65, bf16[2048,2048]{1,0:T(8,128)(2,1)} %param.23, s32[]{:T(128)S(6)} %select_n.289), kind=kOutput, calls=%fused_computation.35 | convolution fusion | flops 4294967296 | bytes 14680068 | tf_op jit(solution)/shard_map/rf,df->rd/dot_general | solution.py:549
  321.0 3.7 convolution_convert_fusion.3
  324.7 3.7 convolution_convert_fusion.2
  330.4 8.2 %add_convert_fusion.1 = bf16[1024,2048]{1,0:T(8,128)(2,1)S(1)} fusion(f32[1024,2048]{1,0:T(8,128)} %fusion.17, bf16[1024,1024]{1,0:T(8,128)(2,1)S(1)} %get-tuple-element.64, bf16[2048,2048]{1,0:T(8,128)(2,1)} %param.24, s32[]{:T(128)S(6)} %select_n.289), kind=kOutput, calls=%fused_computation.3 | convolution fusion | flops 4299161600 | bytes 18874372 | tf_op jit(solution)/shard_map/rf,df->rd/dot_general | solution.py:550
  342.1 10.4 %constant_dynamic-slice_fusion.8 = (bf16[1024,1,256]{2,1,0:T(2,128)(2,1)}, bf16[1024,1,256]{2,1,0:T(2,128)(2,1)S(1)}, bf16[1024,1,256]{2,1,0:T(2,128)(2,1)}, bf1...) fusion(bf16[1024,8,256]{2,1,0:T(8,128)(2,1)S(1)} %bitcast.428, ...), kind=kLoop, calls=%fused_computation.419 | loop fusion | bytes 8388640 | tf_op jit(solution)/shard_map/jit(dynamic_index_in_dim)/dynamic_slice | solution.py:437
  364.7 12.5 %collective-permute-done.74 = bf16[1024,1024]{1,0:T(8,128)(2,1)} collective-permute-done((bf16[1024,1024]{1,0:T(8,128)(2,1)}, bf16[1024,1024]{1,0:T(8,128)(2,1)}, u32[]{:S(2)}, u32[]{:S(2)}) %collective-permute-start.74) | collective-permute-done | bytes 2097184 | tf_op jit(solution)/shard_map/ppermute | solution.py:376
  385.6 36.5 %collective-permute-done.77 = bf16[1024,1024]{1,0:T(8,128)(2,1)} collective-permute-done((bf16[1024,1024]{1,0:T(8,128)(2,1)}, bf16[1024,1024]{1,0:T(8,128)(2,1)}, u32[]{:S(2)}, u32[]{:S(2)}) %collective-permute-start.77) | collective-permute-done | bytes 2097184 | tf_op jit(solution)/shard_map/ppermute | solution.py:376
  431.8 20.0 %collective-permute-done.44 = bf16[64,2048]{1,0:T(8,128)(2,1)S(1)} collective-permute-done((bf16[64,2048]{1,0:T(8,128)(2,1)S(1)}, bf16[64,2048]{1,0:T(8,128)(2,1)S(1)}, u32[]{:S(2)}, u32[]{:S(2)}) %collective-permute-start.44) | collective-permute-done | bytes 262176 | tf_op jit(solution)/shard_map/ppermute | solution.py:376
  455.5 10.7 %collective-permute-done.80 = bf16[1024,1024]{1,0:T(8,128)(2,1)S(1)} collective-permute-done((bf16[1024,1024]{1,0:T(8,128)(2,1)S(1)}, bf16[1024,1024]{1,0:T(8,128)(2,1)S(1)}, u32[]{:S(2)}, u32[]{:S(2)}) %collective-permute-start.80) | collective-permute-done | bytes 2097184 | tf_op jit(solution)/shard_map/ppermute | solution.py:376
  474.6 19.1 %collective-permute-done.78 = bf16[512,1024]{1,0:T(8,128)(2,1)S(1)} collective-permute-done((bf16[512,1024]{1,0:T(8,128)(2,1)S(1)}, bf16[512,1024]{1,0:T(8,128)(2,1)S(1)}, u32[]{:S(2)}, u32[]{:S(2)}) %collective-permute-start.78) | collective-permute-done | bytes 1048608 | tf_op jit(solution)/shard_map/ppermute | solution.py:376
  495.7 12.6 %collective-permute-done.46 = bf16[128,2048]{1,0:T(8,128)(2,1)S(1)} collective-permute-done((bf16[128,2048]{1,0:T(8,128)(2,1)S(1)}, bf16[128,2048]{1,0:T(8,128)(2,1)S(1)}, u32[]{:S(2)}, u32[]{:S(2)}) %collective-permute-start.46) | collective-permute-done | bytes 524320 | tf_op jit(solution)/shard_map/ppermute | solution.py:376
  508.4 7.8 %collective-permute-done.81 = bf16[1024,512]{1,0:T(8,128)(2,1)S(1)} collective-permute-done((bf16[1024,512]{1,0:T(8,128)(2,1)S(1)}, bf16[1024,512]{1,0:T(8,128)(2,1)S(1)}, u32[]{:S(2)}, u32[]{:S(2)}) %collective-permute-start.81) | collective-permute-done | bytes 1048608 | tf_op jit(solution)/shard_map/ppermute | solution.py:376
  518.6 5.1 collective-permute-done.76
  523.8 11.1 %collective-permute-done.79 = bf16[256,1024]{1,0:T(8,128)(2,1)S(1)} collective-permute-done((bf16[256,1024]{1,0:T(8,128)(2,1)S(1)}, bf16[256,1024]{1,0:T(8,128)(2,1)S(1)}, u32[]{:S(2)}, u32[]{:S(2)}) %collective-permute-start.79) | collective-permute-done | bytes 524320 | tf_op jit(solution)/shard_map/ppermute | solution.py:376
  538.7 5.7 collective-permute-done.82
  547.6 3.5 copy.292
  553.8 3.7 multiply_convert_fusion
  565.1 41.8 %psum.7 = f32[4,2048]{1,0:T(4,128)S(1)} all-reduce(f32[4,2048]{1,0:T(4,128)S(1)} %pad_maximum_fusion.54), channel_id=1, replica_groups=mesh['seq'=8,'tp'=4] {'seq','tp'}, use_global_device_ids=true, to_apply=%region_16.17 | all-reduce | flops 8192 | bytes 65536 | tf_op jit(solution)/shard_map/psum | solution.py:608
  607.1 22.7 %constant_dynamic-slice_fusion.24 = (bf16[1024,1,256]{2,1,0:T(2,128)(2,1)S(1)}, bf16[1024,1,256]{2,1,0:T(2,128)(2,1)S(1)}, bf16[1024,1,256]{2,1,0:T(2,128)(2,1)}...) fusion(bf16[1024,8,256]{2,1,0:T(8,128)(2,1)} %bitcast.427, ...), kind=kLoop, calls=%fused_computation.435 | loop fusion | bytes 8388640 | tf_op jit(solution)/shard_map/jit(dynamic_index_in_dim)/dynamic_slice | solution.py:437
  680.8 6.3 collective-permute-done.62
  690.1 12.0 %collective-permute-done.69 = bf16[512,256]{0,1:T(8,128)(2,1)S(1)} collective-permute-done((bf16[512,256]{0,1:T(8,128)(2,1)S(1)}, bf16[512,256]{0,1:T(8,128)(2,1)S(1)}, u32[]{:S(2)}, u32[]{:S(2)}) %collective-permute-start.69) | collective-permute-done | bytes 262176 | tf_op jit(solution)/shard_map/ppermute | solution.py:376
  703.3 4.5 collective-permute-done.72
  714.6 4.0 collective-permute-done.63
  734.0 7.9 %collective-permute-done.55 = bf16[128,2048]{1,0:T(8,128)(2,1)} collective-permute-done((bf16[128,2048]{1,0:T(8,128)(2,1)}, bf16[128,2048]{1,0:T(8,128)(2,1)}, u32[]{:S(2)}, u32[]{:S(2)}) %collective-permute-start.55) | collective-permute-done | bytes 524320 | tf_op jit(solution)/shard_map/ppermute | solution.py:376
  746.0 4.8 collective-permute-done.56
  (716 shorter events, 311.1 us)
Async XLA Ops:
  7.0 21.6 %collective-permute-start.2 = (bf16[32,2048]{1,0:T(8,128)(2,1)}, bf16[32,2048]{1,0:T(8,128)(2,1)S(1)}, u32[]{:S(2)}, u32[]{:S(2)}) collective-permute-start(bf16[32,2048]{1,0:T(8,128)(2,1)} %bitcast.424), channel_id=1, source_target_pairs={{0,20},{4,16},{8,28},{12,24},{16,4},{20,0},{24,12},{28,8},{1,21},{... | collective-permute-start | bytes 393224 | tf_op jit(solution)/shard_map/ppermute | solution.py:376
  12.7 15.9 %collective-permute-start.1 = (bf16[32,2048]{1,0:T(8,128)(2,1)}, bf16[32,2048]{1,0:T(8,128)(2,1)S(1)}, u32[]{:S(2)}, u32[]{:S(2)}) collective-permute-start(bf16[32,2048]{1,0:T(8,128)(2,1)} %bitcast.425), channel_id=1, source_target_pairs={{0,16},{4,20},{8,24},{12,28},{16,0},{20,4},{24,8},{28,12},{1,17},{... | collective-permute-start | bytes 393224 | tf_op jit(solution)/shard_map/ppermute | solution.py:376
  25.8 15.8 %collective-permute-start.4 = (bf16[128,2048]{1,0:T(8,128)(2,1)}, bf16[128,2048]{1,0:T(8,128)(2,1)S(1)}, u32[]{:S(2)}, u32[]{:S(2)}) collective-permute-start(bf16[128,2048]{1,0:T(8,128)(2,1)} %pad_maximum_fusion.25), channel_id=1, source_target_pairs={{0,8},{4,12},{8,0},{12,4},{16,24},{20,28},{24,16},{28,20},{1,9},{5... | collective-permute-start | bytes 1572872 | tf_op jit(solution)/shard_map/ppermute | solution.py:376
  29.4 15.3 %collective-permute-start.6 = (bf16[64,2048]{1,0:T(8,128)(2,1)}, bf16[64,2048]{1,0:T(8,128)(2,1)}, u32[]{:S(2)}, u32[]{:S(2)}) collective-permute-start(bf16[64,2048]{1,0:T(8,128)(2,1)} %pad_maximum_fusion.53), channel_id=1, source_target_pairs={{0,8},{4,12},{8,0},{12,4},{16,24},{20,28},{24,16},{28,20},{1,9},{5... | collective-permute-start | bytes 786440 | tf_op jit(solution)/shard_map/ppermute | solution.py:376
  114.6 14.5 %collective-permute-start.15 = (bf16[2,64,2048]{2,1,0:T(8,128)(2,1)S(1)}, bf16[2,64,2048]{2,1,0:T(8,128)(2,1)S(1)}, u32[]{:S(2)}, u32[]{:S(2)}) collective-permute-start(bf16[2,64,2048]{2,1,0:T(8,128)(2,1)S(1)} %slice_bitcast_fusion.20), channel_id=1, source_target_pairs={{0,2},{1,3},{2,0},{3,1},{4,6},{5,7},{6,4},{7,5},{8,10},{9,11},{10,... | collective-permute-start | bytes 1572872 | tf_op jit(solution)/shard_map/ppermute | solution.py:379
  146.5 19.5 %collective-permute-start.18 = (bf16[128,2048]{1,0:T(8,128)(2,1)}, bf16[128,2048]{1,0:T(8,128)(2,1)}, u32[]{:S(2)}, u32[]{:S(2)}) collective-permute-start(bf16[128,2048]{1,0:T(8,128)(2,1)} %pad_maximum_fusion.29), channel_id=1, source_target_pairs={{0,8},{4,12},{8,0},{12,4},{16,24},{20,28},{24,16},{28,20},{1,9},{5... | collective-permute-start | bytes 1572872 | tf_op jit(solution)/shard_map/ppermute | solution.py:376
  148.5 102.6 %collective-permute-start.33 = (bf16[32,2048]{1,0:T(8,128)(2,1)}, bf16[32,2048]{1,0:T(8,128)(2,1)}, u32[]{:S(2)}, u32[]{:S(2)}) collective-permute-start(bf16[32,2048]{1,0:T(8,128)(2,1)} %bitcast.420), channel_id=1, source_target_pairs={{0,20},{4,16},{8,28},{12,24},{16,4},{20,0},{24,12},{28,8},{1,21},{... | collective-permute-start | bytes 393224 | tf_op jit(solution)/shard_map/ppermute | solution.py:376
  152.4 98.7 %collective-permute-start.31 = (bf16[32,2048]{1,0:T(8,128)(2,1)}, bf16[32,2048]{1,0:T(8,128)(2,1)}, u32[]{:S(2)}, u32[]{:S(2)}) collective-permute-start(bf16[32,2048]{1,0:T(8,128)(2,1)} %bitcast.422), channel_id=1, source_target_pairs={{0,4},{4,0},{8,12},{12,8},{16,20},{20,16},{24,28},{28,24},{1,5},{5... | collective-permute-start | bytes 393224 | tf_op jit(solution)/shard_map/ppermute | solution.py:376
  153.6 97.5 %collective-permute-start.32 = (bf16[32,2048]{1,0:T(8,128)(2,1)}, bf16[32,2048]{1,0:T(8,128)(2,1)}, u32[]{:S(2)}, u32[]{:S(2)}) collective-permute-start(bf16[32,2048]{1,0:T(8,128)(2,1)} %bitcast.421), channel_id=1, source_target_pairs={{0,16},{4,20},{8,24},{12,28},{16,0},{20,4},{24,8},{28,12},{1,17},{... | collective-permute-start | bytes 393224 | tf_op jit(solution)/shard_map/ppermute | solution.py:376
  170.5 14.4 %collective-permute-start.21 = (bf16[128,2048]{1,0:T(8,128)(2,1)S(1)}, bf16[128,2048]{1,0:T(8,128)(2,1)S(1)}, u32[]{:S(2)}, u32[]{:S(2)}) collective-permute-start(bf16[128,2048]{1,0:T(8,128)(2,1)S(1)} %pad_maximum_fusion.30), channel_id=1, source_target_pairs={{0,2},{1,3},{2,0},{3,1},{4,6},{5,7},{6,4},{7,5},{8,10},{9,11},{10,... | collective-permute-start | bytes 1572872 | tf_op jit(solution)/shard_map/ppermute | solution.py:379
  218.3 21.6 %collective-permute-start.24 = (bf16[128,2048]{1,0:T(8,128)(2,1)}, bf16[128,2048]{1,0:T(8,128)(2,1)}, u32[]{:S(2)}, u32[]{:S(2)}) collective-permute-start(bf16[128,2048]{1,0:T(8,128)(2,1)} %slice_bitcast_fusion.18), channel_id=1, source_target_pairs={{0,8},{4,12},{8,0},{12,4},{16,24},{20,28},{24,16},{28,20},{1,9},{5... | collective-permute-start | bytes 1572872 | tf_op jit(solution)/shard_map/ppermute | solution.py:376
  220.1 21.6 %collective-permute-start.26 = (bf16[2,64,2048]{2,1,0:T(8,128)(2,1)}, bf16[2,64,2048]{2,1,0:T(8,128)(2,1)}, u32[]{:S(2)}, u32[]{:S(2)}) collective-permute-start(bf16[2,64,2048]{2,1,0:T(8,128)(2,1)} %slice_bitcast_fusion.16), channel_id=1, source_target_pairs={{0,2},{1,3},{2,0},{3,1},{4,6},{5,7},{6,4},{7,5},{8,10},{9,11},{10,... | collective-permute-start | bytes 1572872 | tf_op jit(solution)/shard_map/ppermute | solution.py:379
  260.8 23.2 %collective-permute-start.37 = (bf16[64,2048]{1,0:T(8,128)(2,1)S(1)}, bf16[64,2048]{1,0:T(8,128)(2,1)S(1)}, u32[]{:S(2)}, u32[]{:S(2)}) collective-permute-start(bf16[64,2048]{1,0:T(8,128)(2,1)S(1)} %get-tuple-element.130), channel_id=1, source_target_pairs={{0,8},{4,12},{8,0},{12,4},{16,24},{20,28},{24,16},{28,20},{1,9},{5... | collective-permute-start | bytes 786440 | tf_op jit(solution)/shard_map/ppermute | solution.py:376
  261.8 22.0 %collective-permute-start.35 = (bf16[128,2048]{1,0:T(8,128)(2,1)S(1)}, bf16[128,2048]{1,0:T(8,128)(2,1)S(1)}, u32[]{:S(2)}, u32[]{:S(2)}) collective-permute-start(bf16[128,2048]{1,0:T(8,128)(2,1)S(1)} %pad_maximum_fusion.33), channel_id=1, source_target_pairs={{0,8},{4,12},{8,0},{12,4},{16,24},{20,28},{24,16},{28,20},{1,9},{5... | collective-permute-start | bytes 1572872 | tf_op jit(solution)/shard_map/ppermute | solution.py:376
  284.1 14.4 %collective-permute-start.38 = (bf16[128,2048]{1,0:T(8,128)(2,1)S(1)}, bf16[128,2048]{1,0:T(8,128)(2,1)S(1)}, u32[]{:S(2)}, u32[]{:S(2)}) collective-permute-start(bf16[128,2048]{1,0:T(8,128)(2,1)S(1)} %pad_maximum_fusion.34), channel_id=1, source_target_pairs={{0,2},{1,3},{2,0},{3,1},{4,6},{5,7},{6,4},{7,5},{8,10},{9,11},{10,... | collective-permute-start | bytes 1572872 | tf_op jit(solution)/shard_map/ppermute | solution.py:379
  328.4 48.8 %collective-permute-start.74 = (bf16[1024,1024]{1,0:T(8,128)(2,1)}, bf16[1024,1024]{1,0:T(8,128)(2,1)}, u32[]{:S(2)}, u32[]{:S(2)}) collective-permute-start(bf16[1024,1024]{1,0:T(8,128)(2,1)} %convolution_convert_fusion.3), channel_id=1, source_target_pairs={{0,4},{4,0},{8,12},{12,8},{16,20},{20,16},{24,28},{28,24},{1,5},{5... | collective-permute-start | bytes 6291464 | tf_op jit(solution)/shard_map/ppermute | solution.py:376
  329.0 93.1 %collective-permute-start.77 = (bf16[1024,1024]{1,0:T(8,128)(2,1)}, bf16[1024,1024]{1,0:T(8,128)(2,1)}, u32[]{:S(2)}, u32[]{:S(2)}) collective-permute-start(bf16[1024,1024]{1,0:T(8,128)(2,1)} %convolution_convert_fusion.2), channel_id=1, source_target_pairs={{0,4},{4,0},{8,12},{12,8},{16,20},{20,16},{24,28},{28,24},{1,5},{5... | collective-permute-start | bytes 6291464 | tf_op jit(solution)/shard_map/ppermute | solution.py:376
  342.1 37.9 %collective-permute-start.40 = (bf16[2,256,2048]{2,1,0:T(8,128)(2,1)}, bf16[2,256,2048]{2,1,0:T(8,128)(2,1)}, u32[]{:S(2)}, u32[]{:S(2)}) collective-permute-start(bf16[2,256,2048]{2,1,0:T(8,128)(2,1)} %slice_bitcast_fusion.2), channel_id=1, source_target_pairs={{0,1},{1,0},{2,3},{3,2},{4,5},{5,4},{6,7},{7,6},{8,9},{9,8},{10,11... | collective-permute-start | bytes 6291464 | tf_op jit(solution)/shard_map/ppermute | solution.py:379
  359.6 106.6 %collective-permute-start.80 = (bf16[1024,1024]{1,0:T(8,128)(2,1)S(1)}, bf16[1024,1024]{1,0:T(8,128)(2,1)S(1)}, u32[]{:S(2)}, u32[]{:S(2)}) collective-permute-start(bf16[1024,1024]{1,0:T(8,128)(2,1)S(1)} %fusion.37), channel_id=1, source_target_pairs={{0,4},{4,0},{8,12},{12,8},{16,20},{20,16},{24,28},{28,24},{1,5},{5... | collective-permute-start | bytes 6291464 | tf_op jit(solution)/shard_map/ppermute | solution.py:376
  379.7 90.7 %collective-permute-start.75 = (bf16[512,1024]{1,0:T(8,128)(2,1)S(1)}, bf16[512,1024]{1,0:T(8,128)(2,1)S(1)}, u32[]{:S(2)}, u32[]{:S(2)}) collective-permute-start(bf16[512,1024]{1,0:T(8,128)(2,1)S(1)} %add_convert_fusion.4), channel_id=1, source_target_pairs={{0,16},{4,20},{8,24},{12,28},{16,0},{20,4},{24,8},{28,12},{1,17},{... | collective-permute-start | bytes 3145736 | tf_op jit(solution)/shard_map/ppermute | solution.py:376
  382.6 42.4 %collective-permute-start.41 = (bf16[128,2048]{1,0:T(8,128)(2,1)S(1)}, bf16[128,2048]{1,0:T(8,128)(2,1)S(1)}, u32[]{:S(2)}, u32[]{:S(2)}) collective-permute-start(bf16[128,2048]{1,0:T(8,128)(2,1)S(1)} %slice_bitcast_fusion.14), channel_id=1, source_target_pairs={{0,8},{4,12},{8,0},{12,4},{16,24},{20,28},{24,16},{28,20},{1,9},{5... | collective-permute-start | bytes 1572872 | tf_op jit(solution)/shard_map/ppermute | solution.py:376
  385.2 40.4 %collective-permute-start.43 = (bf16[2,64,2048]{2,1,0:T(8,128)(2,1)S(1)}, bf16[2,64,2048]{2,1,0:T(8,128)(2,1)S(1)}, u32[]{:S(2)}, u32[]{:S(2)}) collective-permute-start(bf16[2,64,2048]{2,1,0:T(8,128)(2,1)S(1)} %slice_bitcast_fusion.12), channel_id=1, source_target_pairs={{0,2},{1,3},{2,0},{3,1},{4,6},{5,7},{6,4},{7,5},{8,10},{9,11},{10,... | collective-permute-start | bytes 1572872 | tf_op jit(solution)/shard_map/ppermute | solution.py:379
  424.7 69.1 %collective-permute-start.78 = (bf16[512,1024]{1,0:T(8,128)(2,1)S(1)}, bf16[512,1024]{1,0:T(8,128)(2,1)S(1)}, u32[]{:S(2)}, u32[]{:S(2)}) collective-permute-start(bf16[512,1024]{1,0:T(8,128)(2,1)S(1)} %add_convert_fusion.3), channel_id=1, source_target_pairs={{0,16},{4,20},{8,24},{12,28},{16,0},{20,4},{24,8},{28,12},{1,17},{... | collective-permute-start | bytes 3145736 | tf_op jit(solution)/shard_map/ppermute | solution.py:376
  425.8 26.0 %collective-permute-start.44 = (bf16[64,2048]{1,0:T(8,128)(2,1)S(1)}, bf16[64,2048]{1,0:T(8,128)(2,1)S(1)}, u32[]{:S(2)}, u32[]{:S(2)}) collective-permute-start(bf16[64,2048]{1,0:T(8,128)(2,1)S(1)} %slice_bitcast_fusion.26), channel_id=1, source_target_pairs={{0,8},{4,12},{8,0},{12,4},{16,24},{20,28},{24,16},{28,20},{1,9},{5... | collective-permute-start | bytes 786440 | tf_op jit(solution)/shard_map/ppermute | solution.py:376
  454.9 15.4 %collective-permute-start.45 = (bf16[64,2048]{1,0:T(8,128)(2,1)S(1)}, bf16[64,2048]{1,0:T(8,128)(2,1)S(1)}, u32[]{:S(2)}, u32[]{:S(2)}) collective-permute-start(bf16[64,2048]{1,0:T(8,128)(2,1)S(1)} %get-tuple-element.126), channel_id=1, source_target_pairs={{0,2},{1,3},{2,0},{3,1},{4,6},{5,7},{6,4},{7,5},{8,10},{9,11},{10,... | collective-permute-start | bytes 786440 | tf_op jit(solution)/shard_map/ppermute | solution.py:379
  467.5 48.7 %collective-permute-start.81 = (bf16[1024,512]{1,0:T(8,128)(2,1)S(1)}, bf16[1024,512]{1,0:T(8,128)(2,1)S(1)}, u32[]{:S(2)}, u32[]{:S(2)}) collective-permute-start(bf16[1024,512]{1,0:T(8,128)(2,1)S(1)} %add_convert_fusion.2), channel_id=1, source_target_pairs={{0,16},{4,20},{8,24},{12,28},{16,0},{20,4},{24,8},{28,12},{1,17},{... | collective-permute-start | bytes 3145736 | tf_op jit(solution)/shard_map/ppermute | solution.py:376
  467.8 49.1 %collective-permute-start.48 = (bf16[64,2048]{1,0:T(8,128)(2,1)S(1)}, bf16[64,2048]{1,0:T(8,128)(2,1)S(1)}, u32[]{:S(2)}, u32[]{:S(2)}) collective-permute-start(bf16[64,2048]{1,0:T(8,128)(2,1)S(1)} %get-tuple-element.124), channel_id=1, source_target_pairs={{0,8},{4,12},{8,0},{12,4},{16,24},{20,28},{24,16},{28,20},{1,9},{5... | collective-permute-start | bytes 786440 | tf_op jit(solution)/shard_map/ppermute | solution.py:376
  470.3 37.9 %collective-permute-start.46 = (bf16[128,2048]{1,0:T(8,128)(2,1)S(1)}, bf16[128,2048]{1,0:T(8,128)(2,1)S(1)}, u32[]{:S(2)}, u32[]{:S(2)}) collective-permute-start(bf16[128,2048]{1,0:T(8,128)(2,1)S(1)} %pad_maximum_fusion.35), channel_id=1, source_target_pairs={{0,8},{4,12},{8,0},{12,4},{16,24},{20,28},{24,16},{28,20},{1,9},{5... | collective-permute-start | bytes 1572872 | tf_op jit(solution)/shard_map/ppermute | solution.py:376
  472.5 51.2 %collective-permute-start.76 = (bf16[256,1024]{1,0:T(8,128)(2,1)S(1)}, bf16[256,1024]{1,0:T(8,128)(2,1)S(1)}, u32[]{:S(2)}, u32[]{:S(2)}) collective-permute-start(bf16[256,1024]{1,0:T(8,128)(2,1)S(1)} %slice.714), channel_id=1, source_target_pairs={{0,8},{4,12},{8,0},{12,4},{16,24},{20,28},{24,16},{28,20},{1,9},{5... | collective-permute-start | bytes 1572872 | tf_op jit(solution)/shard_map/ppermute | solution.py:376
  495.6 39.3 %collective-permute-start.79 = (bf16[256,1024]{1,0:T(8,128)(2,1)S(1)}, bf16[256,1024]{1,0:T(8,128)(2,1)S(1)}, u32[]{:S(2)}, u32[]{:S(2)}) collective-permute-start(bf16[256,1024]{1,0:T(8,128)(2,1)S(1)} %slice.713), channel_id=1, source_target_pairs={{0,8},{4,12},{8,0},{12,4},{16,24},{20,28},{24,16},{28,20},{1,9},{5... | collective-permute-start | bytes 1572872 | tf_op jit(solution)/shard_map/ppermute | solution.py:376
  508.3 28.3 %collective-permute-start.47 = (bf16[256,2048]{1,0:T(8,128)(2,1)S(1)}, bf16[256,2048]{1,0:T(8,128)(2,1)S(1)}, u32[]{:S(2)}, u32[]{:S(2)}) collective-permute-start(bf16[256,2048]{1,0:T(8,128)(2,1)S(1)} %pad_maximum_fusion.9), channel_id=1, source_target_pairs={{0,1},{1,0},{2,3},{3,2},{4,5},{5,4},{6,7},{7,6},{8,9},{9,8},{10,11... | collective-permute-start | bytes 3145736 | tf_op jit(solution)/shard_map/ppermute | solution.py:379
  516.8 27.6 %collective-permute-start.82 = (bf16[1024,256]{1,0:T(8,128)(2,1)S(1)}, bf16[1024,256]{1,0:T(8,128)(2,1)S(1)}, u32[]{:S(2)}, u32[]{:S(2)}) collective-permute-start(bf16[1024,256]{1,0:T(8,128)(2,1)S(1)} %slice.712), channel_id=1, source_target_pairs={{0,8},{4,12},{8,0},{12,4},{16,24},{20,28},{24,16},{28,20},{1,9},{5... | collective-permute-start | bytes 1572872 | tf_op jit(solution)/shard_map/ppermute | solution.py:376
  518.1 18.7 %collective-permute-start.49 = (bf16[128,2048]{1,0:T(8,128)(2,1)S(1)}, bf16[128,2048]{1,0:T(8,128)(2,1)S(1)}, u32[]{:S(2)}, u32[]{:S(2)}) collective-permute-start(bf16[128,2048]{1,0:T(8,128)(2,1)S(1)} %pad_maximum_fusion.36), channel_id=1, source_target_pairs={{0,2},{1,3},{2,0},{3,1},{4,6},{5,7},{6,4},{7,5},{8,10},{9,11},{10,... | collective-permute-start | bytes 1572872 | tf_op jit(solution)/shard_map/ppermute | solution.py:379
  561.9 106.2 %collective-permute-start.68 = (bf16[1024,256]{0,1:T(8,128)(2,1)}, bf16[1024,256]{0,1:T(8,128)(2,1)}, u32[]{:S(2)}, u32[]{:S(2)}) collective-permute-start(bf16[1024,256]{0,1:T(8,128)(2,1)} %convolution_convert_fusion.4), channel_id=1, source_target_pairs={{0,4},{4,0},{8,12},{12,8},{16,20},{20,16},{24,28},{28,24},{1,5},{5... | collective-permute-start | bytes 1572872 | tf_op jit(solution)/shard_map/ppermute | solution.py:376
  607.1 32.8 %collective-permute-start.51 = (f32[2,2,2,2,2,64]{5,4,3,2,1,0:T(2,128)S(1)}, f32[2,2,2,2,2,64]{5,4,3,2,1,0:T(2,128)S(1)}, u32[]{:S(2)}, u32[]{:S(2)}) collective-permute-start(f32[2,2,2,2,2,64]{5,4,3,2,1,0:T(2,128)S(1)} %constant_dynamic-update-slice_fusion.45), channel_id=1, source_target_pairs={{0,1},{1,0},{2,3},{3,2},{4,5},{5,4},{6,7},{7,6},{8,9},{9,8},{10,11... | collective-permute-start | bytes 24584 | tf_op jit(solution)/shard_map/ppermute | solution.py:379
  637.6 34.2 %collective-permute-start.71 = (bf16[256,1024]{1,0:T(8,128)(2,1)}, bf16[256,1024]{1,0:T(8,128)(2,1)}, u32[]{:S(2)}, u32[]{:S(2)}) collective-permute-start(bf16[256,1024]{1,0:T(8,128)(2,1)} %fusion.44), channel_id=1, source_target_pairs={{0,4},{4,0},{8,12},{12,8},{16,20},{20,16},{24,28},{28,24},{1,5},{5... | collective-permute-start | bytes 1572872 | tf_op jit(solution)/shard_map/ppermute | solution.py:376
  662.9 15.2 %collective-permute-start.65 = (bf16[1024,256]{0,1:T(8,128)(2,1)}, bf16[1024,256]{0,1:T(8,128)(2,1)}, u32[]{:S(2)}, u32[]{:S(2)}) collective-permute-start(bf16[1024,256]{0,1:T(8,128)(2,1)} %convolution_convert_fusion.5), channel_id=1, source_target_pairs={{0,4},{4,0},{8,12},{12,8},{16,20},{20,16},{24,28},{28,24},{1,5},{5... | collective-permute-start | bytes 1572872 | tf_op jit(solution)/shard_map/ppermute | solution.py:376
  663.4 23.6 %collective-permute-start.62 = (bf16[1024,256]{0,1:T(8,128)(2,1)}, bf16[1024,256]{0,1:T(8,128)(2,1)}, u32[]{:S(2)}, u32[]{:S(2)}) collective-permute-start(bf16[1024,256]{0,1:T(8,128)(2,1)} %convolution_convert_fusion.6), channel_id=1, source_target_pairs={{0,4},{4,0},{8,12},{12,8},{16,20},{20,16},{24,28},{28,24},{1,5},{5... | collective-permute-start | bytes 1572872 | tf_op jit(solution)/shard_map/ppermute | solution.py:376
  668.0 57.0 %collective-permute-start.54 = (bf16[2,256,2048]{2,1,0:T(8,128)(2,1)S(1)}, bf16[2,256,2048]{2,1,0:T(8,128)(2,1)S(1)}, u32[]{:S(2)}, u32[]{:S(2)}) collective-permute-start(bf16[2,256,2048]{2,1,0:T(8,128)(2,1)S(1)} %slice_bitcast_fusion), channel_id=1, source_target_pairs={{0,1},{1,0},{2,3},{3,2},{4,5},{5,4},{6,7},{7,6},{8,9},{9,8},{10,11... | collective-permute-start | bytes 6291464 | tf_op jit(solution)/shard_map/ppermute | solution.py:379
  670.6 31.6 %collective-permute-start.69 = (bf16[512,256]{0,1:T(8,128)(2,1)S(1)}, bf16[512,256]{0,1:T(8,128)(2,1)S(1)}, u32[]{:S(2)}, u32[]{:S(2)}) collective-permute-start(bf16[512,256]{0,1:T(8,128)(2,1)S(1)} %add_convert_fusion.7), channel_id=1, source_target_pairs={{0,16},{4,20},{8,24},{12,28},{16,0},{20,4},{24,8},{28,12},{1,17},{... | collective-permute-start | bytes 786440 | tf_op jit(solution)/shard_map/ppermute | solution.py:376
  673.3 34.5 %collective-permute-start.72 = (bf16[256,512]{1,0:T(8,128)(2,1)S(1)}, bf16[256,512]{1,0:T(8,128)(2,1)S(1)}, u32[]{:S(2)}, u32[]{:S(2)}) collective-permute-start(bf16[256,512]{1,0:T(8,128)(2,1)S(1)} %add_convert_fusion.6), channel_id=1, source_target_pairs={{0,16},{4,20},{8,24},{12,28},{16,0},{20,4},{24,8},{28,12},{1,17},{... | collective-permute-start | bytes 786440 | tf_op jit(solution)/shard_map/ppermute | solution.py:376
  679.5 33.9 %collective-permute-start.66 = (bf16[512,256]{0,1:T(8,128)(2,1)S(1)}, bf16[512,256]{0,1:T(8,128)(2,1)S(1)}, u32[]{:S(2)}, u32[]{:S(2)}) collective-permute-start(bf16[512,256]{0,1:T(8,128)(2,1)S(1)} %add_convert_fusion.8), channel_id=1, source_target_pairs={{0,16},{4,20},{8,24},{12,28},{16,0},{20,4},{24,8},{28,12},{1,17},{... | collective-permute-start | bytes 786440 | tf_op jit(solution)/shard_map/ppermute | solution.py:376
  688.4 30.2 %collective-permute-start.63 = (bf16[512,256]{0,1:T(8,128)(2,1)S(1)}, bf16[512,256]{0,1:T(8,128)(2,1)S(1)}, u32[]{:S(2)}, u32[]{:S(2)}) collective-permute-start(bf16[512,256]{0,1:T(8,128)(2,1)S(1)} %add_convert_fusion.9), channel_id=1, source_target_pairs={{0,16},{4,20},{8,24},{12,28},{16,0},{20,4},{24,8},{28,12},{1,17},{... | collective-permute-start | bytes 786440 | tf_op jit(solution)/shard_map/ppermute | solution.py:376
  708.9 14.9 %collective-permute-start.70 = (bf16[256,256]{0,1:T(8,128)(2,1)S(1)}, bf16[256,256]{0,1:T(8,128)(2,1)S(1)}, u32[]{:S(2)}, u32[]{:S(2)}) collective-permute-start(bf16[256,256]{0,1:T(8,128)(2,1)S(1)} %slice.716), channel_id=1, source_target_pairs={{0,8},{4,12},{8,0},{12,4},{16,24},{20,28},{24,16},{28,20},{1,9},{5... | collective-permute-start | bytes 393224 | tf_op jit(solution)/shard_map/ppermute | solution.py:376
  709.0 15.2 %collective-permute-start.73 = (bf16[256,256]{1,0:T(8,128)(2,1)S(1)}, bf16[256,256]{1,0:T(8,128)(2,1)S(1)}, u32[]{:S(2)}, u32[]{:S(2)}) collective-permute-start(bf16[256,256]{1,0:T(8,128)(2,1)S(1)} %slice.715), channel_id=1, source_target_pairs={{0,8},{4,12},{8,0},{12,4},{16,24},{20,28},{24,16},{28,20},{1,9},{5... | collective-permute-start | bytes 393224 | tf_op jit(solution)/shard_map/ppermute | solution.py:376
  721.7 38.3 %collective-permute-start.64 = (bf16[256,256]{0,1:T(8,128)(2,1)}, bf16[256,256]{0,1:T(8,128)(2,1)}, u32[]{:S(2)}, u32[]{:S(2)}) collective-permute-start(bf16[256,256]{0,1:T(8,128)(2,1)} %slice.718), channel_id=1, source_target_pairs={{0,8},{4,12},{8,0},{12,4},{16,24},{20,28},{24,16},{28,20},{1,9},{5... | collective-permute-start | bytes 393224 | tf_op jit(solution)/shard_map/ppermute | solution.py:376
  727.8 14.2 %collective-permute-start.55 = (bf16[128,2048]{1,0:T(8,128)(2,1)}, bf16[128,2048]{1,0:T(8,128)(2,1)}, u32[]{:S(2)}, u32[]{:S(2)}) collective-permute-start(bf16[128,2048]{1,0:T(8,128)(2,1)} %slice_bitcast_fusion.10), channel_id=1, source_target_pairs={{0,8},{4,12},{8,0},{12,4},{16,24},{20,28},{24,16},{28,20},{1,9},{5... | collective-permute-start | bytes 1572872 | tf_op jit(solution)/shard_map/ppermute | solution.py:376
  729.5 14.6 %collective-permute-start.57 = (bf16[2,64,2048]{2,1,0:T(8,128)(2,1)}, bf16[2,64,2048]{2,1,0:T(8,128)(2,1)}, u32[]{:S(2)}, u32[]{:S(2)}) collective-permute-start(bf16[2,64,2048]{2,1,0:T(8,128)(2,1)} %slice_bitcast_fusion.8), channel_id=1, source_target_pairs={{0,2},{1,3},{2,0},{3,1},{4,6},{5,7},{6,4},{7,5},{8,10},{9,11},{10,... | collective-permute-start | bytes 1572872 | tf_op jit(solution)/shard_map/ppermute | solution.py:379
  (172 other events, 1634.3 us)

commit v2 on v0

--- a/solution.py
+++ b/solution.py
@@ -1,6 +1,10 @@
 import jax
 import jax.numpy as jnp
 from jax import lax
+from jax.experimental.layout import Layout, with_layout_constraint
+from jax.experimental import pallas as pl
+from jax.experimental.pallas import tpu as pltpu
+from jax.sharding import Mesh
 from jax.sharding import PartitionSpec as P
 
 HEAD = 128
@@ -339,40 +343,674 @@
     )
 
 
+VMEM_BYTES = 56 * 2**20
+BITS = ("zh", "zl", "x", "y", "c")
+
+
+def turn(v, table):
+    return v * table[:, :HEAD] + pltpu.roll(v, HEAD // 2, 1) * table[:, HEAD:]
+
+
+def turn_back(g, table):
+    return g * table[:, :HEAD] - pltpu.roll(g, HEAD // 2, 1) * table[:, HEAD:]
+
+
+def dot_last(left, right):
+    return lax.dot_general(
+        left, right, (((1,), (1,)), ((), ())), preferred_element_type=jnp.float32
+    )
+
+
+def dot_first(left, right):
+    return lax.dot_general(
+        left, right, (((0,), (0,)), ((), ())), preferred_element_type=jnp.float32
+    )
+
+
+def attend_kernel(
+    heads, proj_ref, inv_ref, table_ref, place_ref, kp_ref, gain_ref,
+    mixed_ref, o_ref, lse_ref, q_ref, k_ref, v_ref,
+):
+    bf16 = jnp.bfloat16
+    width = heads * HEAD
+    scale = HEAD ** (-0.5)
+
+    def rows(ref, h, cols=slice(None)):
+        v = ref[:, h, :, cols]
+        return v.reshape(v.shape[0] * v.shape[1], v.shape[2])
+
+    def put(ref, h, cols, v):
+        ref[:, h, :, cols] = v.reshape(ref.shape[0], ref.shape[2], v.shape[1])
+
+    for h in range(2):
+        table = rows(table_ref, h)
+        inv = rows(inv_ref, h)
+        place = rows(place_ref, h)
+        masks = [
+            (kp_ref[e] >= place[:, 1:2]) & (kp_ref[e] <= place[:, 0:1]) for e in range(h + 1)
+        ]
+        for head in range(heads):
+            cols = slice(head * HEAD, (head + 1) * HEAD)
+            key_cols = slice(width + head * HEAD, width + (head + 1) * HEAD)
+            value_cols = slice(2 * width + head * HEAD, 2 * width + (head + 1) * HEAD)
+            query = turn(rows(proj_ref, h, cols) * inv[:, 0:1] * gain_ref[0:1, cols], table)
+            key = turn(rows(proj_ref, h, key_cols) * inv[:, 1:2] * gain_ref[1:2, cols], table)
+            query = query.astype(bf16)
+            put(q_ref, h, cols, query)
+            put(k_ref, h, cols, key.astype(bf16))
+            put(v_ref, h, cols, rows(proj_ref, h, value_cols).astype(bf16))
+            scores = [
+                jnp.where(masks[e], dot_last(query, rows(k_ref, e, cols)), NEGATIVE)
+                for e in range(h + 1)
+            ]
+            top = scores[0].max(axis=-1, keepdims=True)
+            if h:
+                top = jnp.maximum(top, scores[1].max(axis=-1, keepdims=True))
+            spread = [jnp.exp((v - top) * scale) for v in scores]
+            total = sum(v.sum(axis=-1, keepdims=True) for v in spread)
+            mixed = sum(
+                jnp.dot(p.astype(bf16), rows(v_ref, e, cols), preferred_element_type=jnp.float32)
+                for e, p in enumerate(spread)
+            )
+            mixed = mixed / total
+            put(o_ref, h, cols, mixed)
+            put(mixed_ref, h, cols, mixed.astype(bf16))
+            put(lse_ref, h, slice(head, head + 1), top * scale + jnp.log(total))
+
+
+def attend_back_kernel(
+    heads, q_ref, k_ref, v_ref, o_ref, lse_ref, g_ref, table_ref, place_ref, kp_ref,
+    yq_ref, yk_ref, dv_ref, acc_k, acc_v,
+):
+    f32 = jnp.float32
+    bf16 = jnp.bfloat16
+    scale = HEAD ** (-0.5)
+
+    def rows(ref, h, cols=slice(None)):
+        v = ref[:, h, :, cols]
+        return v.reshape(v.shape[0] * v.shape[1], v.shape[2])
+
+    def put(ref, h, cols, v):
+        ref[:, h, :, cols] = v.reshape(ref.shape[0], ref.shape[2], v.shape[1])
+
+    for head in range(heads):
+        cols = slice(head * HEAD, (head + 1) * HEAD)
+        for h in range(2):
+            query = rows(q_ref, h, cols)
+            grad = rows(g_ref, h, cols)
+            delta = jnp.sum(grad.astype(f32) * rows(o_ref, h, cols), axis=-1, keepdims=True)
+            place = rows(place_ref, h)
+            lse = rows(lse_ref, h, slice(head, head + 1))
+            query_grad = 0.0
+            for e in range(h + 1):
+                key, value, kp = rows(k_ref, e, cols), rows(v_ref, e, cols), kp_ref[e]
+                allowed = (kp >= place[:, 1:2]) & (kp <= place[:, 0:1])
+                scores = jnp.where(allowed, dot_last(query, key) * scale, NEGATIVE)
+                weights = jnp.exp(scores - lse)
+                score_grad = (weights * (dot_last(grad, value) - delta) * scale).astype(bf16)
+                query_grad += jnp.dot(score_grad, key, preferred_element_type=f32)
+                key_part = dot_first(score_grad, query)
+                value_part = dot_first(weights.astype(bf16), grad)
+                if h > e:
+                    key_part += acc_k[...]
+                    value_part += acc_v[...]
+                elif h == 0:
+                    acc_k[...] = key_part
+                    acc_v[...] = value_part
+                    continue
+                put(yk_ref, e, cols, turn_back(key_part, rows(table_ref, e)))
+                put(dv_ref, e, cols, value_part.astype(bf16))
+            put(yq_ref, h, cols, turn_back(query_grad, rows(table_ref, h)))
+
+
+def feed_back_kernel(
+    zl_ref, rows_ref, wg_ref, wu_ref, wd_ref, gate_ref, up_ref,
+    gg_ref, ug_ref, own_ref, other0_ref, other1_ref, acc_ref,
+):
+    f32 = jnp.float32
+    bf16 = jnp.bfloat16
+    step = pl.program_id(0)
+    half = rows_ref.shape[0] // 2
+    for part in (1, 0):
+        at = slice(part * half, (part + 1) * half)
+        act_grad = dot_last(rows_ref[at, :], wd_ref[...])
+        gate, up = gate_ref[at, :], up_ref[at, :]
+        sig = jax.nn.sigmoid(gate)
+        up_low = (act_grad * gate * sig).astype(bf16)
+        gate_low = (act_grad * up * sig * (1.0 + gate * (1.0 - sig))).astype(bf16)
+        ug_ref[at, :] = up_low
+        gg_ref[at, :] = gate_low
+        value = dot_last(gate_low, wg_ref[...]) + dot_last(up_low, wu_ref[...])
+
+        @pl.when(step == 0)
+        def _():
+            acc_ref[at, :] = value
+
+        @pl.when(step == 1)
+        def _():
+            total = (acc_ref[at, :] + value).astype(bf16)
+            if part:
+                other0_ref[...] = total[: half // 2]
+                other1_ref[...] = total[half // 2 :]
+            else:
+                own_ref[...] = total
+
+
+def mixed_back_kernel(zl_ref, rows_ref, weight_ref, out_ref):
+    out_ref[...] = dot_last(rows_ref[...], weight_ref[...]).astype(out_ref.dtype)
+
+
+def grads_kernel(count, ids_ref, features_ref, right_ref, *refs):
+    value = dot_first(features_ref[...], right_ref[...])
+    for ref in refs[:count]:
+        value = value + ref[...].astype(jnp.float32)
+    refs[count][...] = value.astype(refs[count].dtype)
+
+
+def grads(features, right, ids, *terms, kind=jnp.bfloat16):
+    tokens, units = right.shape
+    block = features.shape[1] // 8
+    count = ids.shape[0]
+    return pl.pallas_call(
+        lambda *refs: grads_kernel(len(terms), *refs),
+        grid_spec=pltpu.PrefetchScalarGridSpec(
+            num_scalar_prefetch=1,
+            grid=(count,),
+            in_specs=[
+                pl.BlockSpec((tokens, block), lambda i, ids: (0, ids[i])),
+                pl.BlockSpec((tokens, units), lambda i, ids: (0, 0)),
+            ]
+            + [
+                pl.BlockSpec((block, units), lambda i, ids, first=first: (first + i, 0))
+                for _, first in terms
+            ],
+            out_specs=pl.BlockSpec((block, units), lambda i, ids: (i, 0)),
+        ),
+        out_shape=jax.ShapeDtypeStruct((count * block, units), kind),
+        compiler_params=pltpu.CompilerParams(vmem_limit_bytes=VMEM_BYTES),
+        cost_estimate=pl.CostEstimate(flops=0, bytes_accessed=0, transcendentals=0),
+        name="grads",
+    )(ids, features, right, *(term for term, _ in terms))
+
+
+def assemble_kernel(moves, *refs):
+    pieces, out_ref, sems = refs[:-2], refs[-2], refs[-1]
+    copies = [
+        pltpu.make_async_copy(
+            pieces[piece].at[pl.ds(first, rows)], out_ref.at[pl.ds(to, rows)], sems.at[index]
+        )
+        for index, (piece, first, rows, to) in enumerate(moves)
+    ]
+    for copy in copies:
+        copy.start()
+    for copy in copies:
+        copy.wait()
+
+
+def assemble(pieces, moves):
+    rows = sum(move[2] for move in moves)
+    return pl.pallas_call(
+        lambda *refs: assemble_kernel(moves, *refs),
+        in_specs=[pl.BlockSpec(memory_space=pltpu.VMEM)] * len(pieces),
+        out_specs=pl.BlockSpec(memory_space=pl.ANY),
+        out_shape=jax.ShapeDtypeStruct((rows, pieces[0].shape[1]), pieces[0].dtype),
+        scratch_shapes=[pltpu.SemaphoreType.DMA((len(moves),))],
+        compiler_params=pltpu.CompilerParams(vmem_limit_bytes=VMEM_BYTES),
+        cost_estimate=pl.CostEstimate(flops=0, bytes_accessed=0, transcendentals=0),
+        name="assemble",
+    )(*pieces)
+
+
+def both(*values):
+    return lax.optimization_barrier(values)
+
+
+def grouped(
+    inputs,
+    documents,
+    query_weight,
+    key_weight,
+    value_weight,
+    output_weight,
+    query_gain,
+    key_gain,
+    attention_gain,
+    gate_weight,
+    up_weight,
+    down_weight,
+    feed_gain,
+    cotangent,
+):
+    f32 = jnp.float32
+    bf16 = jnp.bfloat16
+    row_count, seq_count, width = inputs.shape
+    half_count = 2 * row_count
+    half_all = 8 * half_count
+    all_count = 2 * half_all
+    block = width // 8
+    zh, zl, x, y, c = (lax.axis_index(name) for name in BITS)
+    s = 4 * zh + 2 * zl + x
+    t = 2 * y + c
+    sequence = 2 * zh + x
+
+    def swap(v, name):
+        return lax.ppermute(v, name, ((0, 1), (1, 0)))
+
+    def to_sequence(v):
+        v = lax.all_to_all(jnp.transpose(v, (1, 0, 2)), ("zh", "x"), 0, 0, tiled=True)
+        return v.reshape(2 * half_count, width)
+
+    def from_sequence(v):
+        v = v.astype(bf16).reshape(4, row_count, width)
+        v = lax.all_to_all(v, ("zh", "x"), 0, 0, tiled=True)
+        return jnp.transpose(v, (1, 0, 2)).astype(f32)
+
+    def gather(a, late=None):
+        a0, b0 = a[:half_count], a[half_count:]
+        a1, b2 = both(swap(a0, "y"), swap(b0, "zl"))
+        a01, b02 = jnp.concatenate([a0, a1]), jnp.concatenate([b0, b2])
+        if late is None:
+            a01, b02 = both(a01, b02)
+        else:
+            a01, b02, late = both(a01, b02, late)
+        a01_c, b02_c = swap(a01, "c"), swap(b02, "c")
+        a23, b13 = both(swap(a01, "zl"), swap(b02, "y"))
+        a23_c, b13_c = both(swap(a23, "c"), swap(b13, "c"))
+        k = half_count
+        v = assemble(
+            (a01, a23, b02, b13, a01_c, a23_c, b02_c, b13_c),
+            [
+                move
+                for dc in range(2)
+                for move in (
+                    (4 * dc, 0, 2 * k, 8 * dc * k),
+                    (4 * dc + 1, 0, 2 * k, (8 * dc + 2) * k),
+                    (4 * dc + 2, 0, k, (8 * dc + 4) * k),
+                    (4 * dc + 3, 0, k, (8 * dc + 5) * k),
+                    (4 * dc + 2, k, k, (8 * dc + 6) * k),
+                    (4 * dc + 3, k, k, (8 * dc + 7) * k),
+                )
+            ],
+        )
+        return v if late is None else (v, late)
+
+    def swap_zy(v):
+        return lax.ppermute(v, ("zl", "y"), ((0, 3), (3, 0), (1, 2), (2, 1)))
+
+    def gather_direct(a, late):
+        others = both(swap(a, "y"), swap(a, "zl"), swap_zy(a), swap(a, "c"), late)
+        own, late = (a, *others[:3]), others[4]
+        crossed = both(others[3], *(swap(v, "c") for v in own[1:]))
+        k = half_count
+        v = assemble(
+            (*own, *crossed),
+            [
+                (4 * dc + chip, h * k, k, (8 * dc + 4 * h + chip) * k)
+                for dc in range(2)
+                for h in range(2)
+                for chip in range(4)
+            ],
+        )
+        return v, late
+
+    def scatter_direct(own, *other):
+        other = both(*(swap(v, "c") for v in other))
+        p = [
+            (v.astype(f32) + w.astype(f32)).astype(bf16)
+            for v, w in zip(own.reshape(2, 4 * half_count, width), other)
+        ]
+        k = half_count
+        mine, *sent = (
+            jnp.concatenate([v[chip * k : (chip + 1) * k] for v in p]) for chip in range(4)
+        )
+        sent = both(swap(sent[0], "y"), swap(sent[1], "zl"), swap_zy(sent[2]))
+        return sum(v.astype(f32) for v in (mine, *sent))
+
+    def scatter(own, *other):
+        a, b = own.reshape(2, 4 * half_count, width)
+        a_c, b_c = both(*(swap(v, "c") for v in other))
+        a = (a.astype(f32) + a_c.astype(f32)).astype(bf16).reshape(2, 2 * half_count, width)
+        b = (b.astype(f32) + b_c.astype(f32)).astype(bf16).reshape(2, 2, half_count, width)
+        a1, b1 = both(swap(a[1], "zl"), swap(b[:, 1], "y"))
+        a = (a[0].astype(f32) + a1.astype(f32)).astype(bf16)
+        b = (b[:, 0].astype(f32) + b1.astype(f32)).astype(bf16)
+        a1, b1 = both(swap(a[half_count:], "y"), swap(b[1], "zl"))
+        a = a[:half_count].astype(f32) + a1.astype(f32)
+        b = b[0].astype(f32) + b1.astype(f32)
+        return jnp.concatenate([a, b])
+
+    def times(rows, weight, dims):
+        parts = [
+            jnp.einsum(dims, v, weight, preferred_element_type=f32).astype(bf16)
+            for v in (rows[half_all:], rows[:half_all])
+        ]
+        return parts[1], *jnp.split(parts[0], 2)
+
+    def group_sum(v):
+        v = v.reshape(-1, 2, 2, 2, 2, half_count)
+        v = v + swap(v, "c")[:, ::-1]
+        v = v + swap(v, "y")[:, :, :, :, ::-1]
+        v = v + swap(v, "zl")[:, :, :, ::-1]
+        return v.reshape(-1, all_count)
+
+    ids_x, ids_zh, ids_zl = (
+        s ^ jnp.array(bits, jnp.int32) for bits in ((1, 3, 5, 7), (4, 6), (0, 2))
+    )
+
+    def grads_x(features, right):
+        return grads(features, right, ids_x)
+
+    def grads_zh(features, right, far):
+        return grads(features, right, ids_zh, (far, 2))
+
+    def finish(features, right, far, sent):
+        kept = grads(features, right, ids_zl, (far, 0), (sent, 0))
+        return kept[:block], swap(kept[block:], "zl")
+
+    def joined(mine, other, transposed=False):
+        mine, other = mine.astype(f32), other.astype(f32)
+        if transposed:
+            mine, other = mine.T, other.T
+        axis = 0 if transposed else 1
+        return jnp.where(
+            zl == 0,
+            jnp.concatenate([mine, other], axis=axis),
+            jnp.concatenate([other, mine], axis=axis),
+        )
+
+    def zl_half(w, axis):
+        size = w.shape[axis] // 2
+        return lax.dynamic_slice_in_dim(w, zl * size, size, axis)
+
+    rows_in = to_sequence(inputs)
+    weights = (
+        query_weight, key_weight, value_weight, output_weight, gate_weight, up_weight, down_weight
+    )
+    whole, (cotangent, weights) = gather(rows_in, (cotangent, weights))
+    (
+        query_weight, key_weight, value_weight, output_weight, gate_weight, up_weight, down_weight
+    ) = weights
+    wqkv = jnp.concatenate([zl_half(w, 1) for w in (query_weight, key_weight, value_weight)], 1)
+    wo = zl_half(output_weight, 0)
+    wg, wu, wd = zl_half(gate_weight, 1), zl_half(up_weight, 1), zl_half(down_weight, 0)
+    gq, gk = zl_half(query_gain, 0), zl_half(key_gain, 0)
+    heads_width = wo.shape[0]
+    heads = heads_width // HEAD
+
+    whole, grad_top = both(whole, to_sequence(cotangent))
+    grad_top = grad_top.astype(f32)
+
+    def gathered_order(v):
+        v = v.reshape(2, 2, 2, 2, 2, row_count)
+        for axis, bit in ((1, zl), (3, y), (4, c)):
+            v = jnp.where(bit == 1, jnp.flip(v, axis), v)
+        return jnp.transpose(v, (4, 0, 1, 3, 2, 5)).reshape(all_count)
+
+    doc_row = lax.dynamic_index_in_dim(documents, sequence, 0, keepdims=False)
+    places = gathered_order(jnp.arange(all_count, dtype=jnp.int32))
+    docs = gathered_order(doc_row)
+    starts = jnp.sum((doc_row[None, :] < docs[:, None]).astype(jnp.int32), axis=-1)
+    cosine, sine_part = rope_tables(places - starts, HEAD)
+    signs = jnp.where(jnp.arange(HEAD) < HEAD // 2, -1.0, 1.0).astype(f32)
+
+    def by_half(v):
+        return v.reshape(2, 2, half_all // 2, v.shape[-1])
+
+    table = by_half(jnp.concatenate([cosine[:, 0], sine_part[:, 0] * signs], axis=-1))
+    row_places = by_half(jnp.stack([places, starts], axis=-1))
+    key_places = jnp.transpose(places.reshape(2, 2, half_all // 2), (1, 0, 2))
+    key_places = key_places.reshape(2, 1, half_all)
+    head_gain = jnp.stack([gq, gk])
+
+    projected = jnp.einsum("rd,dh->rh", whole, wqkv, preferred_element_type=f32)
+    queries, keys_proj = projected[:, :heads_width], projected[:, heads_width : 2 * heads_width]
+    sums = group_sum(
+        jnp.stack([jnp.sum(queries * queries, axis=-1), jnp.sum(keys_proj * keys_proj, axis=-1)])
+    )
+    inverse = lax.rsqrt(sums / width + EPS).T
+
+    def rows_shape(size, kind):
+        return jax.ShapeDtypeStruct((2, 2, half_all // 2, size), kind)
+
+    mixed_low, attended, log_total, query_low, key_low, value_low = pl.pallas_call(
+        lambda *refs: attend_kernel(heads, *refs),
+        out_shape=[
+            rows_shape(heads_width, bf16),
+            rows_shape(heads_width, f32),
+            rows_shape(heads, f32),
+        ]
+        + [rows_shape(heads_width, bf16)] * 3,
+        compiler_params=pltpu.CompilerParams(vmem_limit_bytes=VMEM_BYTES),
+        cost_estimate=pl.CostEstimate(flops=0, bytes_accessed=0, transcendentals=0),
+        name="attend",
+    )(by_half(projected), by_half(inverse), table, row_places, key_places, head_gain)
+    mixed_low = mixed_low.reshape(all_count, heads_width)
+
+    branch = scatter(*times(mixed_low, wo, "rh,hd->rd"))
+    attn_inv = rms_scale(branch)
+    hidden = rows_in.astype(f32) + branch * attn_inv * attention_gain
+    hidden_whole = gather(hidden.astype(bf16))
+    gate_value = jnp.einsum("rd,df->rf", hidden_whole, wg, preferred_element_type=f32)
+    up_value = jnp.einsum("rd,df->rf", hidden_whole, wu, preferred_element_type=f32)
+    sigmoid_value = jax.nn.sigmoid(gate_value)
+    act_low = (gate_value * sigmoid_value * up_value).astype(bf16)
+    down_value = scatter(*times(act_low, wd, "rf,fd->rd"))
+    feed_inv = rms_scale(down_value)
+    down_low = norm_back(down_value, feed_inv, feed_gain, grad_top).astype(bf16)
+    down_whole, late_hidden = gather(down_low, hidden)
+    layer_out = from_sequence(late_hidden + down_value * feed_inv * feed_gain)
+    down_whole, layer_out = both(down_whole, layer_out)
+
+    down_far = grads_x(down_whole, act_low)
+    down_whole, down_far = both(down_whole, down_far)
+    down_far = swap(down_far, "x")
+    tile = gate_value.shape[1] // 2
+    unit_tile = pl.BlockSpec((all_count, tile), lambda j, z: (0, j))
+    rows_full = pl.BlockSpec((all_count, width), lambda j, z: (0, 0))
+    rows_part = pl.BlockSpec((half_all // 2, width), lambda j, z: (0, 0))
+    rows_half = pl.BlockSpec((half_all, width), lambda j, z: (0, 0))
+    weight_tile = pl.BlockSpec((width, tile), lambda j, z: (0, 2 * z[0] + j))
+    gate_low, up_low, *hidden_part = pl.pallas_call(
+        feed_back_kernel,
+        grid_spec=pltpu.PrefetchScalarGridSpec(
+            num_scalar_prefetch=1,
+            grid=(2,),
+            in_specs=[
+                rows_full,
+                weight_tile,
+                weight_tile,
+                pl.BlockSpec((tile, width), lambda j, z: (2 * z[0] + j, 0)),
+                unit_tile,
+                unit_tile,
+            ],
+            out_specs=[unit_tile, unit_tile, rows_half, rows_part, rows_part],
+            scratch_shapes=[pltpu.VMEM((all_count, width), f32)],
+        ),
+        out_shape=[
+            jax.ShapeDtypeStruct(gate_value.shape, bf16),
+            jax.ShapeDtypeStruct(gate_value.shape, bf16),
+            jax.ShapeDtypeStruct((half_all, width), bf16),
+        ]
+        + [jax.ShapeDtypeStruct((half_all // 2, width), bf16)] * 2,
+        compiler_params=pltpu.CompilerParams(vmem_limit_bytes=VMEM_BYTES),
+        cost_estimate=pl.CostEstimate(flops=0, bytes_accessed=0, transcendentals=0),
+        name="feed_back",
+    )(
+        zl[None], down_whole, gate_weight, up_weight, down_weight, gate_value,
+        up_value,
+    )
+    gate_far = grads_x(hidden_whole, gate_low)
+    hidden_grad = grad_top + scatter_direct(*hidden_part)
+    hidden_grad, gate_far = both(hidden_grad, gate_far)
+    gate_far = swap(gate_far, "x")
+    hidden_grad, down_far = both(hidden_grad, down_far)
+    down_sent = grads_zh(down_whole, act_low, down_far)
+    hidden_grad, down_sent = both(hidden_grad, down_sent)
+    down_sent = swap(down_sent, "zh")
+
+    branch_low = norm_back(branch, attn_inv, attention_gain, hidden_grad).astype(bf16)
+    branch_whole, late_up = gather_direct(branch_low, up_low)
+    up_far = grads_x(hidden_whole, late_up)
+    branch_whole, up_far = both(branch_whole, up_far)
+    up_far = swap(up_far, "x")
+    mixed_grad = pl.pallas_call(
+        mixed_back_kernel,
+        grid_spec=pltpu.PrefetchScalarGridSpec(
+            num_scalar_prefetch=1,
+            grid=(2,),
+            in_specs=[
+                pl.BlockSpec((half_all, width), lambda i, z: (i, 0)),
+                pl.BlockSpec((heads_width, width), lambda i, z: (z[0], 0)),
+            ],
+            out_specs=pl.BlockSpec((half_all, heads_width), lambda i, z: (i, 0)),
+        ),
+        out_shape=jax.ShapeDtypeStruct((all_count, heads_width), bf16),
+        compiler_params=pltpu.CompilerParams(vmem_limit_bytes=VMEM_BYTES),
+        cost_estimate=pl.CostEstimate(flops=0, bytes_accessed=0, transcendentals=0),
+        name="mixed_back",
+    )(zl[None], branch_whole, output_weight)
+
+    yq, yk, value_grad_low = pl.pallas_call(
+        lambda *refs: attend_back_kernel(heads, *refs),
+        out_shape=[rows_shape(heads_width, f32)] * 2 + [rows_shape(heads_width, bf16)],
+        scratch_shapes=[pltpu.VMEM((half_all, HEAD), f32)] * 2,
+        compiler_params=pltpu.CompilerParams(vmem_limit_bytes=VMEM_BYTES),
+        cost_estimate=pl.CostEstimate(flops=0, bytes_accessed=0, transcendentals=0),
+        name="attend_back",
+    )(
+        query_low, key_low, value_low, attended, log_total, by_half(mixed_grad), table,
+        row_places, key_places,
+    )
+    yq, yk, value_grad_low = (
+        v.reshape(all_count, heads_width) for v in (yq, yk, value_grad_low)
+    )
+    query_inv, key_inv = inverse[:, 0:1], inverse[:, 1:2]
+    dots = jnp.stack([jnp.sum(yq * gq * queries, axis=-1), jnp.sum(yk * gk * keys_proj, axis=-1)])
+    late_yq, gate_far, down_sent = both(yq, gate_far, down_sent)
+    down_pair = finish(down_whole, act_low, down_far, down_sent)
+    gate_sent = grads_zh(hidden_whole, gate_low, gate_far)
+    dots, gate_sent, down_keep = both(group_sum(dots), gate_sent, down_pair[0])
+    down_pair = (down_keep, down_pair[1])
+    dots = dots.T
+    gate_sent = swap(gate_sent, "zh")
+    query_grad_low = (
+        query_inv * gq * yq - queries * query_inv**3 * (dots[:, 0:1] / width)
+    ).astype(bf16)
+    key_grad_low = (
+        key_inv * gk * yk - keys_proj * key_inv**3 * (dots[:, 1:2] / width)
+    ).astype(bf16)
+    projected_grad = jnp.concatenate([query_grad_low, key_grad_low, value_grad_low], axis=1)
+    input_part = times(projected_grad, wqkv, "rh,dh->rd")
+    input_own, late_grad = both(input_part[0], projected_grad)
+    in_far = grads_x(whole, late_grad)
+    input_sum, in_far = both(scatter_direct(input_own, *input_part[1:]), in_far)
+    in_far = swap(in_far, "x")
+    input_rows = hidden_grad + input_sum
+    input_rows, up_far, late_mixed, gate_sent = both(input_rows, up_far, mixed_low, gate_sent)
+    up_sent = grads_zh(hidden_whole, up_low, up_far)
+    out_far = grads_x(branch_whole, late_mixed)
+    input_rows, up_sent, out_far, late_yq = both(input_rows, up_sent, out_far, late_yq)
+    up_sent, out_far = swap(up_sent, "zh"), swap(out_far, "x")
+    input_grad = from_sequence(input_rows)
+    gate_pair = finish(hidden_whole, gate_low, gate_far, gate_sent)
+    in_far, gate_keep = both(in_far, gate_pair[0])
+    gate_pair = (gate_keep, gate_pair[1])
+    in_sent = swap(grads_zh(whole, projected_grad, in_far), "zh")
+    up_pair = finish(hidden_whole, up_low, up_far, up_sent)
+    out_far, up_keep = both(out_far, up_pair[0])
+    up_pair = (up_keep, up_pair[1])
+    out_sent = swap(grads_zh(branch_whole, mixed_low, out_far), "zh")
+    in_mine, in_other = finish(whole, projected_grad, in_far, in_sent)
+    out_pair = finish(branch_whole, mixed_low, out_far, out_sent)
+    head_gains = jnp.stack(
+        [jnp.sum(late_yq * queries * query_inv, axis=0), jnp.sum(yk * keys_proj * key_inv, axis=0)]
+    )
+    head_gains = lax.dynamic_update_slice(
+        jnp.zeros((2, width), f32), head_gains, (0, (2 * t + zl) * heads_width)
+    )
+    row_gains = jnp.stack(
+        [
+            jnp.sum(hidden_grad * branch * attn_inv, axis=0),
+            jnp.sum(grad_top * down_value * feed_inv, axis=0),
+        ]
+    )
+    gains = jnp.concatenate([head_gains, row_gains])
+    for name in ("c", "y", "zl"):
+        gains = gains + swap(gains, name)
+    gains, up_keep = both(gains, up_pair[0])
+    up_pair = (up_keep, up_pair[1])
+    gains = gains + swap(gains, "x")
+    gains, in_mine = both(gains, in_mine)
+    gains = gains + swap(gains, "zh")
+    gains = lax.dynamic_slice_in_dim(gains, s * block, block, 1)
+    down_term = joined(*down_pair, True)
+    gate_term = joined(*gate_pair)
+    up_term = joined(*up_pair)
+    out_term = joined(*out_pair, True)
+    query_term, key_term, value_term = (
+        joined(
+            in_mine[:, k * heads_width : (k + 1) * heads_width],
+            in_other[:, k * heads_width : (k + 1) * heads_width],
+        )
+        for k in range(3)
+    )
+    return (
+        layer_out,
+        input_grad,
+        query_term,
+        key_term,
+        value_term,
+        out_term,
+        gate_term,
+        up_term,
+        down_term,
+        gains[0],
+        gains[1],
+        gains[2],
+        gains[3],
+    )
+
+
 def solution(mesh):
+    rows, columns, inner = ("seq", "tp"), ("tp",), ("seq",)
+    step = local
+    if mesh.shape["seq"] == 8 and mesh.shape["tp"] == 4:
+        mesh = Mesh(mesh.devices.reshape(2, 2, 2, 2, 2), BITS)
+        rows, columns, inner = BITS, BITS[3:], BITS[:3]
+        step = grouped
     return jax.shard_map(
-        local,
+        step,
         mesh=mesh,
         in_specs=(
-            P(("seq", "tp"), None, None),
+            P(rows, None, None),
             P(),
-            P(None, "tp"),
-            P(None, "tp"),
-            P(None, "tp"),
-            P("tp", None),
-            P("tp"),
-            P("tp"),
+            P(None, columns),
+            P(None, columns),
+            P(None, columns),
+            P(columns, None),
+            P(columns),
+            P(columns),
             P(),
-            P(None, "tp"),
-            P(None, "tp"),
-            P("tp", None),
+            P(None, columns),
+            P(None, columns),
+            P(columns, None),
             P(),
-            P(("seq", "tp"), None, None),
+            P(rows, None, None),
         ),
         out_specs=(
-            P(("seq", "tp"), None, None),
-            P(("seq", "tp"), None, None),
-            P("seq", "tp"),
-            P("seq", "tp"),
-            P("seq", "tp"),
-            P("tp", "seq"),
-            P("seq", "tp"),
-            P("seq", "tp"),
-            P("tp", "seq"),
-            P("seq"),
-            P("seq"),
-            P("seq"),
-            P("seq"),
+            P(rows, None, None),
+            P(rows, None, None),
+            P(inner, columns),
+            P(inner, columns),
+            P(inner, columns),
+            P(columns, inner),
+            P(inner, columns),
+            P(inner, columns),
+            P(columns, inner),
+            P(inner),
+            P(inner),
+            P(inner),
+            P(inner),
         ),
         check_vma=False,
     )

time: 1500 us -> 652 us (0.43)
  waiting for transfers between devices: 1100 us -> 276 us
  Pallas kernels: 0 us -> 149 us
  matrix products: 167 us -> 34.5 us
  starting transfers between devices: 2.06 us -> 92.7 us
  local copies, waits for them, and re-layouts: 107 us -> 40.9 us
  blocking collectives: 48.1 us -> 0 us
    reduce_scatter x12 -> x0, waiting for transfers between devices: 848 us -> none  [the longest x1 149 us: local(): lax.psum_scatter(up_term.astype(jnp.bfloat16), 'seq', scatter_dimension=0...]
    ppermute x0 -> x79, waiting for transfers between devices: none -> 264 us  [the longest x76 225 us: swap(): return lax.ppermute(v, name, ((0, 1), (1, 0)))]
    all_gather x6 -> x0, waiting for transfers between devices: 198 us -> none  [the longest x1 68.2 us: cycle_values(): lax.all_gather(jnp.transpose(key_low, (1, 0, 2)), 'seq', axis=1, tiled=True)]
    pallas_call x0 -> x23, Pallas kernels: none -> 149 us  [the longest x15 79 us: grads(): pl.pallas_call(lambda *refs: grads_kernel(len(terms), *refs), grid_spec=p...]
    dot_general x49 -> x9, matrix products: 167 us -> 34.5 us  [the longest x6 10.7 us: times(): jnp.einsum(dims, v, weight, preferred_element_type=f32).astype(bf16)]
    ppermute x0 -> x79, starting transfers between devices: none -> 71.2 us  [the longest x76 66.8 us: swap(): return lax.ppermute(v, name, ((0, 1), (1, 0)))]
    unnamed x20 -> x0, waiting for transfers between devices: 50.4 us -> none
    unnamed x1 -> x0, blocking collectives: 36 us -> none
  transfers between devices with their start and end apart: 19 -> 83, of which waited for: 18 -> 51; matrix products, arithmetic and copies ran while one was open for 9% -> 9% of each run, Pallas kernels for 0% -> 12%
where the time goes in v2:
time: 652 us; the launch traced here: 643 us
  waiting for transfers between devices  276 us (42%)
  Pallas kernels  149 us (23%)
  starting transfers between devices  92.7 us (14%)
  other arithmetic  47.4 us (7%)
  local copies, waits for them, and re-layouts  40.9 us (6%)
  matrix products  34.5 us (5%)
    ppermute x76, waiting for transfers between devices, swap(): return lax.ppermute(v, name, ((0, 1), (1, 0)))  225 us
    pallas_call x15, Pallas kernels, grads(): pl.pallas_call(lambda *refs: grads_kernel(len(terms), *refs), grid_spec=p...  79 us
    ppermute x76, starting transfers between devices, swap(): return lax.ppermute(v, name, ((0, 1), (1, 0)))  66.8 us
    ppermute x3, waiting for transfers between devices, swap_zy(): return lax.ppermute(v, ('zl', 'y'), ((0, 3), (3, 0), (1, 2), (2, 1)))  39.4 us
    pallas_call x1, Pallas kernels, grouped(): pl.pallas_call(feed_back_kernel, grid_spec=pltpu.PrefetchScalarGridSpec(n...  25.5 us
    unnamed x153, local copies, waits for them, and re-layouts  20.3 us
    pallas_call x4, Pallas kernels, assemble(): pl.pallas_call(lambda *refs: assemble_kernel(moves, *refs), in_specs=[pl....  17.3 us
  transfers between devices with their start and end apart: 83, of which 51 were waited for; matrix products, arithmetic and copies ran while one was open for 9% of the time, Pallas kernels for 12%

profile of v2, /device:TPU:0, one launch (start us, length us, event | category | flops | bytes accessed | tf_op | source)
XLA Modules:
  0.0 642.9 jit_solution(4549129585116467016)
XLA Ops:
  2.9 6.2 all-to-all-start
  12.0 11.6 %all-to-all-done = bf16[4,32,2048]{2,1,0:T(8,128)(2,1)S(1)} async-done(((bf16[4,32,2048]{2,1,0:T(8,128)(2,1)}), bf16[4,32,2048]{2,1,0:T(8,128)(2,1)S(1)}, u32[]{:S(2)}, u32[]{:S(2)}) %all-to-all-start) | async-done | bytes 524320 | tf_op jit(solution)/shard_map/all_to_all | solution.py:600
  25.4 5.5 collective-permute-done
  39.2 5.1 all-to-all-start.1
  52.6 4.3 assemble.4.refs_1_
  57.2 5.9 fusion.42
  77.1 12.8 %attend.1 = (bf16[2,2,256,256]{3,2,1,0:T(8,128)(2,1)}, f32[2,2,256,256]{3,2,1,0:T(8,128)}, f32[2,2,256,2]{3,2,1,0:T(8,128)}, bf16[2,2,256,256]{3,2,1,0:T(8,128)(...) custom-call(f32[2,2,256,768]{3,2,1,0:T(8,128)} %bitcast.121, f32[2,2,256,2]{3,2,1,0:T(8,128)} %bitcast.138, ...), custom_call_target="tpu_custom_call" | custom-call | tf_op jit(solution)/shard_map/attend/pallas_call | solution.py:775
  99.1 12.3 %collective-permute-done.13 = bf16[128,2048]{1,0:T(8,128)(2,1)S(1)} collective-permute-done((bf16[128,2048]{1,0:T(8,128)(2,1)S(1)}, bf16[128,2048]{1,0:T(8,128)(2,1)S(1)}, u32[]{:S(2)}, u32[]{:S(2)}) %collective-permute-start.13) | collective-permute-done | bytes 524320 | tf_op jit(solution)/shard_map/ppermute | solution.py:597
  115.2 4.1 collective-permute-done.15
  124.4 4.2 collective-permute-done.17
  132.8 7.7 %collective-permute-done.19.refs_1_ = bf16[128,2048]{1,0:T(8,128)(2,1)S(1)} collective-permute-done((bf16[128,2048]{1,0:T(8,128)(2,1)S(1)}, bf16[128,2048]{1,0:T(8,128)(2,1)S(1)}, u32[]{:S(2)}, u32[]{:S(2)}) %collective-permute-start.19) | collective-permute-done | bytes 524320 | tf_op jit(solution)/shard_map/ppermute | solution.py:597
  145.2 4.5 assemble.5.refs_1_
  149.7 7.9 %fusion.2.gate_ref = f32[1024,1024]{1,0:T(8,128)S(1)} fusion(bf16[1024,2048]{1,0:T(8,128)(2,1)} %assemble.5.refs_1_, bf16[2048,2048]{1,0:T(8,128)(2,1)} %wg_ref, s32[]{:T(128)S(6)} %select_n.119), kind=kOutput, calls=%fused_computation.3 | convolution fusion | flops 4294967296 | bytes 12582916 | tf_op jit(solution)/shard_map/rd,df->rf/dot_general | solution.py:793
  157.7 10.0 %multiply_convert_fusion = (bf16[1024,1024]{1,0:T(8,128)(2,1)S(1)}, f32[1024,1024]{1,0:T(8,128)}) fusion(f32[1024,1024]{1,0:T(8,128)S(1)} %fusion.2.gate_ref, bf16[1024,2048]{1,0:T(8,128)(2,1)S(1)} %copy-done.2, bf16[2048,2048]{1,0:T(8,128)(2,1)} %wu_ref, s32[]{:T(128)S(6)} %select_n.119), kind=kOutput, calls=%fused_computation | convolution fusion | flops 4301258752 | bytes 18874372 | tf_op jit(solution)/shard_map/rd,df->rf/dot_general | solution.py:794
  178.1 11.3 %collective-permute-done.27 = bf16[128,2048]{1,0:T(8,128)(2,1)S(1)} collective-permute-done((bf16[128,2048]{1,0:T(8,128)(2,1)S(1)}, bf16[128,2048]{1,0:T(8,128)(2,1)S(1)}, u32[]{:S(2)}, u32[]{:S(2)}) %collective-permute-start.27) | collective-permute-done | bytes 524320 | tf_op jit(solution)/shard_map/ppermute | solution.py:597
  193.3 4.5 collective-permute-done.29
  201.7 4.9 collective-permute-done.31
  209.2 5.6 all-to-all-start.2
  217.3 13.3 %collective-permute-done.33.refs_1_ = bf16[128,2048]{1,0:T(8,128)(2,1)S(1)} collective-permute-done((bf16[128,2048]{1,0:T(8,128)(2,1)S(1)}, bf16[128,2048]{1,0:T(8,128)(2,1)S(1)}, u32[]{:S(2)}, u32[]{:S(2)}) %collective-permute-start.33) | collective-permute-done | bytes 524320 | tf_op jit(solution)/shard_map/ppermute | solution.py:597
  234.3 4.2 assemble.6.refs_1_.rows_ref
  238.5 6.8 %grads.15 = bf16[1024,1024]{1,0:T(8,128)(2,1)} custom-call(s32[4]{0:T(128)} %broadcast_xor_fusion.1.refs_0_, bf16[1024,2048]{1,0:T(8,128)(2,1)} %assemble.6.refs_1_.rows_ref, bf16[1024,1024]{1,0:T(8,128)(2,1)} %copy-done.7), custom_call_target="tpu_custom_call" | custom-call | tf_op jit(solution)/shard_map/grads/pallas_call | solution.py:514
  245.3 25.5 %feed_back.1 = (bf16[1024,1024]{1,0:T(8,128)(2,1)}, bf16[1024,1024]{1,0:T(8,128)(2,1)}, bf16[512,2048]{1,0:T(8,128)(2,1)}, bf16[256,2048]{1,0:T(8,128)(2,1)}, bf16[256,2048]{1,0:T(8,128)(2,1)}) custom-call(s32[1]{0:T(128)} %bitcast.29.zl_ref, bf16[1024,2048]{1,0:T(8,128)(2,1)} %assemble.6.refs_1_.rows_ref, bf16[2048,2048]{1,0:T(8,128)(2,1)} %wg_ref, ...), custom_call_target="tpu_custom_call" | custom-call | tf_op jit(solution)/shard_map/feed_back/pallas_call | solution.py:813
  282.9 6.8 %grads.16 = bf16[1024,1024]{1,0:T(8,128)(2,1)} custom-call(s32[4]{0:T(128)} %broadcast_xor_fusion.1.refs_0_, bf16[1024,2048]{1,0:T(8,128)(2,1)} %assemble.5.refs_1_, bf16[1024,1024]{1,0:T(8,128)(2,1)} %get-tuple-element.190.refs_2_), custom_call_target="tpu_custom_call" | custom-call | tf_op jit(solution)/shard_map/grads/pallas_call | solution.py:514
  293.8 10.7 %collective-permute-done.43 = bf16[128,2048]{1,0:T(8,128)(2,1)S(1)} collective-permute-done((bf16[128,2048]{1,0:T(8,128)(2,1)}, bf16[128,2048]{1,0:T(8,128)(2,1)S(1)}, u32[]{:S(2)}, u32[]{:S(2)}) %collective-permute-start.43) | collective-permute-done | bytes 524320 | tf_op jit(solution)/shard_map/ppermute | solution.py:638
  304.9 14.2 %collective-permute-done.44.refs_3_ = bf16[1024,1024]{1,0:T(8,128)(2,1)S(1)} collective-permute-done((bf16[1024,1024]{1,0:T(8,128)(2,1)S(1)}, bf16[1024,1024]{1,0:T(8,128)(2,1)S(1)}, u32[]{:S(2)}, u32[]{:S(2)}) %collective-permute-start.44) | collective-permute-done | bytes 2097184 | tf_op jit(solution)/shard_map/ppermute | solution.py:597
  320.5 5.1 grads.17
  331.6 8.7 %collective-permute-done.45.refs_1_ = bf16[128,2048]{1,0:T(8,128)(2,1)S(1)} collective-permute-done((bf16[128,2048]{1,0:T(8,128)(2,1)S(1)}, bf16[128,2048]{1,0:T(8,128)(2,1)S(1)}, u32[]{:S(2)}, u32[]{:S(2)}) %collective-permute-start.45) | collective-permute-done | bytes 524320 | tf_op jit(solution)/shard_map/ppermute | solution.py:597
  342.1 9.8 %collective-permute-done.47.refs_3_ = bf16[128,2048]{1,0:T(8,128)(2,1)S(1)} collective-permute-done((bf16[128,2048]{1,0:T(8,128)(2,1)S(1)}, bf16[128,2048]{1,0:T(8,128)(2,1)S(1)}, u32[]{:S(2)}, u32[]{:S(2)}) %collective-permute-start.47) | collective-permute-done | bytes 524320 | tf_op jit(solution)/shard_map/ppermute | solution.py:638
  354.6 6.8 %grads.18 = bf16[1024,1024]{1,0:T(8,128)(2,1)} custom-call(s32[4]{0:T(128)} %broadcast_xor_fusion.1.refs_0_, bf16[1024,2048]{1,0:T(8,128)(2,1)} %assemble.5.refs_1_, bf16[1024,1024]{1,0:T(8,128)(2,1)} %get-tuple-element.210.refs_2_), custom_call_target="tpu_custom_call" | custom-call | tf_op jit(solution)/shard_map/grads/pallas_call | solution.py:514
  363.2 4.3 assemble.7.rows_ref.refs_1_
  371.6 10.1 %attend_back.1 = (f32[2,2,256,256]{3,2,1,0:T(8,128)}, f32[2,2,256,256]{3,2,1,0:T(8,128)}, bf16[2,2,256,256]{3,2,1,0:T(8,128)(2,1)}) custom-call(bf16[2,2,256,256]{3,2,1,0:T(8,128)(2,1)} %get-tuple-element.196.refs_0_, bf16[2,2,256,256]{3,2,1,0:T(8,128)(2,1)} %get-tuple-element.197.refs_1_, bf16[2,2,256,256]{3,2,1,0:T(8,128)(2,1)} %get-tuple-element.198.refs_2_, ...), custom_call_target="tpu_custom_call" | custom-call | tf_op jit(solution)/shard_map/attend_back/pallas_call | solution.py:873
  390.6 11.3 %collective-permute-done.54 = f32[2,2,2,2,2,64]{5,4,3,2,1,0:T(2,128)S(1)} collective-permute-done((f32[2,2,2,2,2,64]{5,4,3,2,1,0:T(2,128)S(1)}, f32[2,2,2,2,2,64]{5,4,3,2,1,0:T(2,128)S(1)}, u32[]{:S(2)}, u32[]{:S(2)}) %collective-permute-start.54) | collective-permute-done | bytes 8224 | tf_op jit(solution)/shard_map/ppermute | solution.py:597
  402.0 4.9 grads.19
  406.9 5.6 grads.20
  435.3 6.3 grads.21
  444.2 16.5 %collective-permute-done.60 = bf16[128,2048]{1,0:T(8,128)(2,1)} collective-permute-done((bf16[128,2048]{1,0:T(8,128)(2,1)}, bf16[128,2048]{1,0:T(8,128)(2,1)}, u32[]{:S(2)}, u32[]{:S(2)}) %collective-permute-start.60) | collective-permute-done | bytes 524320 | tf_op jit(solution)/shard_map/ppermute | solution.py:597
  460.7 18.9 %collective-permute-done.61 = bf16[128,2048]{1,0:T(8,128)(2,1)} collective-permute-done((bf16[128,2048]{1,0:T(8,128)(2,1)}, bf16[128,2048]{1,0:T(8,128)(2,1)}, u32[]{:S(2)}, u32[]{:S(2)}) %collective-permute-start.61) | collective-permute-done | bytes 524320 | tf_op jit(solution)/shard_map/ppermute | solution.py:638
  482.1 4.9 grads.22
  487.1 5.1 grads.23
  494.9 4.5 all-to-all-start.3
  501.6 5.3 grads.25
  513.2 29.8 %collective-permute-done.68.refs_4_ = bf16[512,1024]{1,0:T(8,128)(2,1)} collective-permute-done((bf16[512,1024]{1,0:T(8,128)(2,1)S(1)}, bf16[512,1024]{1,0:T(8,128)(2,1)}, u32[]{:S(2)}, u32[]{:S(2)}) %collective-permute-start.68) | collective-permute-done | bytes 1048608 | tf_op jit(solution)/shard_map/ppermute | solution.py:597
  543.0 5.3 grads.24
  565.8 6.1 collective-permute-done.73.refs_4_
  580.5 4.4 grads.26
  593.8 28.8 %collective-permute-done.71.refs_4_ = bf16[512,768]{1,0:T(8,128)(2,1)} collective-permute-done((bf16[512,768]{1,0:T(8,128)(2,1)}, bf16[512,768]{1,0:T(8,128)(2,1)}, u32[]{:S(2)}, u32[]{:S(2)}) %collective-permute-start.71) | collective-permute-done | bytes 786464 | tf_op jit(solution)/shard_map/ppermute | solution.py:597
  622.5 4.7 grads.27
  631.7 6.3 collective-permute-done.78
  (455 shorter events, 217.1 us)
Async XLA Ops:
  2.9 20.7 %all-to-all-start = ((bf16[4,32,2048]{2,1,0:T(8,128)(2,1)}), bf16[4,32,2048]{2,1,0:T(8,128)(2,1)S(1)}, u32[]{:S(2)}, u32[]{:S(2)}) async-start(bf16[4,32,2048]{2,1,0:T(8,128)(2,1)} %bitcast.120), calls=%async_computation | async-start | bytes 1048576 | tf_op jit(solution)/shard_map/all_to_all | solution.py:600
  34.3 12.7 %collective-permute-start.2 = (bf16[128,2048]{1,0:T(8,128)(2,1)}, bf16[128,2048]{1,0:T(8,128)(2,1)}, u32[]{:S(2)}, u32[]{:S(2)}) collective-permute-start(bf16[128,2048]{1,0:T(8,128)(2,1)} %get-tuple-element.133.refs_0_), channel_id=1, source_target_pairs={{0,8},{8,0},{1,9},{9,1},{2,10},{10,2},{3,11},{11,3},{4,12},{12,4},... | collective-permute-start | bytes 1572872 | tf_op jit(solution)/shard_map/ppermute | solution.py:597
  34.6 12.5 %collective-permute-start.3 = (bf16[128,2048]{1,0:T(8,128)(2,1)}, bf16[128,2048]{1,0:T(8,128)(2,1)}, u32[]{:S(2)}, u32[]{:S(2)}) collective-permute-start(bf16[128,2048]{1,0:T(8,128)(2,1)} %get-tuple-element.134.refs_2_), channel_id=1, source_target_pairs={{0,2},{2,0},{1,3},{3,1},{4,6},{6,4},{5,7},{7,5},{8,10},{10,8},{9,1... | collective-permute-start | bytes 1572872 | tf_op jit(solution)/shard_map/ppermute | solution.py:597
  39.2 18.0 %all-to-all-start.1 = ((bf16[4,32,2048]{2,1,0:T(8,128)(2,1)}), bf16[4,32,2048]{2,1,0:T(8,128)(2,1)S(1)}, u32[]{:S(2)}, u32[]{:S(2)}) async-start(bf16[4,32,2048]{2,1,0:T(8,128)(2,1)} %bitcast.135), calls=%async_computation.1 | async-start | bytes 1048576 | tf_op jit(solution)/shard_map/all_to_all | solution.py:600
  97.4 14.0 %collective-permute-start.13 = (bf16[128,2048]{1,0:T(8,128)(2,1)S(1)}, bf16[128,2048]{1,0:T(8,128)(2,1)S(1)}, u32[]{:S(2)}, u32[]{:S(2)}) collective-permute-start(bf16[128,2048]{1,0:T(8,128)(2,1)S(1)} %slice.313), channel_id=1, source_target_pairs={{0,8},{8,0},{1,9},{9,1},{2,10},{10,2},{3,11},{11,3},{4,12},{12,4},... | collective-permute-start | bytes 1572872 | tf_op jit(solution)/shard_map/ppermute | solution.py:597
  97.5 14.0 %collective-permute-start.14 = (bf16[2,64,2048]{2,1,0:T(8,128)(2,1)S(1)}, bf16[2,64,2048]{2,1,0:T(8,128)(2,1)S(1)}, u32[]{:S(2)}, u32[]{:S(2)}) collective-permute-start(bf16[2,64,2048]{2,1,0:T(8,128)(2,1)S(1)} %slice_bitcast_fusion.3), channel_id=1, source_target_pairs={{0,2},{2,0},{1,3},{3,1},{4,6},{6,4},{5,7},{7,5},{8,10},{10,8},{9,1... | collective-permute-start | bytes 1572872 | tf_op jit(solution)/shard_map/ppermute | solution.py:597
  129.6 10.9 %collective-permute-start.19 = (bf16[128,2048]{1,0:T(8,128)(2,1)S(1)}, bf16[128,2048]{1,0:T(8,128)(2,1)S(1)}, u32[]{:S(2)}, u32[]{:S(2)}) collective-permute-start(bf16[128,2048]{1,0:T(8,128)(2,1)S(1)} %pad_maximum_fusion.7.refs_0_), channel_id=1, source_target_pairs={{0,8},{8,0},{1,9},{9,1},{2,10},{10,2},{3,11},{11,3},{4,12},{12,4},... | collective-permute-start | bytes 1572872 | tf_op jit(solution)/shard_map/ppermute | solution.py:597
  131.7 9.2 %collective-permute-start.20 = (bf16[128,2048]{1,0:T(8,128)(2,1)S(1)}, bf16[128,2048]{1,0:T(8,128)(2,1)S(1)}, u32[]{:S(2)}, u32[]{:S(2)}) collective-permute-start(bf16[128,2048]{1,0:T(8,128)(2,1)S(1)} %pad_maximum_fusion.8.refs_2_), channel_id=1, source_target_pairs={{0,2},{2,0},{1,3},{3,1},{4,6},{6,4},{5,7},{7,5},{8,10},{10,8},{9,1... | collective-permute-start | bytes 1572872 | tf_op jit(solution)/shard_map/ppermute | solution.py:597
  175.3 14.0 %collective-permute-start.27 = (bf16[128,2048]{1,0:T(8,128)(2,1)S(1)}, bf16[128,2048]{1,0:T(8,128)(2,1)S(1)}, u32[]{:S(2)}, u32[]{:S(2)}) collective-permute-start(bf16[128,2048]{1,0:T(8,128)(2,1)S(1)} %slice.325), channel_id=1, source_target_pairs={{0,8},{8,0},{1,9},{9,1},{2,10},{10,2},{3,11},{11,3},{4,12},{12,4},... | collective-permute-start | bytes 1572872 | tf_op jit(solution)/shard_map/ppermute | solution.py:597
  176.6 13.8 %collective-permute-start.28 = (bf16[2,64,2048]{2,1,0:T(8,128)(2,1)S(1)}, bf16[2,64,2048]{2,1,0:T(8,128)(2,1)S(1)}, u32[]{:S(2)}, u32[]{:S(2)}) collective-permute-start(bf16[2,64,2048]{2,1,0:T(8,128)(2,1)S(1)} %slice_bitcast_fusion.1), channel_id=1, source_target_pairs={{0,2},{2,0},{1,3},{3,1},{4,6},{6,4},{5,7},{7,5},{8,10},{10,8},{9,1... | collective-permute-start | bytes 1572872 | tf_op jit(solution)/shard_map/ppermute | solution.py:597
  209.2 22.6 %all-to-all-start.2 = ((bf16[4,32,2048]{2,1,0:T(8,128)(2,1)}), bf16[4,32,2048]{2,1,0:T(8,128)(2,1)S(1)}, u32[]{:S(2)}, u32[]{:S(2)}) async-start(bf16[4,32,2048]{2,1,0:T(8,128)(2,1)} %bitcast.136), calls=%async_computation.2 | async-start | bytes 1048576 | tf_op jit(solution)/shard_map/all_to_all | solution.py:605
  214.8 15.9 %collective-permute-start.33 = (bf16[128,2048]{1,0:T(8,128)(2,1)S(1)}, bf16[128,2048]{1,0:T(8,128)(2,1)S(1)}, u32[]{:S(2)}, u32[]{:S(2)}) collective-permute-start(bf16[128,2048]{1,0:T(8,128)(2,1)S(1)} %pad_maximum_fusion.9.refs_0_), channel_id=1, source_target_pairs={{0,8},{8,0},{1,9},{9,1},{2,10},{10,2},{3,11},{11,3},{4,12},{12,4},... | collective-permute-start | bytes 1572872 | tf_op jit(solution)/shard_map/ppermute | solution.py:597
  215.7 14.9 %collective-permute-start.34 = (bf16[128,2048]{1,0:T(8,128)(2,1)}, bf16[128,2048]{1,0:T(8,128)(2,1)S(1)}, u32[]{:S(2)}, u32[]{:S(2)}) collective-permute-start(bf16[128,2048]{1,0:T(8,128)(2,1)} %pad_maximum_fusion.10.refs_2_), channel_id=1, source_target_pairs={{0,2},{2,0},{1,3},{3,1},{4,6},{6,4},{5,7},{7,5},{8,10},{10,8},{9,1... | collective-permute-start | bytes 1572872 | tf_op jit(solution)/shard_map/ppermute | solution.py:597
  216.8 16.7 %collective-permute-start.35 = (bf16[128,2048]{1,0:T(8,128)(2,1)S(1)}, bf16[128,2048]{1,0:T(8,128)(2,1)S(1)}, u32[]{:S(2)}, u32[]{:S(2)}) collective-permute-start(bf16[128,2048]{1,0:T(8,128)(2,1)S(1)} %pad_maximum_fusion.9.refs_0_), channel_id=1, source_target_pairs={{0,1},{1,0},{2,3},{3,2},{4,5},{5,4},{6,7},{7,6},{8,9},{9,8},{10,11... | collective-permute-start | bytes 1572872 | tf_op jit(solution)/shard_map/ppermute | solution.py:597
  216.8 16.7 %collective-permute-start.38 = (bf16[128,2048]{1,0:T(8,128)(2,1)}, bf16[128,2048]{1,0:T(8,128)(2,1)}, u32[]{:S(2)}, u32[]{:S(2)}) collective-permute-start(bf16[128,2048]{1,0:T(8,128)(2,1)} %pad_maximum_fusion.10.refs_2_), channel_id=1, source_target_pairs={{0,1},{1,0},{2,3},{3,2},{4,5},{5,4},{6,7},{7,6},{8,9},{9,8},{10,11... | collective-permute-start | bytes 1572872 | tf_op jit(solution)/shard_map/ppermute | solution.py:597
  271.4 47.7 %collective-permute-start.44 = (bf16[1024,1024]{1,0:T(8,128)(2,1)S(1)}, bf16[1024,1024]{1,0:T(8,128)(2,1)S(1)}, u32[]{:S(2)}, u32[]{:S(2)}) collective-permute-start(bf16[1024,1024]{1,0:T(8,128)(2,1)S(1)} %copy-done.28), channel_id=1, source_target_pairs={{0,4},{4,0},{1,5},{5,1},{2,6},{6,2},{3,7},{7,3},{8,12},{12,8},{9,1... | collective-permute-start | bytes 6291464 | tf_op jit(solution)/shard_map/ppermute | solution.py:597
  277.9 14.0 %collective-permute-start.41 = (bf16[128,2048]{1,0:T(8,128)(2,1)S(1)}, bf16[128,2048]{1,0:T(8,128)(2,1)S(1)}, u32[]{:S(2)}, u32[]{:S(2)}) collective-permute-start(bf16[128,2048]{1,0:T(8,128)(2,1)S(1)} %pad_maximum_fusion.11), channel_id=1, source_target_pairs={{0,2},{2,0},{1,3},{3,1},{4,6},{6,4},{5,7},{7,5},{8,10},{10,8},{9,1... | collective-permute-start | bytes 1572872 | tf_op jit(solution)/shard_map/ppermute | solution.py:597
  278.9 14.9 %collective-permute-start.42 = (bf16[128,2048]{1,0:T(8,128)(2,1)S(1)}, bf16[128,2048]{1,0:T(8,128)(2,1)S(1)}, u32[]{:S(2)}, u32[]{:S(2)}) collective-permute-start(bf16[128,2048]{1,0:T(8,128)(2,1)S(1)} %pad_maximum_fusion.12), channel_id=1, source_target_pairs={{0,8},{8,0},{1,9},{9,1},{2,10},{10,2},{3,11},{11,3},{4,12},{12,4},... | collective-permute-start | bytes 1572872 | tf_op jit(solution)/shard_map/ppermute | solution.py:597
  280.3 24.2 %collective-permute-start.43 = (bf16[128,2048]{1,0:T(8,128)(2,1)}, bf16[128,2048]{1,0:T(8,128)(2,1)S(1)}, u32[]{:S(2)}, u32[]{:S(2)}) collective-permute-start(bf16[128,2048]{1,0:T(8,128)(2,1)} %pad_maximum_fusion.13), channel_id=1, source_target_pairs={{0,10},{10,0},{2,8},{8,2},{1,11},{11,1},{3,9},{9,3},{4,14},{14,4},... | collective-permute-start | bytes 1572872 | tf_op jit(solution)/shard_map/ppermute | solution.py:638
  326.3 14.0 %collective-permute-start.45 = (bf16[128,2048]{1,0:T(8,128)(2,1)S(1)}, bf16[128,2048]{1,0:T(8,128)(2,1)S(1)}, u32[]{:S(2)}, u32[]{:S(2)}) collective-permute-start(bf16[128,2048]{1,0:T(8,128)(2,1)S(1)} %subtract_convert_fusion.1.refs_0_), channel_id=1, source_target_pairs={{0,2},{2,0},{1,3},{3,1},{4,6},{6,4},{5,7},{7,5},{8,10},{10,8},{9,1... | collective-permute-start | bytes 1572872 | tf_op jit(solution)/shard_map/ppermute | solution.py:597
  327.2 14.9 %collective-permute-start.46 = (bf16[128,2048]{1,0:T(8,128)(2,1)S(1)}, bf16[128,2048]{1,0:T(8,128)(2,1)S(1)}, u32[]{:S(2)}, u32[]{:S(2)}) collective-permute-start(bf16[128,2048]{1,0:T(8,128)(2,1)S(1)} %subtract_convert_fusion.1.refs_0_), channel_id=1, source_target_pairs={{0,8},{8,0},{1,9},{9,1},{2,10},{10,2},{3,11},{11,3},{4,12},{12,4},... | collective-permute-start | bytes 1572872 | tf_op jit(solution)/shard_map/ppermute | solution.py:597
  327.7 24.2 %collective-permute-start.47 = (bf16[128,2048]{1,0:T(8,128)(2,1)S(1)}, bf16[128,2048]{1,0:T(8,128)(2,1)S(1)}, u32[]{:S(2)}, u32[]{:S(2)}) collective-permute-start(bf16[128,2048]{1,0:T(8,128)(2,1)S(1)} %subtract_convert_fusion.1.refs_0_), channel_id=1, source_target_pairs={{0,10},{10,0},{2,8},{8,2},{1,11},{11,1},{3,9},{9,3},{4,14},{14,4},... | collective-permute-start | bytes 1572872 | tf_op jit(solution)/shard_map/ppermute | solution.py:638
  329.8 22.1 %collective-permute-start.48 = (bf16[128,2048]{1,0:T(8,128)(2,1)S(1)}, bf16[128,2048]{1,0:T(8,128)(2,1)S(1)}, u32[]{:S(2)}, u32[]{:S(2)}) collective-permute-start(bf16[128,2048]{1,0:T(8,128)(2,1)S(1)} %subtract_convert_fusion.1.refs_0_), channel_id=1, source_target_pairs={{0,1},{1,0},{2,3},{3,2},{4,5},{5,4},{6,7},{7,6},{8,9},{9,8},{10,11... | collective-permute-start | bytes 1572872 | tf_op jit(solution)/shard_map/ppermute | solution.py:597
  329.8 72.1 %collective-permute-start.55 = (bf16[1024,1024]{1,0:T(8,128)(2,1)}, bf16[1024,1024]{1,0:T(8,128)(2,1)}, u32[]{:S(2)}, u32[]{:S(2)}) collective-permute-start(bf16[1024,1024]{1,0:T(8,128)(2,1)} %grads.16), channel_id=1, source_target_pairs={{0,4},{4,0},{1,5},{5,1},{2,6},{6,2},{3,7},{7,3},{8,12},{12,8},{9,1... | collective-permute-start | bytes 6291464 | tf_op jit(solution)/shard_map/ppermute | solution.py:597
  351.9 9.5 %collective-permute-start.49 = (bf16[128,2048]{1,0:T(8,128)(2,1)S(1)}, bf16[128,2048]{1,0:T(8,128)(2,1)S(1)}, u32[]{:S(2)}, u32[]{:S(2)}) collective-permute-start(bf16[128,2048]{1,0:T(8,128)(2,1)S(1)} %collective-permute-done.45.refs_1_), channel_id=1, source_target_pairs={{0,1},{1,0},{2,3},{3,2},{4,5},{5,4},{6,7},{7,6},{8,9},{9,8},{10,11... | collective-permute-start | bytes 1572872 | tf_op jit(solution)/shard_map/ppermute | solution.py:597
  352.0 9.5 %collective-permute-start.50 = (bf16[128,2048]{1,0:T(8,128)(2,1)S(1)}, bf16[128,2048]{1,0:T(8,128)(2,1)S(1)}, u32[]{:S(2)}, u32[]{:S(2)}) collective-permute-start(bf16[128,2048]{1,0:T(8,128)(2,1)S(1)} %collective-permute-done.46.refs_2_), channel_id=1, source_target_pairs={{0,1},{1,0},{2,3},{3,2},{4,5},{5,4},{6,7},{7,6},{8,9},{9,8},{10,11... | collective-permute-start | bytes 1572872 | tf_op jit(solution)/shard_map/ppermute | solution.py:597
  352.6 49.4 %collective-permute-start.56 = (bf16[512,1024]{1,0:T(8,128)(2,1)S(1)}, bf16[512,1024]{1,0:T(8,128)(2,1)S(1)}, u32[]{:S(2)}, u32[]{:S(2)}) collective-permute-start(bf16[512,1024]{1,0:T(8,128)(2,1)S(1)} %copy-done.32), channel_id=1, source_target_pairs={{0,16},{16,0},{1,17},{17,1},{2,18},{18,2},{3,19},{19,3},{4,20},{20... | collective-permute-start | bytes 3145736 | tf_op jit(solution)/shard_map/ppermute | solution.py:597
  389.1 12.7 %collective-permute-start.54 = (f32[2,2,2,2,2,64]{5,4,3,2,1,0:T(2,128)S(1)}, f32[2,2,2,2,2,64]{5,4,3,2,1,0:T(2,128)S(1)}, u32[]{:S(2)}, u32[]{:S(2)}) collective-permute-start(f32[2,2,2,2,2,64]{5,4,3,2,1,0:T(2,128)S(1)} %add.221), channel_id=1, source_target_pairs={{0,8},{8,0},{1,9},{9,1},{2,10},{10,2},{3,11},{11,3},{4,12},{12,4},... | collective-permute-start | bytes 24584 | tf_op jit(solution)/shard_map/ppermute | solution.py:597
  421.4 60.7 %collective-permute-start.62 = (bf16[1024,1024]{1,0:T(8,128)(2,1)}, bf16[1024,1024]{1,0:T(8,128)(2,1)}, u32[]{:S(2)}, u32[]{:S(2)}) collective-permute-start(bf16[1024,1024]{1,0:T(8,128)(2,1)} %grads.18), channel_id=1, source_target_pairs={{0,4},{4,0},{1,5},{5,1},{2,6},{6,2},{3,7},{7,3},{8,12},{12,8},{9,1... | collective-permute-start | bytes 6291464 | tf_op jit(solution)/shard_map/ppermute | solution.py:597
  425.2 57.0 %collective-permute-start.63 = (bf16[512,1024]{1,0:T(8,128)(2,1)}, bf16[512,1024]{1,0:T(8,128)(2,1)}, u32[]{:S(2)}, u32[]{:S(2)}) collective-permute-start(bf16[512,1024]{1,0:T(8,128)(2,1)} %grads.19), channel_id=1, source_target_pairs={{0,16},{16,0},{1,17},{17,1},{2,18},{18,2},{3,19},{19,3},{4,20},{20... | collective-permute-start | bytes 3145736 | tf_op jit(solution)/shard_map/ppermute | solution.py:597
  428.0 13.8 %collective-permute-start.59 = (bf16[128,2048]{1,0:T(8,128)(2,1)}, bf16[128,2048]{1,0:T(8,128)(2,1)}, u32[]{:S(2)}, u32[]{:S(2)}) collective-permute-start(bf16[128,2048]{1,0:T(8,128)(2,1)} %pad_maximum_fusion.14), channel_id=1, source_target_pairs={{0,2},{2,0},{1,3},{3,1},{4,6},{6,4},{5,7},{7,5},{8,10},{10,8},{9,1... | collective-permute-start | bytes 1572872 | tf_op jit(solution)/shard_map/ppermute | solution.py:597
  430.1 30.5 %collective-permute-start.60 = (bf16[128,2048]{1,0:T(8,128)(2,1)}, bf16[128,2048]{1,0:T(8,128)(2,1)}, u32[]{:S(2)}, u32[]{:S(2)}) collective-permute-start(bf16[128,2048]{1,0:T(8,128)(2,1)} %pad_maximum_fusion.15), channel_id=1, source_target_pairs={{0,8},{8,0},{1,9},{9,1},{2,10},{10,2},{3,11},{11,3},{4,12},{12,4},... | collective-permute-start | bytes 1572872 | tf_op jit(solution)/shard_map/ppermute | solution.py:597
  433.4 46.1 %collective-permute-start.61 = (bf16[128,2048]{1,0:T(8,128)(2,1)}, bf16[128,2048]{1,0:T(8,128)(2,1)}, u32[]{:S(2)}, u32[]{:S(2)}) collective-permute-start(bf16[128,2048]{1,0:T(8,128)(2,1)} %pad_maximum_fusion.16), channel_id=1, source_target_pairs={{0,10},{10,0},{2,8},{8,2},{1,11},{11,1},{3,9},{9,3},{4,14},{14,4},... | collective-permute-start | bytes 1572872 | tf_op jit(solution)/shard_map/ppermute | solution.py:638
  441.9 51.9 %collective-permute-start.77 = (bf16[256,1024]{1,0:T(8,128)(2,1)S(1)}, bf16[256,1024]{1,0:T(8,128)(2,1)S(1)}, u32[]{:S(2)}, u32[]{:S(2)}) collective-permute-start(bf16[256,1024]{1,0:T(8,128)(2,1)S(1)} %copy-done.61), channel_id=1, source_target_pairs={{0,8},{8,0},{1,9},{9,1},{2,10},{10,2},{3,11},{11,3},{4,12},{12,4},... | collective-permute-start | bytes 1572872 | tf_op jit(solution)/shard_map/ppermute | solution.py:597
  492.2 50.8 %collective-permute-start.68 = (bf16[512,1024]{1,0:T(8,128)(2,1)S(1)}, bf16[512,1024]{1,0:T(8,128)(2,1)}, u32[]{:S(2)}, u32[]{:S(2)}) collective-permute-start(bf16[512,1024]{1,0:T(8,128)(2,1)S(1)} %copy-done.33), channel_id=1, source_target_pairs={{0,16},{16,0},{1,17},{17,1},{2,18},{18,2},{3,19},{19,3},{4,20},{20... | collective-permute-start | bytes 3145736 | tf_op jit(solution)/shard_map/ppermute | solution.py:597
  493.7 13.3 %collective-permute-start.64 = (f32[4,2048]{1,0:T(4,128)S(1)}, f32[4,2048]{1,0:T(4,128)S(1)}, u32[]{:S(2)}, u32[]{:S(2)}) collective-permute-start(f32[4,2048]{1,0:T(4,128)S(1)} %pad_maximum_fusion.17), channel_id=1, source_target_pairs={{0,1},{1,0},{2,3},{3,2},{4,5},{5,4},{6,7},{7,6},{8,9},{9,8},{10,11... | collective-permute-start | bytes 98312 | tf_op jit(solution)/shard_map/ppermute | solution.py:597
  494.9 82.6 %all-to-all-start.3 = ((bf16[4,32,2048]{2,1,0:T(8,128)(2,1)}), bf16[4,32,2048]{2,1,0:T(8,128)(2,1)}, u32[]{:S(2)}, u32[]{:S(2)}) async-start(bf16[4,32,2048]{2,1,0:T(8,128)(2,1)} %bitcast.42), calls=%async_computation.3 | async-start | bytes 1048576 | tf_op jit(solution)/shard_map/all_to_all | solution.py:605
  499.5 81.0 %collective-permute-start.70 = (bf16[1024,768]{1,0:T(8,128)(2,1)}, bf16[1024,768]{1,0:T(8,128)(2,1)}, u32[]{:S(2)}, u32[]{:S(2)}) collective-permute-start(bf16[1024,768]{1,0:T(8,128)(2,1)} %grads.21), channel_id=1, source_target_pairs={{0,4},{4,0},{1,5},{5,1},{2,6},{6,2},{3,7},{7,3},{8,12},{12,8},{9,1... | collective-permute-start | bytes 4718600 | tf_op jit(solution)/shard_map/ppermute | solution.py:597
  506.9 46.1 %collective-permute-start.67 = (bf16[1024,256]{1,0:T(8,128)(2,1)S(1)}, bf16[1024,256]{1,0:T(8,128)(2,1)S(1)}, u32[]{:S(2)}, u32[]{:S(2)}) collective-permute-start(bf16[1024,256]{1,0:T(8,128)(2,1)S(1)} %copy-done.63), channel_id=1, source_target_pairs={{0,4},{4,0},{1,5},{5,1},{2,6},{6,2},{3,7},{7,3},{8,12},{12,8},{9,1... | collective-permute-start | bytes 1572872 | tf_op jit(solution)/shard_map/ppermute | solution.py:597
  510.5 51.2 %collective-permute-start.75 = (bf16[256,1024]{1,0:T(8,128)(2,1)}, bf16[256,1024]{1,0:T(8,128)(2,1)}, u32[]{:S(2)}, u32[]{:S(2)}) collective-permute-start(bf16[256,1024]{1,0:T(8,128)(2,1)} %get-tuple-element.347), channel_id=1, source_target_pairs={{0,8},{8,0},{1,9},{9,1},{2,10},{10,2},{3,11},{11,3},{4,12},{12,4},... | collective-permute-start | bytes 1572872 | tf_op jit(solution)/shard_map/ppermute | solution.py:597
  512.4 49.3 %collective-permute-start.66 = (f32[4,2048]{1,0:T(4,128)S(1)}, f32[4,2048]{1,0:T(4,128)S(1)}, u32[]{:S(2)}, u32[]{:S(2)}) collective-permute-start(f32[4,2048]{1,0:T(4,128)S(1)} %add.233), channel_id=1, source_target_pairs={{0,8},{8,0},{1,9},{9,1},{2,10},{10,2},{3,11},{11,3},{4,12},{12,4},... | collective-permute-start | bytes 98312 | tf_op jit(solution)/shard_map/ppermute | solution.py:597
  557.3 14.6 %collective-permute-start.73 = (bf16[512,256]{1,0:T(8,128)(2,1)}, bf16[512,256]{1,0:T(8,128)(2,1)S(1)}, u32[]{:S(2)}, u32[]{:S(2)}) collective-permute-start(bf16[512,256]{1,0:T(8,128)(2,1)} %grads.28), channel_id=1, source_target_pairs={{0,16},{16,0},{1,17},{17,1},{2,18},{18,2},{3,19},{19,3},{4,20},{20... | collective-permute-start | bytes 786440 | tf_op jit(solution)/shard_map/ppermute | solution.py:597
  562.9 17.5 %collective-permute-start.69 = (f32[4,2048]{1,0:T(4,128)S(1)}, f32[4,2048]{1,0:T(4,128)S(1)}, u32[]{:S(2)}, u32[]{:S(2)}) collective-permute-start(f32[4,2048]{1,0:T(4,128)S(1)} %add.234), channel_id=1, source_target_pairs={{0,4},{4,0},{1,5},{5,1},{2,6},{6,2},{3,7},{7,3},{8,12},{12,8},{9,1... | collective-permute-start | bytes 98312 | tf_op jit(solution)/shard_map/ppermute | solution.py:597
  563.8 25.6 %collective-permute-start.76 = (bf16[256,1024]{1,0:T(8,128)(2,1)}, bf16[256,1024]{1,0:T(8,128)(2,1)}, u32[]{:S(2)}, u32[]{:S(2)}) collective-permute-start(bf16[256,1024]{1,0:T(8,128)(2,1)} %get-tuple-element.345), channel_id=1, source_target_pairs={{0,8},{8,0},{1,9},{9,1},{2,10},{10,2},{3,11},{11,3},{4,12},{12,4},... | collective-permute-start | bytes 1572872 | tf_op jit(solution)/shard_map/ppermute | solution.py:597
  577.1 11.2 %collective-permute-start.74 = (bf16[256,256]{1,0:T(8,128)(2,1)S(1)}, bf16[256,256]{1,0:T(8,128)(2,1)S(1)}, u32[]{:S(2)}, u32[]{:S(2)}) collective-permute-start(bf16[256,256]{1,0:T(8,128)(2,1)S(1)} %get-tuple-element.382), channel_id=1, source_target_pairs={{0,8},{8,0},{1,9},{9,1},{2,10},{10,2},{3,11},{11,3},{4,12},{12,4},... | collective-permute-start | bytes 393224 | tf_op jit(solution)/shard_map/ppermute | solution.py:597
  584.9 37.6 %collective-permute-start.71 = (bf16[512,768]{1,0:T(8,128)(2,1)}, bf16[512,768]{1,0:T(8,128)(2,1)}, u32[]{:S(2)}, u32[]{:S(2)}) collective-permute-start(bf16[512,768]{1,0:T(8,128)(2,1)} %grads.26), channel_id=1, source_target_pairs={{0,16},{16,0},{1,17},{17,1},{2,18},{18,2},{3,19},{19,3},{4,20},{20... | collective-permute-start | bytes 2359304 | tf_op jit(solution)/shard_map/ppermute | solution.py:597
  628.4 11.8 %collective-permute-start.72 = (bf16[256,768]{1,0:T(8,128)(2,1)S(1)}, bf16[256,768]{1,0:T(8,128)(2,1)S(1)}, u32[]{:S(2)}, u32[]{:S(2)}) collective-permute-start(bf16[256,768]{1,0:T(8,128)(2,1)S(1)} %get-tuple-element.366), channel_id=1, source_target_pairs={{0,8},{8,0},{1,9},{9,1},{2,10},{10,2},{3,11},{11,3},{4,12},{12,4},... | collective-permute-start | bytes 1179656 | tf_op jit(solution)/shard_map/ppermute | solution.py:597
  628.4 9.5 %collective-permute-start.78 = (f32[4,2048]{1,0:T(4,128)S(1)}, f32[4,2048]{1,0:T(4,128)S(1)}, u32[]{:S(2)}, u32[]{:S(2)}) collective-permute-start(f32[4,2048]{1,0:T(4,128)S(1)} %add.235), channel_id=1, source_target_pairs={{0,16},{16,0},{1,17},{17,1},{2,18},{18,2},{3,19},{19,3},{4,20},{20... | collective-permute-start | bytes 98312 | tf_op jit(solution)/shard_map/ppermute | solution.py:597
  (108 other events, 779.6 us)

commit v3 on v2

--- a/solution.py
+++ b/solution.py
@@ -686,26 +686,33 @@
         ]
         return parts[1], *jnp.split(parts[0], 2)
 
-    def group_sum(v):
-        v = v.reshape(-1, 2, 2, 2, 2, half_count)
-        v = v + swap(v, "c")[:, ::-1]
-        v = v + swap(v, "y")[:, :, :, :, ::-1]
-        v = v + swap(v, "zl")[:, :, :, ::-1]
-        return v.reshape(-1, all_count)
-
+    def group_sum(v, extra=None):
+        for name, axis in (("c", 1), ("y", 4), ("zl", 3)):
+            if extra is None:
+                other = swap(v, name)
+            else:
+                other = swap(jnp.concatenate([v, extra]), name)
+                other, other_extra = other[: v.shape[0]], other[v.shape[0] :]
+                extra = extra + other_extra
+            other = jnp.flip(other.reshape(-1, 2, 2, 2, 2, half_count), axis)
+            v = v + other.reshape(-1, all_count)
+        return v if extra is None else (v, extra)
+
+    ids_all = (2 * zl + jnp.array([0, 0, 1, 1, 4, 4, 5, 5], jnp.int32)) ^ jnp.array(
+        [0, 2] * 4, jnp.int32
+    )
     ids_x, ids_zh, ids_zl = (
         s ^ jnp.array(bits, jnp.int32) for bits in ((1, 3, 5, 7), (4, 6), (0, 2))
     )
 
-    def grads_x(features, right):
-        return grads(features, right, ids_x)
-
-    def grads_zh(features, right, far):
-        return grads(features, right, ids_zh, (far, 2))
+    def whole_sum(v):
+        return lax.psum_scatter(v, ("zh", "x"), scatter_dimension=0, tiled=True)
+
+    def cross_zl(kept):
+        return kept[:block], swap(kept[block:], "zl")
 
     def finish(features, right, far, sent):
-        kept = grads(features, right, ids_zl, (far, 0), (sent, 0))
-        return kept[:block], swap(kept[block:], "zl")
+        return cross_zl(grads(features, right, ids_zl, (far, 0), (sent, 0)))
 
     def joined(mine, other, transposed=False):
         mine, other = mine.astype(f32), other.astype(f32)
@@ -801,9 +808,9 @@
     layer_out = from_sequence(late_hidden + down_value * feed_inv * feed_gain)
     down_whole, layer_out = both(down_whole, layer_out)
 
-    down_far = grads_x(down_whole, act_low)
-    down_whole, down_far = both(down_whole, down_far)
-    down_far = swap(down_far, "x")
+    down_part = grads(down_whole, act_low, ids_all)
+    down_whole, down_part = both(down_whole, down_part)
+    down_sum = whole_sum(down_part)
     tile = gate_value.shape[1] // 2
     unit_tile = pl.BlockSpec((all_count, tile), lambda j, z: (0, j))
     rows_full = pl.BlockSpec((all_count, width), lambda j, z: (0, 0))
@@ -839,20 +846,16 @@
         zl[None], down_whole, gate_weight, up_weight, down_weight, gate_value,
         up_value,
     )
-    gate_far = grads_x(hidden_whole, gate_low)
+    gate_part = grads(hidden_whole, gate_low, ids_all)
     hidden_grad = grad_top + scatter_direct(*hidden_part)
-    hidden_grad, gate_far = both(hidden_grad, gate_far)
-    gate_far = swap(gate_far, "x")
-    hidden_grad, down_far = both(hidden_grad, down_far)
-    down_sent = grads_zh(down_whole, act_low, down_far)
-    hidden_grad, down_sent = both(hidden_grad, down_sent)
-    down_sent = swap(down_sent, "zh")
+    hidden_grad, gate_part = both(hidden_grad, gate_part)
+    gate_sum = whole_sum(gate_part)
 
     branch_low = norm_back(branch, attn_inv, attention_gain, hidden_grad).astype(bf16)
     branch_whole, late_up = gather_direct(branch_low, up_low)
-    up_far = grads_x(hidden_whole, late_up)
-    branch_whole, up_far = both(branch_whole, up_far)
-    up_far = swap(up_far, "x")
+    up_part = grads(hidden_whole, late_up, ids_all)
+    branch_whole, up_part = both(branch_whole, up_part)
+    up_sum = whole_sum(up_part)
     mixed_grad = pl.pallas_call(
         mixed_back_kernel,
         grid_spec=pltpu.PrefetchScalarGridSpec(
@@ -886,13 +889,28 @@
     )
     query_inv, key_inv = inverse[:, 0:1], inverse[:, 1:2]
     dots = jnp.stack([jnp.sum(yq * gq * queries, axis=-1), jnp.sum(yk * gk * keys_proj, axis=-1)])
-    late_yq, gate_far, down_sent = both(yq, gate_far, down_sent)
-    down_pair = finish(down_whole, act_low, down_far, down_sent)
-    gate_sent = grads_zh(hidden_whole, gate_low, gate_far)
-    dots, gate_sent, down_keep = both(group_sum(dots), gate_sent, down_pair[0])
-    down_pair = (down_keep, down_pair[1])
+    head_gains = jnp.stack(
+        [jnp.sum(yq * queries * query_inv, axis=0), jnp.sum(yk * keys_proj * key_inv, axis=0)]
+    )
+    head_gains = lax.dynamic_update_slice(
+        jnp.zeros((2, width), f32), head_gains, (0, (2 * t + zl) * heads_width)
+    )
+    row_gains = jnp.stack(
+        [
+            jnp.sum(hidden_grad * branch * attn_inv, axis=0),
+            jnp.sum(grad_top * down_value * feed_inv, axis=0),
+        ]
+    )
+    gains = jnp.concatenate([head_gains, row_gains]).reshape(-1, all_count)
+    yq, late_mixed = both(yq, mixed_low)
+    out_far = grads(branch_whole, late_mixed, ids_x)
+    dots, gains = group_sum(dots, gains)
+    dots, out_far, down_sum = both(dots, out_far, down_sum)
+    out_far = swap(out_far, "x")
+    down_mine, down_other = cross_zl(down_sum)
     dots = dots.T
-    gate_sent = swap(gate_sent, "zh")
+    gains = gains.reshape(4, width)
+    gains = gains + swap(gains, "x")
     query_grad_low = (
         query_inv * gq * yq - queries * query_inv**3 * (dots[:, 0:1] / width)
     ).astype(bf16)
@@ -901,52 +919,31 @@
     ).astype(bf16)
     projected_grad = jnp.concatenate([query_grad_low, key_grad_low, value_grad_low], axis=1)
     input_part = times(projected_grad, wqkv, "rh,dh->rd")
-    input_own, late_grad = both(input_part[0], projected_grad)
-    in_far = grads_x(whole, late_grad)
-    input_sum, in_far = both(scatter_direct(input_own, *input_part[1:]), in_far)
-    in_far = swap(in_far, "x")
-    input_rows = hidden_grad + input_sum
-    input_rows, up_far, late_mixed, gate_sent = both(input_rows, up_far, mixed_low, gate_sent)
-    up_sent = grads_zh(hidden_whole, up_low, up_far)
-    out_far = grads_x(branch_whole, late_mixed)
-    input_rows, up_sent, out_far, late_yq = both(input_rows, up_sent, out_far, late_yq)
-    up_sent, out_far = swap(up_sent, "zh"), swap(out_far, "x")
-    input_grad = from_sequence(input_rows)
-    gate_pair = finish(hidden_whole, gate_low, gate_far, gate_sent)
-    in_far, gate_keep = both(in_far, gate_pair[0])
-    gate_pair = (gate_keep, gate_pair[1])
-    in_sent = swap(grads_zh(whole, projected_grad, in_far), "zh")
-    up_pair = finish(hidden_whole, up_low, up_far, up_sent)
-    out_far, up_keep = both(out_far, up_pair[0])
-    up_pair = (up_keep, up_pair[1])
-    out_sent = swap(grads_zh(branch_whole, mixed_low, out_far), "zh")
+    input_own, late_grad, out_far, gains, down_other = both(
+        input_part[0], projected_grad, out_far, gains, down_other
+    )
+    in_far = swap(grads(whole, late_grad, ids_x), "x")
+    gains = gains + swap(gains, "zh")
+    out_sent = grads(branch_whole, late_mixed, ids_zh, (out_far, 2))
+    down_term = joined(down_mine, down_other, True)
+    input_sum = scatter_direct(input_own, *input_part[1:])
+    input_sum, in_far, out_sent, gate_sum, down_term = both(
+        input_sum, in_far, out_sent, gate_sum, down_term
+    )
+    in_sent = grads(whole, projected_grad, ids_zh, (in_far, 2))
+    input_sum, in_sent, out_sent, gate_sum = both(input_sum, in_sent, out_sent, gate_sum)
+    in_sent, out_sent = swap(in_sent, "zh"), swap(out_sent, "zh")
+    gate_mine, gate_other = cross_zl(gate_sum)
+    gate_term = joined(gate_mine, gate_other)
+    in_sent, gate_term, input_sum = both(in_sent, gate_term, input_sum)
     in_mine, in_other = finish(whole, projected_grad, in_far, in_sent)
-    out_pair = finish(branch_whole, mixed_low, out_far, out_sent)
-    head_gains = jnp.stack(
-        [jnp.sum(late_yq * queries * query_inv, axis=0), jnp.sum(yk * keys_proj * key_inv, axis=0)]
-    )
-    head_gains = lax.dynamic_update_slice(
-        jnp.zeros((2, width), f32), head_gains, (0, (2 * t + zl) * heads_width)
-    )
-    row_gains = jnp.stack(
-        [
-            jnp.sum(hidden_grad * branch * attn_inv, axis=0),
-            jnp.sum(grad_top * down_value * feed_inv, axis=0),
-        ]
-    )
-    gains = jnp.concatenate([head_gains, row_gains])
-    for name in ("c", "y", "zl"):
-        gains = gains + swap(gains, name)
-    gains, up_keep = both(gains, up_pair[0])
-    up_pair = (up_keep, up_pair[1])
-    gains = gains + swap(gains, "x")
-    gains, in_mine = both(gains, in_mine)
-    gains = gains + swap(gains, "zh")
+    out_sent, in_mine = both(out_sent, in_mine)
+    out_mine, out_other = finish(branch_whole, mixed_low, out_far, out_sent)
+    out_term = joined(out_mine, out_other, True)
+    up_pair = cross_zl(up_sum)
+    input_grad = from_sequence(hidden_grad + input_sum)
     gains = lax.dynamic_slice_in_dim(gains, s * block, block, 1)
-    down_term = joined(*down_pair, True)
-    gate_term = joined(*gate_pair)
     up_term = joined(*up_pair)
-    out_term = joined(*out_pair, True)
     query_term, key_term, value_term = (
         joined(
             in_mine[:, k * heads_width : (k + 1) * heads_width],

time: 652 us -> 615 us (0.943)
  starting transfers between devices: 92.7 us -> 74.1 us
  Pallas kernels: 149 us -> 131 us
  between operations: 2.22 us -> 15.4 us
  waiting for transfers between devices: 276 us -> 266 us
  local copies, waits for them, and re-layouts: 40.9 us -> 33.4 us
  other arithmetic: 47.4 us -> 54.5 us
    ppermute x76 -> x67, waiting for transfers between devices: 225 us -> 173 us  [swap(): return lax.ppermute(v, name, ((0, 1), (1, 0)))]
    reduce_scatter x0 -> x3, waiting for transfers between devices: none -> 40 us  [whole_sum(): return lax.psum_scatter(v, ('zh', 'x'), scatter_dimension=0, tiled=True)]
    ppermute x76 -> x67, starting transfers between devices: 66.8 us -> 47.8 us  [swap(): return lax.ppermute(v, name, ((0, 1), (1, 0)))]
    pallas_call x15 -> x9, Pallas kernels: 79 us -> 60.3 us  [grads(): pl.pallas_call(lambda *refs: grads_kernel(len(terms), *refs), grid_spec=p...]
    unnamed x153 -> x127, local copies, waits for them, and re-layouts: 20.3 us -> 17 us
  transfers between devices with their start and end apart: 83 -> 77, of which waited for: 51 -> 47; matrix products, arithmetic and copies ran while one was open for 9% -> 12% of each run, Pallas kernels for 12% -> 16%
where the time goes in v3:
time: 615 us; the launch traced here: 610 us
  waiting for transfers between devices  266 us (43%)
  Pallas kernels  131 us (21%)
  starting transfers between devices  74.1 us (12%)
  other arithmetic  54.5 us (9%)
  matrix products  35.9 us (6%)
  local copies, waits for them, and re-layouts  33.4 us (5%)
  between operations  15.4 us (3%)
    ppermute x67, waiting for transfers between devices, swap(): return lax.ppermute(v, name, ((0, 1), (1, 0)))  173 us
    pallas_call x9, Pallas kernels, grads(): pl.pallas_call(lambda *refs: grads_kernel(len(terms), *refs), grid_spec=p...  60.3 us
    ppermute x67, starting transfers between devices, swap(): return lax.ppermute(v, name, ((0, 1), (1, 0)))  47.8 us
    ppermute x3, waiting for transfers between devices, swap_zy(): return lax.ppermute(v, ('zl', 'y'), ((0, 3), (3, 0), (1, 2), (2, 1)))  40.9 us
    reduce_scatter x3, waiting for transfers between devices, whole_sum(): return lax.psum_scatter(v, ('zh', 'x'), scatter_dimension=0, tiled=True)  40 us
    pallas_call x1, Pallas kernels, grouped(): pl.pallas_call(feed_back_kernel, grid_spec=pltpu.PrefetchScalarGridSpec(n...  25.7 us
    pallas_call x4, Pallas kernels, assemble(): pl.pallas_call(lambda *refs: assemble_kernel(moves, *refs), in_specs=[pl....  17.3 us
    unnamed x127, local copies, waits for them, and re-layouts  17 us
  transfers between devices with their start and end apart: 77, of which 47 were waited for; matrix products, arithmetic and copies ran while one was open for 12% of the time, Pallas kernels for 16%

profile of v3, /device:TPU:0, one launch (start us, length us, event | category | flops | bytes accessed | tf_op | source)
XLA Modules:
  0.0 610.0 jit_solution(10540239655828007347)
XLA Ops:
  9.5 6.2 %all-to-all-start = ((bf16[4,32,2048]{2,1,0:T(8,128)(2,1)}), bf16[4,32,2048]{2,1,0:T(8,128)(2,1)S(1)}, u32[]{:S(2)}, u32[]{:S(2)}) async-start(bf16[4,32,2048]{2,1,0:T(8,128)(2,1)} %bitcast.125), calls=%async_computation | async-start | bytes 1048576 | tf_op jit(solution)/shard_map/all_to_all | solution.py:600
  18.6 11.6 %all-to-all-done = bf16[4,32,2048]{2,1,0:T(8,128)(2,1)S(1)} async-done(((bf16[4,32,2048]{2,1,0:T(8,128)(2,1)}), bf16[4,32,2048]{2,1,0:T(8,128)(2,1)S(1)}, u32[]{:S(2)}, u32[]{:S(2)}) %all-to-all-start) | async-done | bytes 524320 | tf_op jit(solution)/shard_map/all_to_all | solution.py:600
  32.0 5.5 collective-permute-done
  41.6 3.0 multiply_cosine_fusion
  45.7 5.1 all-to-all-start.1
  59.2 4.3 assemble.4.refs_1_
  63.7 6.1 fusion.42
  84.1 12.8 %attend.1 = (bf16[2,2,256,256]{3,2,1,0:T(8,128)(2,1)}, f32[2,2,256,256]{3,2,1,0:T(8,128)}, f32[2,2,256,2]{3,2,1,0:T(8,128)}, bf16[2,2,256,256]{3,2,1,0:T(8,128)(...) custom-call(f32[2,2,256,768]{3,2,1,0:T(8,128)} %bitcast.126, f32[2,2,256,2]{3,2,1,0:T(8,128)} %bitcast.144, ...), custom_call_target="tpu_custom_call" | custom-call | tf_op jit(solution)/shard_map/attend/pallas_call | solution.py:782
  106.0 12.3 %collective-permute-done.13 = bf16[128,2048]{1,0:T(8,128)(2,1)S(1)} collective-permute-done((bf16[128,2048]{1,0:T(8,128)(2,1)S(1)}, bf16[128,2048]{1,0:T(8,128)(2,1)S(1)}, u32[]{:S(2)}, u32[]{:S(2)}) %collective-permute-start.13) | collective-permute-done | bytes 524320 | tf_op jit(solution)/shard_map/ppermute | solution.py:597
  122.0 4.1 collective-permute-done.15
  131.2 4.2 collective-permute-done.17
  139.7 7.7 %collective-permute-done.19.refs_1_ = bf16[128,2048]{1,0:T(8,128)(2,1)S(1)} collective-permute-done((bf16[128,2048]{1,0:T(8,128)(2,1)S(1)}, bf16[128,2048]{1,0:T(8,128)(2,1)S(1)}, u32[]{:S(2)}, u32[]{:S(2)}) %collective-permute-start.19) | collective-permute-done | bytes 524320 | tf_op jit(solution)/shard_map/ppermute | solution.py:597
  152.2 4.4 assemble.5.refs_1_
  156.6 7.9 %fusion.2.gate_ref = f32[1024,1024]{1,0:T(8,128)S(1)} fusion(bf16[1024,2048]{1,0:T(8,128)(2,1)} %assemble.5.refs_1_, bf16[2048,2048]{1,0:T(8,128)(2,1)} %wg_ref, s32[]{:T(128)S(6)} %select_n.119), kind=kOutput, calls=%fused_computation.3 | convolution fusion | flops 4294967296 | bytes 12582916 | tf_op jit(solution)/shard_map/rd,df->rf/dot_general | solution.py:800
  164.6 10.4 %multiply_convert_fusion = (bf16[1024,1024]{1,0:T(8,128)(2,1)S(1)}, f32[1024,1024]{1,0:T(8,128)}) fusion(f32[1024,1024]{1,0:T(8,128)S(1)} %fusion.2.gate_ref, bf16[1024,2048]{1,0:T(8,128)(2,1)S(1)} %copy-done.2, bf16[2048,2048]{1,0:T(8,128)(2,1)} %wu_ref, s32[]{:T(128)S(6)} %select_n.119), kind=kOutput, calls=%fused_computation | convolution fusion | flops 4301258752 | bytes 18874372 | tf_op jit(solution)/shard_map/rd,df->rf/dot_general | solution.py:801
  185.0 11.5 %collective-permute-done.27 = bf16[128,2048]{1,0:T(8,128)(2,1)S(1)} collective-permute-done((bf16[128,2048]{1,0:T(8,128)(2,1)S(1)}, bf16[128,2048]{1,0:T(8,128)(2,1)S(1)}, u32[]{:S(2)}, u32[]{:S(2)}) %collective-permute-start.27) | collective-permute-done | bytes 524320 | tf_op jit(solution)/shard_map/ppermute | solution.py:597
  200.5 4.4 collective-permute-done.29
  208.9 4.7 collective-permute-done.31
  215.5 5.5 all-to-all-start.2
  223.5 13.3 %collective-permute-done.33.refs_1_ = bf16[128,2048]{1,0:T(8,128)(2,1)S(1)} collective-permute-done((bf16[128,2048]{1,0:T(8,128)(2,1)S(1)}, bf16[128,2048]{1,0:T(8,128)(2,1)S(1)}, u32[]{:S(2)}, u32[]{:S(2)}) %collective-permute-start.33) | collective-permute-done | bytes 524320 | tf_op jit(solution)/shard_map/ppermute | solution.py:597
  239.8 4.3 assemble.6.refs_1_.rows_ref
  244.1 10.9 %grads.9 = bf16[2048,1024]{1,0:T(8,128)(2,1)} custom-call(s32[8]{0:T(128)} %add_xor_fusion.refs_0_, bf16[1024,2048]{1,0:T(8,128)(2,1)} %assemble.6.refs_1_.rows_ref, bf16[1024,1024]{1,0:T(8,128)(2,1)} %copy-done.21), custom_call_target="tpu_custom_call" | custom-call | tf_op jit(solution)/shard_map/grads/pallas_call | solution.py:514
  255.0 25.7 %feed_back.1 = (bf16[1024,1024]{1,0:T(8,128)(2,1)}, bf16[1024,1024]{1,0:T(8,128)(2,1)}, bf16[512,2048]{1,0:T(8,128)(2,1)}, bf16[256,2048]{1,0:T(8,128)(2,1)}, bf16[256,2048]{1,0:T(8,128)(2,1)}) custom-call(s32[1]{0:T(128)} %bitcast.31.zl_ref, bf16[1024,2048]{1,0:T(8,128)(2,1)} %assemble.6.refs_1_.rows_ref, bf16[2048,2048]{1,0:T(8,128)(2,1)} %wg_ref, ...), custom_call_target="tpu_custom_call" | custom-call | tf_op jit(solution)/shard_map/feed_back/pallas_call | solution.py:820
  294.4 11.0 %grads.10 = bf16[2048,1024]{1,0:T(8,128)(2,1)} custom-call(s32[8]{0:T(128)} %add_xor_fusion.refs_0_, bf16[1024,2048]{1,0:T(8,128)(2,1)} %assemble.5.refs_1_, bf16[1024,1024]{1,0:T(8,128)(2,1)} %get-tuple-element.184.refs_2_), custom_call_target="tpu_custom_call" | custom-call | tf_op jit(solution)/shard_map/grads/pallas_call | solution.py:514
  305.4 12.9 %collective-permute-done.42 = bf16[128,2048]{1,0:T(8,128)(2,1)S(1)} collective-permute-done((bf16[128,2048]{1,0:T(8,128)(2,1)}, bf16[128,2048]{1,0:T(8,128)(2,1)S(1)}, u32[]{:S(2)}, u32[]{:S(2)}) %collective-permute-start.42) | collective-permute-done | bytes 524320 | tf_op jit(solution)/shard_map/ppermute | solution.py:597
  318.2 12.1 %collective-permute-done.43 = bf16[128,2048]{1,0:T(8,128)(2,1)} collective-permute-done((bf16[128,2048]{1,0:T(8,128)(2,1)}, bf16[128,2048]{1,0:T(8,128)(2,1)}, u32[]{:S(2)}, u32[]{:S(2)}) %collective-permute-start.43) | collective-permute-done | bytes 524320 | tf_op jit(solution)/shard_map/ppermute | solution.py:638
  336.4 9.3 %collective-permute-done.44.refs_1_ = bf16[128,2048]{1,0:T(8,128)(2,1)S(1)} collective-permute-done((bf16[128,2048]{1,0:T(8,128)(2,1)S(1)}, bf16[128,2048]{1,0:T(8,128)(2,1)S(1)}, u32[]{:S(2)}, u32[]{:S(2)}) %collective-permute-start.44) | collective-permute-done | bytes 524320 | tf_op jit(solution)/shard_map/ppermute | solution.py:597
  345.7 6.4 %collective-permute-done.45.refs_2_ = bf16[128,2048]{1,0:T(8,128)(2,1)S(1)} collective-permute-done((bf16[128,2048]{1,0:T(8,128)(2,1)S(1)}, bf16[128,2048]{1,0:T(8,128)(2,1)S(1)}, u32[]{:S(2)}, u32[]{:S(2)}) %collective-permute-start.45) | collective-permute-done | bytes 524320 | tf_op jit(solution)/shard_map/ppermute | solution.py:597
  352.1 15.8 %collective-permute-done.46.refs_3_ = bf16[128,2048]{1,0:T(8,128)(2,1)S(1)} collective-permute-done((bf16[128,2048]{1,0:T(8,128)(2,1)S(1)}, bf16[128,2048]{1,0:T(8,128)(2,1)S(1)}, u32[]{:S(2)}, u32[]{:S(2)}) %collective-permute-start.46) | collective-permute-done | bytes 524320 | tf_op jit(solution)/shard_map/ppermute | solution.py:638
  369.2 11.1 %grads.11 = bf16[2048,1024]{1,0:T(8,128)(2,1)} custom-call(s32[8]{0:T(128)} %add_xor_fusion.refs_0_, bf16[1024,2048]{1,0:T(8,128)(2,1)} %assemble.5.refs_1_, bf16[1024,1024]{1,0:T(8,128)(2,1)} %get-tuple-element.200.refs_2_), custom_call_target="tpu_custom_call" | custom-call | tf_op jit(solution)/shard_map/grads/pallas_call | solution.py:514
  380.4 4.3 assemble.7.rows_ref.refs_1_
  384.7 4.2 mixed_back.1
  389.0 10.1 %attend_back.1 = (f32[2,2,256,256]{3,2,1,0:T(8,128)}, f32[2,2,256,256]{3,2,1,0:T(8,128)}, bf16[2,2,256,256]{3,2,1,0:T(8,128)(2,1)}) custom-call(bf16[2,2,256,256]{3,2,1,0:T(8,128)(2,1)} %get-tuple-element.186.refs_0_, bf16[2,2,256,256]{3,2,1,0:T(8,128)(2,1)} %get-tuple-element.187.refs_1_, bf16[2,2,256,256]{3,2,1,0:T(8,128)(2,1)} %get-tuple-element.188.refs_2_, ...), custom_call_target="tpu_custom_call" | custom-call | tf_op jit(solution)/shard_map/attend_back/pallas_call | solution.py:876
  408.3 5.1 grads.12
  429.4 3.0 copy.110
  432.5 3.0 convolution_convert_fusion.3
  437.7 3.9 collective-permute-done.56
  441.6 6.1 %grads.13 = bf16[1024,768]{1,0:T(8,128)(2,1)} custom-call(s32[4]{0:T(128)} %broadcast_xor_fusion.1.refs_0_, bf16[1024,2048]{1,0:T(8,128)(2,1)} %assemble.4.refs_1_, bf16[1024,768]{1,0:T(8,128)(2,1)} %copy-done.5), custom_call_target="tpu_custom_call" | custom-call | tf_op jit(solution)/shard_map/grads/pallas_call | solution.py:514
  450.3 3.3 grads.14
  461.6 6.8 %collective-permute-done.59 = bf16[128,2048]{1,0:T(8,128)(2,1)S(1)} collective-permute-done((bf16[128,2048]{1,0:T(8,128)(2,1)S(1)}, bf16[128,2048]{1,0:T(8,128)(2,1)S(1)}, u32[]{:S(2)}, u32[]{:S(2)}) %collective-permute-start.59) | collective-permute-done | bytes 524320 | tf_op jit(solution)/shard_map/ppermute | solution.py:597
  468.4 21.4 %collective-permute-done.60 = bf16[128,2048]{1,0:T(8,128)(2,1)S(1)} collective-permute-done((bf16[128,2048]{1,0:T(8,128)(2,1)S(1)}, bf16[128,2048]{1,0:T(8,128)(2,1)S(1)}, u32[]{:S(2)}, u32[]{:S(2)}) %collective-permute-start.60) | collective-permute-done | bytes 524320 | tf_op jit(solution)/shard_map/ppermute | solution.py:597
  489.8 13.1 %collective-permute-done.61 = bf16[128,2048]{1,0:T(8,128)(2,1)S(1)} collective-permute-done((bf16[128,2048]{1,0:T(8,128)(2,1)S(1)}, bf16[128,2048]{1,0:T(8,128)(2,1)S(1)}, u32[]{:S(2)}, u32[]{:S(2)}) %collective-permute-start.61) | collective-permute-done | bytes 524320 | tf_op jit(solution)/shard_map/ppermute | solution.py:638
  504.1 4.6 grads.15
  515.3 40.0 %reduce-scatter.8.cloned.1.call-done = bf16[512,1024]{1,0:T(8,128)(2,1)} async-done(((bf16[2048,1024]{1,0:T(8,128)(2,1)}), bf16[512,1024]{1,0:T(8,128)(2,1)}) %reduce-scatter.8.cloned.1.call-update) | async-done | bytes 1048592 | tf_op jit(solution)/shard_map/reduce_scatter | solution.py:709
  561.3 3.5 all-to-all-start.3
  564.8 4.7 grads.16
  573.3 3.4 grads.17
  578.0 16.0 %collective-permute-done.67 = bf16[256,256]{1,0:T(8,128)(2,1)S(1)} collective-permute-done((bf16[256,256]{1,0:T(8,128)(2,1)S(1)}, bf16[256,256]{1,0:T(8,128)(2,1)S(1)}, u32[]{:S(2)}, u32[]{:S(2)}) %collective-permute-start.67) | collective-permute-done | bytes 131104 | tf_op jit(solution)/shard_map/ppermute | solution.py:597
  (428 shorter events, 173.6 us)
Async XLA Ops:
  9.5 20.7 %all-to-all-start = ((bf16[4,32,2048]{2,1,0:T(8,128)(2,1)}), bf16[4,32,2048]{2,1,0:T(8,128)(2,1)S(1)}, u32[]{:S(2)}, u32[]{:S(2)}) async-start(bf16[4,32,2048]{2,1,0:T(8,128)(2,1)} %bitcast.125), calls=%async_computation | async-start | bytes 1048576 | tf_op jit(solution)/shard_map/all_to_all | solution.py:600
  30.2 7.2 %collective-permute-start = (bf16[64,2048]{1,0:T(8,128)(2,1)S(1)}, bf16[64,2048]{1,0:T(8,128)(2,1)S(1)}, u32[]{:S(2)}, u32[]{:S(2)}) collective-permute-start(bf16[64,2048]{1,0:T(8,128)(2,1)S(1)} %bitcast.149), channel_id=1, source_target_pairs={{0,2},{2,0},{1,3},{3,1},{4,6},{6,4},{5,7},{7,5},{8,10},{10,8},{9,1... | collective-permute-start | bytes 786440 | tf_op jit(solution)/shard_map/ppermute | solution.py:597
  40.8 12.8 %collective-permute-start.2 = (bf16[128,2048]{1,0:T(8,128)(2,1)}, bf16[128,2048]{1,0:T(8,128)(2,1)}, u32[]{:S(2)}, u32[]{:S(2)}) collective-permute-start(bf16[128,2048]{1,0:T(8,128)(2,1)} %get-tuple-element.127.refs_0_), channel_id=1, source_target_pairs={{0,8},{8,0},{1,9},{9,1},{2,10},{10,2},{3,11},{11,3},{4,12},{12,4},... | collective-permute-start | bytes 1572872 | tf_op jit(solution)/shard_map/ppermute | solution.py:597
  41.1 12.5 %collective-permute-start.3 = (bf16[128,2048]{1,0:T(8,128)(2,1)}, bf16[128,2048]{1,0:T(8,128)(2,1)}, u32[]{:S(2)}, u32[]{:S(2)}) collective-permute-start(bf16[128,2048]{1,0:T(8,128)(2,1)} %get-tuple-element.128.refs_2_), channel_id=1, source_target_pairs={{0,2},{2,0},{1,3},{3,1},{4,6},{6,4},{5,7},{7,5},{8,10},{10,8},{9,1... | collective-permute-start | bytes 1572872 | tf_op jit(solution)/shard_map/ppermute | solution.py:597
  45.7 18.0 %all-to-all-start.1 = ((bf16[4,32,2048]{2,1,0:T(8,128)(2,1)}), bf16[4,32,2048]{2,1,0:T(8,128)(2,1)S(1)}, u32[]{:S(2)}, u32[]{:S(2)}) async-start(bf16[4,32,2048]{2,1,0:T(8,128)(2,1)} %bitcast.141), calls=%async_computation.1 | async-start | bytes 1048576 | tf_op jit(solution)/shard_map/all_to_all | solution.py:600
  104.3 14.0 %collective-permute-start.13 = (bf16[128,2048]{1,0:T(8,128)(2,1)S(1)}, bf16[128,2048]{1,0:T(8,128)(2,1)S(1)}, u32[]{:S(2)}, u32[]{:S(2)}) collective-permute-start(bf16[128,2048]{1,0:T(8,128)(2,1)S(1)} %slice.337), channel_id=1, source_target_pairs={{0,8},{8,0},{1,9},{9,1},{2,10},{10,2},{3,11},{11,3},{4,12},{12,4},... | collective-permute-start | bytes 1572872 | tf_op jit(solution)/shard_map/ppermute | solution.py:597
  104.4 14.0 %collective-permute-start.14 = (bf16[2,64,2048]{2,1,0:T(8,128)(2,1)S(1)}, bf16[2,64,2048]{2,1,0:T(8,128)(2,1)S(1)}, u32[]{:S(2)}, u32[]{:S(2)}) collective-permute-start(bf16[2,64,2048]{2,1,0:T(8,128)(2,1)S(1)} %slice_bitcast_fusion.3), channel_id=1, source_target_pairs={{0,2},{2,0},{1,3},{3,1},{4,6},{6,4},{5,7},{7,5},{8,10},{10,8},{9,1... | collective-permute-start | bytes 1572872 | tf_op jit(solution)/shard_map/ppermute | solution.py:597
  118.6 7.6 %collective-permute-start.15 = (bf16[64,2048]{1,0:T(8,128)(2,1)S(1)}, bf16[64,2048]{1,0:T(8,128)(2,1)S(1)}, u32[]{:S(2)}, u32[]{:S(2)}) collective-permute-start(bf16[64,2048]{1,0:T(8,128)(2,1)S(1)} %slice.340), channel_id=1, source_target_pairs={{0,2},{2,0},{1,3},{3,1},{4,6},{6,4},{5,7},{7,5},{8,10},{10,8},{9,1... | collective-permute-start | bytes 786440 | tf_op jit(solution)/shard_map/ppermute | solution.py:597
  136.5 10.9 %collective-permute-start.19 = (bf16[128,2048]{1,0:T(8,128)(2,1)S(1)}, bf16[128,2048]{1,0:T(8,128)(2,1)S(1)}, u32[]{:S(2)}, u32[]{:S(2)}) collective-permute-start(bf16[128,2048]{1,0:T(8,128)(2,1)S(1)} %pad_maximum_fusion.7.refs_0_), channel_id=1, source_target_pairs={{0,8},{8,0},{1,9},{9,1},{2,10},{10,2},{3,11},{11,3},{4,12},{12,4},... | collective-permute-start | bytes 1572872 | tf_op jit(solution)/shard_map/ppermute | solution.py:597
  138.5 9.3 %collective-permute-start.20 = (bf16[128,2048]{1,0:T(8,128)(2,1)S(1)}, bf16[128,2048]{1,0:T(8,128)(2,1)}, u32[]{:S(2)}, u32[]{:S(2)}) collective-permute-start(bf16[128,2048]{1,0:T(8,128)(2,1)S(1)} %pad_maximum_fusion.8.refs_2_), channel_id=1, source_target_pairs={{0,2},{2,0},{1,3},{3,1},{4,6},{6,4},{5,7},{7,5},{8,10},{10,8},{9,1... | collective-permute-start | bytes 1572872 | tf_op jit(solution)/shard_map/ppermute | solution.py:597
  182.5 14.0 %collective-permute-start.27 = (bf16[128,2048]{1,0:T(8,128)(2,1)S(1)}, bf16[128,2048]{1,0:T(8,128)(2,1)S(1)}, u32[]{:S(2)}, u32[]{:S(2)}) collective-permute-start(bf16[128,2048]{1,0:T(8,128)(2,1)S(1)} %slice.349), channel_id=1, source_target_pairs={{0,8},{8,0},{1,9},{9,1},{2,10},{10,2},{3,11},{11,3},{4,12},{12,4},... | collective-permute-start | bytes 1572872 | tf_op jit(solution)/shard_map/ppermute | solution.py:597
  183.7 13.8 %collective-permute-start.28 = (bf16[2,64,2048]{2,1,0:T(8,128)(2,1)S(1)}, bf16[2,64,2048]{2,1,0:T(8,128)(2,1)S(1)}, u32[]{:S(2)}, u32[]{:S(2)}) collective-permute-start(bf16[2,64,2048]{2,1,0:T(8,128)(2,1)S(1)} %slice_bitcast_fusion.1), channel_id=1, source_target_pairs={{0,2},{2,0},{1,3},{3,1},{4,6},{6,4},{5,7},{7,5},{8,10},{10,8},{9,1... | collective-permute-start | bytes 1572872 | tf_op jit(solution)/shard_map/ppermute | solution.py:597
  197.6 7.3 %collective-permute-start.29 = (bf16[64,2048]{1,0:T(8,128)(2,1)S(1)}, bf16[64,2048]{1,0:T(8,128)(2,1)S(1)}, u32[]{:S(2)}, u32[]{:S(2)}) collective-permute-start(bf16[64,2048]{1,0:T(8,128)(2,1)S(1)} %slice.352), channel_id=1, source_target_pairs={{0,2},{2,0},{1,3},{3,1},{4,6},{6,4},{5,7},{7,5},{8,10},{10,8},{9,1... | collective-permute-start | bytes 786440 | tf_op jit(solution)/shard_map/ppermute | solution.py:597
  215.5 22.3 %all-to-all-start.2 = ((bf16[4,32,2048]{2,1,0:T(8,128)(2,1)}), bf16[4,32,2048]{2,1,0:T(8,128)(2,1)S(1)}, u32[]{:S(2)}, u32[]{:S(2)}) async-start(bf16[4,32,2048]{2,1,0:T(8,128)(2,1)} %bitcast.142), calls=%async_computation.2 | async-start | bytes 1048576 | tf_op jit(solution)/shard_map/all_to_all | solution.py:605
  221.0 192.7 %reduce-scatter.4.cloned.1.call-start = ((), (), s32[]{:S(2)}) async-start(), calls=%async_computation.7 | async-start | bytes 5242880 | tf_op jit(solution)/shard_map/reduce_scatter | solution.py:709
  221.0 15.8 %collective-permute-start.33 = (bf16[128,2048]{1,0:T(8,128)(2,1)S(1)}, bf16[128,2048]{1,0:T(8,128)(2,1)S(1)}, u32[]{:S(2)}, u32[]{:S(2)}) collective-permute-start(bf16[128,2048]{1,0:T(8,128)(2,1)S(1)} %pad_maximum_fusion.9.refs_0_), channel_id=1, source_target_pairs={{0,8},{8,0},{1,9},{9,1},{2,10},{10,2},{3,11},{11,3},{4,12},{12,4},... | collective-permute-start | bytes 1572872 | tf_op jit(solution)/shard_map/ppermute | solution.py:597
  221.7 15.0 %collective-permute-start.34 = (bf16[128,2048]{1,0:T(8,128)(2,1)S(1)}, bf16[128,2048]{1,0:T(8,128)(2,1)}, u32[]{:S(2)}, u32[]{:S(2)}) collective-permute-start(bf16[128,2048]{1,0:T(8,128)(2,1)S(1)} %pad_maximum_fusion.10.refs_2_), channel_id=1, source_target_pairs={{0,2},{2,0},{1,3},{3,1},{4,6},{6,4},{5,7},{7,5},{8,10},{10,8},{9,1... | collective-permute-start | bytes 1572872 | tf_op jit(solution)/shard_map/ppermute | solution.py:597
  223.0 16.8 %collective-permute-start.35 = (bf16[128,2048]{1,0:T(8,128)(2,1)S(1)}, bf16[128,2048]{1,0:T(8,128)(2,1)}, u32[]{:S(2)}, u32[]{:S(2)}) collective-permute-start(bf16[128,2048]{1,0:T(8,128)(2,1)S(1)} %pad_maximum_fusion.9.refs_0_), channel_id=1, source_target_pairs={{0,1},{1,0},{2,3},{3,2},{4,5},{5,4},{6,7},{7,6},{8,9},{9,8},{10,11... | collective-permute-start | bytes 1572872 | tf_op jit(solution)/shard_map/ppermute | solution.py:597
  223.0 16.8 %collective-permute-start.38 = (bf16[128,2048]{1,0:T(8,128)(2,1)S(1)}, bf16[128,2048]{1,0:T(8,128)(2,1)}, u32[]{:S(2)}, u32[]{:S(2)}) collective-permute-start(bf16[128,2048]{1,0:T(8,128)(2,1)S(1)} %pad_maximum_fusion.10.refs_2_), channel_id=1, source_target_pairs={{0,1},{1,0},{2,3},{3,2},{4,5},{5,4},{6,7},{7,6},{8,9},{9,8},{10,11... | collective-permute-start | bytes 1572872 | tf_op jit(solution)/shard_map/ppermute | solution.py:597
  255.0 249.2 %reduce-scatter.6.cloned.1.call-start = ((), (), s32[]{:S(2)}) async-start(), calls=%async_computation.8 | async-start | bytes 5242880 | tf_op jit(solution)/shard_map/reduce_scatter | solution.py:709
  289.2 16.2 %collective-permute-start.41 = (bf16[128,2048]{1,0:T(8,128)(2,1)}, bf16[128,2048]{1,0:T(8,128)(2,1)S(1)}, u32[]{:S(2)}, u32[]{:S(2)}) collective-permute-start(bf16[128,2048]{1,0:T(8,128)(2,1)} %pad_maximum_fusion.11), channel_id=1, source_target_pairs={{0,2},{2,0},{1,3},{3,1},{4,6},{6,4},{5,7},{7,5},{8,10},{10,8},{9,1... | collective-permute-start | bytes 1572872 | tf_op jit(solution)/shard_map/ppermute | solution.py:597
  290.7 27.5 %collective-permute-start.42 = (bf16[128,2048]{1,0:T(8,128)(2,1)}, bf16[128,2048]{1,0:T(8,128)(2,1)S(1)}, u32[]{:S(2)}, u32[]{:S(2)}) collective-permute-start(bf16[128,2048]{1,0:T(8,128)(2,1)} %pad_maximum_fusion.12), channel_id=1, source_target_pairs={{0,8},{8,0},{1,9},{9,1},{2,10},{10,2},{3,11},{11,3},{4,12},{12,4},... | collective-permute-start | bytes 1572872 | tf_op jit(solution)/shard_map/ppermute | solution.py:597
  292.1 38.2 %collective-permute-start.43 = (bf16[128,2048]{1,0:T(8,128)(2,1)}, bf16[128,2048]{1,0:T(8,128)(2,1)}, u32[]{:S(2)}, u32[]{:S(2)}) collective-permute-start(bf16[128,2048]{1,0:T(8,128)(2,1)} %pad_maximum_fusion.13), channel_id=1, source_target_pairs={{0,10},{10,0},{2,8},{8,2},{1,11},{11,1},{3,9},{9,3},{4,14},{14,4},... | collective-permute-start | bytes 1572872 | tf_op jit(solution)/shard_map/ppermute | solution.py:638
  332.2 223.1 %reduce-scatter.8.cloned.1.call-start = ((), (), s32[]{:S(2)}) async-start(), calls=%async_computation.9 | async-start | bytes 5242880 | tf_op jit(solution)/shard_map/reduce_scatter | solution.py:709
  332.8 12.9 %collective-permute-start.44 = (bf16[128,2048]{1,0:T(8,128)(2,1)S(1)}, bf16[128,2048]{1,0:T(8,128)(2,1)S(1)}, u32[]{:S(2)}, u32[]{:S(2)}) collective-permute-start(bf16[128,2048]{1,0:T(8,128)(2,1)S(1)} %subtract_convert_fusion.1.refs_0_), channel_id=1, source_target_pairs={{0,2},{2,0},{1,3},{3,1},{4,6},{6,4},{5,7},{7,5},{8,10},{10,8},{9,1... | collective-permute-start | bytes 1572872 | tf_op jit(solution)/shard_map/ppermute | solution.py:597
  333.5 18.6 %collective-permute-start.45 = (bf16[128,2048]{1,0:T(8,128)(2,1)S(1)}, bf16[128,2048]{1,0:T(8,128)(2,1)S(1)}, u32[]{:S(2)}, u32[]{:S(2)}) collective-permute-start(bf16[128,2048]{1,0:T(8,128)(2,1)S(1)} %subtract_convert_fusion.1.refs_0_), channel_id=1, source_target_pairs={{0,8},{8,0},{1,9},{9,1},{2,10},{10,2},{3,11},{11,3},{4,12},{12,4},... | collective-permute-start | bytes 1572872 | tf_op jit(solution)/shard_map/ppermute | solution.py:597
  333.5 34.3 %collective-permute-start.46 = (bf16[128,2048]{1,0:T(8,128)(2,1)S(1)}, bf16[128,2048]{1,0:T(8,128)(2,1)S(1)}, u32[]{:S(2)}, u32[]{:S(2)}) collective-permute-start(bf16[128,2048]{1,0:T(8,128)(2,1)S(1)} %subtract_convert_fusion.1.refs_0_), channel_id=1, source_target_pairs={{0,10},{10,0},{2,8},{8,2},{1,11},{11,1},{3,9},{9,3},{4,14},{14,4},... | collective-permute-start | bytes 1572872 | tf_op jit(solution)/shard_map/ppermute | solution.py:638
  336.4 31.5 %collective-permute-start.47 = (bf16[128,2048]{1,0:T(8,128)(2,1)S(1)}, bf16[128,2048]{1,0:T(8,128)(2,1)S(1)}, u32[]{:S(2)}, u32[]{:S(2)}) collective-permute-start(bf16[128,2048]{1,0:T(8,128)(2,1)S(1)} %subtract_convert_fusion.1.refs_0_), channel_id=1, source_target_pairs={{0,1},{1,0},{2,3},{3,2},{4,5},{5,4},{6,7},{7,6},{8,9},{9,8},{10,11... | collective-permute-start | bytes 1572872 | tf_op jit(solution)/shard_map/ppermute | solution.py:597
  367.9 12.5 %collective-permute-start.48 = (bf16[128,2048]{1,0:T(8,128)(2,1)S(1)}, bf16[128,2048]{1,0:T(8,128)(2,1)}, u32[]{:S(2)}, u32[]{:S(2)}) collective-permute-start(bf16[128,2048]{1,0:T(8,128)(2,1)S(1)} %collective-permute-done.44.refs_1_), channel_id=1, source_target_pairs={{0,1},{1,0},{2,3},{3,2},{4,5},{5,4},{6,7},{7,6},{8,9},{9,8},{10,11... | collective-permute-start | bytes 1572872 | tf_op jit(solution)/shard_map/ppermute | solution.py:597
  368.7 11.7 %collective-permute-start.49 = (bf16[128,2048]{1,0:T(8,128)(2,1)S(1)}, bf16[128,2048]{1,0:T(8,128)(2,1)}, u32[]{:S(2)}, u32[]{:S(2)}) collective-permute-start(bf16[128,2048]{1,0:T(8,128)(2,1)S(1)} %collective-permute-done.45.refs_2_), channel_id=1, source_target_pairs={{0,1},{1,0},{2,3},{3,2},{4,5},{5,4},{6,7},{7,6},{8,9},{9,8},{10,11... | collective-permute-start | bytes 1572872 | tf_op jit(solution)/shard_map/ppermute | solution.py:597
  368.8 11.6 %collective-permute-start.50 = (bf16[128,2048]{1,0:T(8,128)(2,1)S(1)}, bf16[128,2048]{1,0:T(8,128)(2,1)}, u32[]{:S(2)}, u32[]{:S(2)}) collective-permute-start(bf16[128,2048]{1,0:T(8,128)(2,1)S(1)} %collective-permute-done.46.refs_3_), channel_id=1, source_target_pairs={{0,1},{1,0},{2,3},{3,2},{4,5},{5,4},{6,7},{7,6},{8,9},{9,8},{10,11... | collective-permute-start | bytes 1572872 | tf_op jit(solution)/shard_map/ppermute | solution.py:597
  421.7 31.9 %collective-permute-start.57 = (bf16[256,2048]{1,0:T(8,128)(2,1)}, bf16[256,2048]{1,0:T(8,128)(2,1)}, u32[]{:S(2)}, u32[]{:S(2)}) collective-permute-start(bf16[256,2048]{1,0:T(8,128)(2,1)} %get-tuple-element.323), channel_id=1, source_target_pairs={{0,1},{1,0},{2,3},{3,2},{4,5},{5,4},{6,7},{7,6},{8,9},{9,8},{10,11... | collective-permute-start | bytes 3145736 | tf_op jit(solution)/shard_map/ppermute | solution.py:597
  421.7 31.9 %collective-permute-start.58 = (bf16[256,2048]{1,0:T(8,128)(2,1)}, bf16[256,2048]{1,0:T(8,128)(2,1)}, u32[]{:S(2)}, u32[]{:S(2)}) collective-permute-start(bf16[256,2048]{1,0:T(8,128)(2,1)} %get-tuple-element.322), channel_id=1, source_target_pairs={{0,1},{1,0},{2,3},{3,2},{4,5},{5,4},{6,7},{7,6},{8,9},{9,8},{10,11... | collective-permute-start | bytes 3145736 | tf_op jit(solution)/shard_map/ppermute | solution.py:597
  422.3 10.2 %collective-permute-start.55 = (f32[4,2048]{1,0:T(4,128)S(1)}, f32[4,2048]{1,0:T(4,128)S(1)}, u32[]{:S(2)}, u32[]{:S(2)}) collective-permute-start(f32[4,2048]{1,0:T(4,128)S(1)} %reshape.359), channel_id=1, source_target_pairs={{0,4},{4,0},{1,5},{5,1},{2,6},{6,2},{3,7},{7,3},{8,12},{12,8},{9,1... | collective-permute-start | bytes 98312 | tf_op jit(solution)/shard_map/ppermute | solution.py:597
  424.0 13.8 %collective-permute-start.54 = (bf16[1024,256]{1,0:T(8,128)(2,1)}, bf16[1024,256]{1,0:T(8,128)(2,1)S(1)}, u32[]{:S(2)}, u32[]{:S(2)}) collective-permute-start(bf16[1024,256]{1,0:T(8,128)(2,1)} %grads.12), channel_id=1, source_target_pairs={{0,4},{4,0},{1,5},{5,1},{2,6},{6,2},{3,7},{7,3},{8,12},{12,8},{9,1... | collective-permute-start | bytes 1572872 | tf_op jit(solution)/shard_map/ppermute | solution.py:597
  426.8 14.8 %collective-permute-start.56 = (bf16[256,1024]{1,0:T(8,128)(2,1)}, bf16[256,1024]{1,0:T(8,128)(2,1)}, u32[]{:S(2)}, u32[]{:S(2)}) collective-permute-start(bf16[256,1024]{1,0:T(8,128)(2,1)} %get-tuple-element.339), channel_id=1, source_target_pairs={{0,8},{8,0},{1,9},{9,1},{2,10},{10,2},{3,11},{11,3},{4,12},{12,4},... | collective-permute-start | bytes 1572872 | tf_op jit(solution)/shard_map/ppermute | solution.py:597
  447.7 56.4 %collective-permute-start.62 = (bf16[1024,768]{1,0:T(8,128)(2,1)}, bf16[1024,768]{1,0:T(8,128)(2,1)}, u32[]{:S(2)}, u32[]{:S(2)}) collective-permute-start(bf16[1024,768]{1,0:T(8,128)(2,1)} %grads.13), channel_id=1, source_target_pairs={{0,4},{4,0},{1,5},{5,1},{2,6},{6,2},{3,7},{7,3},{8,12},{12,8},{9,1... | collective-permute-start | bytes 4718600 | tf_op jit(solution)/shard_map/ppermute | solution.py:597
  449.2 61.8 %collective-permute-start.69 = (f32[4,2048]{1,0:T(4,128)S(1)}, f32[4,2048]{1,0:T(4,128)S(1)}, u32[]{:S(2)}, u32[]{:S(2)}) collective-permute-start(f32[4,2048]{1,0:T(4,128)S(1)} %add.242), channel_id=1, source_target_pairs={{0,16},{16,0},{1,17},{17,1},{2,18},{18,2},{3,19},{19,3},{4,20},{20... | collective-permute-start | bytes 98312 | tf_op jit(solution)/shard_map/ppermute | solution.py:597
  456.3 12.1 %collective-permute-start.59 = (bf16[128,2048]{1,0:T(8,128)(2,1)S(1)}, bf16[128,2048]{1,0:T(8,128)(2,1)S(1)}, u32[]{:S(2)}, u32[]{:S(2)}) collective-permute-start(bf16[128,2048]{1,0:T(8,128)(2,1)S(1)} %pad_maximum_fusion.14), channel_id=1, source_target_pairs={{0,2},{2,0},{1,3},{3,1},{4,6},{6,4},{5,7},{7,5},{8,10},{10,8},{9,1... | collective-permute-start | bytes 1572872 | tf_op jit(solution)/shard_map/ppermute | solution.py:597
  457.5 32.3 %collective-permute-start.60 = (bf16[128,2048]{1,0:T(8,128)(2,1)S(1)}, bf16[128,2048]{1,0:T(8,128)(2,1)S(1)}, u32[]{:S(2)}, u32[]{:S(2)}) collective-permute-start(bf16[128,2048]{1,0:T(8,128)(2,1)S(1)} %pad_maximum_fusion.15), channel_id=1, source_target_pairs={{0,8},{8,0},{1,9},{9,1},{2,10},{10,2},{3,11},{11,3},{4,12},{12,4},... | collective-permute-start | bytes 1572872 | tf_op jit(solution)/shard_map/ppermute | solution.py:597
  459.4 43.5 %collective-permute-start.61 = (bf16[128,2048]{1,0:T(8,128)(2,1)S(1)}, bf16[128,2048]{1,0:T(8,128)(2,1)S(1)}, u32[]{:S(2)}, u32[]{:S(2)}) collective-permute-start(bf16[128,2048]{1,0:T(8,128)(2,1)S(1)} %pad_maximum_fusion.16), channel_id=1, source_target_pairs={{0,10},{10,0},{2,8},{8,2},{1,11},{11,1},{3,9},{9,3},{4,14},{14,4},... | collective-permute-start | bytes 1572872 | tf_op jit(solution)/shard_map/ppermute | solution.py:638
  508.7 51.7 %collective-permute-start.63 = (bf16[512,768]{1,0:T(8,128)(2,1)}, bf16[512,768]{1,0:T(8,128)(2,1)}, u32[]{:S(2)}, u32[]{:S(2)}) collective-permute-start(bf16[512,768]{1,0:T(8,128)(2,1)} %grads.15), channel_id=1, source_target_pairs={{0,16},{16,0},{1,17},{17,1},{2,18},{18,2},{3,19},{19,3},{4,20},{20... | collective-permute-start | bytes 2359304 | tf_op jit(solution)/shard_map/ppermute | solution.py:597
  510.0 47.5 %collective-permute-start.64 = (bf16[256,1024]{1,0:T(8,128)(2,1)}, bf16[256,1024]{1,0:T(8,128)(2,1)}, u32[]{:S(2)}, u32[]{:S(2)}) collective-permute-start(bf16[256,1024]{1,0:T(8,128)(2,1)} %get-tuple-element.337), channel_id=1, source_target_pairs={{0,8},{8,0},{1,9},{9,1},{2,10},{10,2},{3,11},{11,3},{4,12},{12,4},... | collective-permute-start | bytes 1572872 | tf_op jit(solution)/shard_map/ppermute | solution.py:597
  511.6 61.7 %collective-permute-start.65 = (bf16[512,256]{1,0:T(8,128)(2,1)S(1)}, bf16[512,256]{1,0:T(8,128)(2,1)}, u32[]{:S(2)}, u32[]{:S(2)}) collective-permute-start(bf16[512,256]{1,0:T(8,128)(2,1)S(1)} %copy-done.50), channel_id=1, source_target_pairs={{0,16},{16,0},{1,17},{17,1},{2,18},{18,2},{3,19},{19,3},{4,20},{20... | collective-permute-start | bytes 786440 | tf_op jit(solution)/shard_map/ppermute | solution.py:597
  557.5 37.5 %collective-permute-start.68 = (bf16[256,1024]{1,0:T(8,128)(2,1)}, bf16[256,1024]{1,0:T(8,128)(2,1)}, u32[]{:S(2)}, u32[]{:S(2)}) collective-permute-start(bf16[256,1024]{1,0:T(8,128)(2,1)} %get-tuple-element.335), channel_id=1, source_target_pairs={{0,8},{8,0},{1,9},{9,1},{2,10},{10,2},{3,11},{11,3},{4,12},{12,4},... | collective-permute-start | bytes 1572872 | tf_op jit(solution)/shard_map/ppermute | solution.py:597
  561.3 40.2 %all-to-all-start.3 = ((bf16[4,32,2048]{2,1,0:T(8,128)(2,1)}), bf16[4,32,2048]{2,1,0:T(8,128)(2,1)S(1)}, u32[]{:S(2)}, u32[]{:S(2)}) async-start(bf16[4,32,2048]{2,1,0:T(8,128)(2,1)} %bitcast.140), calls=%async_computation.5 | async-start | bytes 1048576 | tf_op jit(solution)/shard_map/all_to_all | solution.py:605
  571.4 26.5 %collective-permute-start.66 = (bf16[256,768]{1,0:T(8,128)(2,1)}, bf16[256,768]{1,0:T(8,128)(2,1)}, u32[]{:S(2)}, u32[]{:S(2)}) collective-permute-start(bf16[256,768]{1,0:T(8,128)(2,1)} %get-tuple-element.357), channel_id=1, source_target_pairs={{0,8},{8,0},{1,9},{9,1},{2,10},{10,2},{3,11},{11,3},{4,12},{12,4},... | collective-permute-start | bytes 1179656 | tf_op jit(solution)/shard_map/ppermute | solution.py:597
  577.7 16.2 %collective-permute-start.67 = (bf16[256,256]{1,0:T(8,128)(2,1)S(1)}, bf16[256,256]{1,0:T(8,128)(2,1)S(1)}, u32[]{:S(2)}, u32[]{:S(2)}) collective-permute-start(bf16[256,256]{1,0:T(8,128)(2,1)S(1)} %get-tuple-element.373), channel_id=1, source_target_pairs={{0,8},{8,0},{1,9},{9,1},{2,10},{10,2},{3,11},{11,3},{4,12},{12,4},... | collective-permute-start | bytes 393224 | tf_op jit(solution)/shard_map/ppermute | solution.py:597
  (90 other events, 901.4 us)
Sparse Core Ops, SparseCore 0:
  255.1 87.2 reduce-scatter.3
  345.6 86.1 reduce-scatter.5
  434.8 120.4 reduce-scatter.7

commit v4 on v3

--- a/solution.py
+++ b/solution.py
@@ -474,7 +474,7 @@
     for part in (1, 0):
         at = slice(part * half, (part + 1) * half)
         act_grad = dot_last(rows_ref[at, :], wd_ref[...])
-        gate, up = gate_ref[at, :], up_ref[at, :]
+        gate, up = gate_ref[at, :].astype(f32), up_ref[at, :].astype(f32)
         sig = jax.nn.sigmoid(gate)
         up_low = (act_grad * gate * sig).astype(bf16)
         gate_low = (act_grad * up * sig * (1.0 + gate * (1.0 - sig))).astype(bf16)
@@ -605,6 +605,16 @@
         v = lax.all_to_all(v, ("zh", "x"), 0, 0, tiled=True)
         return jnp.transpose(v, (1, 0, 2)).astype(f32)
 
+    def swap_zhx(v):
+        return lax.ppermute(v, ("zh", "x"), ((0, 3), (3, 0), (1, 2), (2, 1)))
+
+    def from_sequence_direct(v):
+        v = v.astype(bf16).reshape(4, row_count, width)
+        p = [lax.dynamic_index_in_dim(v, sequence ^ k, 0, keepdims=False) for k in range(4)]
+        p = jnp.stack([p[0], swap(p[1], "x"), swap(p[2], "zh"), swap_zhx(p[3])])
+        p = [lax.dynamic_index_in_dim(p, sequence ^ k, 0, keepdims=False) for k in range(4)]
+        return jnp.stack(p, axis=1).astype(f32)
+
     def gather(a, late=None):
         a0, b0 = a[:half_count], a[half_count:]
         a1, b2 = both(swap(a0, "y"), swap(b0, "zl"))
@@ -653,8 +663,8 @@
         )
         return v, late
 
-    def scatter_direct(own, *other):
-        other = both(*(swap(v, "c") for v in other))
+    def scatter_direct(own, *other, late=None):
+        *other, late = both(*(swap(v, "c") for v in other), 0.0 if late is None else late)
         p = [
             (v.astype(f32) + w.astype(f32)).astype(bf16)
             for v, w in zip(own.reshape(2, 4 * half_count, width), other)
@@ -664,7 +674,8 @@
             jnp.concatenate([v[chip * k : (chip + 1) * k] for v in p]) for chip in range(4)
         )
         sent = both(swap(sent[0], "y"), swap(sent[1], "zl"), swap_zy(sent[2]))
-        return sum(v.astype(f32) for v in (mine, *sent))
+        v = sum(v.astype(f32) for v in (mine, *sent))
+        return v, late
 
     def scatter(own, *other):
         a, b = own.reshape(2, 4 * half_count, width)
@@ -798,15 +809,15 @@
     hidden = rows_in.astype(f32) + branch * attn_inv * attention_gain
     hidden_whole = gather(hidden.astype(bf16))
     gate_value = jnp.einsum("rd,df->rf", hidden_whole, wg, preferred_element_type=f32)
+    gate_value = gate_value.astype(bf16)
     up_value = jnp.einsum("rd,df->rf", hidden_whole, wu, preferred_element_type=f32)
-    sigmoid_value = jax.nn.sigmoid(gate_value)
-    act_low = (gate_value * sigmoid_value * up_value).astype(bf16)
+    gate_wide = gate_value.astype(f32)
+    act_low = (gate_wide * jax.nn.sigmoid(gate_wide) * up_value).astype(bf16)
+    up_value = up_value.astype(bf16)
     down_value = scatter(*times(act_low, wd, "rf,fd->rd"))
     feed_inv = rms_scale(down_value)
     down_low = norm_back(down_value, feed_inv, feed_gain, grad_top).astype(bf16)
-    down_whole, late_hidden = gather(down_low, hidden)
-    layer_out = from_sequence(late_hidden + down_value * feed_inv * feed_gain)
-    down_whole, layer_out = both(down_whole, layer_out)
+    down_whole = gather(down_low)
 
     down_part = grads(down_whole, act_low, ids_all)
     down_whole, down_part = both(down_whole, down_part)
@@ -847,7 +858,9 @@
         up_value,
     )
     gate_part = grads(hidden_whole, gate_low, ids_all)
-    hidden_grad = grad_top + scatter_direct(*hidden_part)
+    hidden_grad, late_hidden = scatter_direct(*hidden_part, late=hidden)
+    layer_out = from_sequence(late_hidden + down_value * feed_inv * feed_gain)
+    hidden_grad, layer_out = both(grad_top + hidden_grad, layer_out)
     hidden_grad, gate_part = both(hidden_grad, gate_part)
     gate_sum = whole_sum(gate_part)
 
@@ -926,22 +939,22 @@
     gains = gains + swap(gains, "zh")
     out_sent = grads(branch_whole, late_mixed, ids_zh, (out_far, 2))
     down_term = joined(down_mine, down_other, True)
-    input_sum = scatter_direct(input_own, *input_part[1:])
+    input_sum, _ = scatter_direct(input_own, *input_part[1:])
+    out_sent = swap(out_sent, "zh")
     input_sum, in_far, out_sent, gate_sum, down_term = both(
         input_sum, in_far, out_sent, gate_sum, down_term
     )
     in_sent = grads(whole, projected_grad, ids_zh, (in_far, 2))
-    input_sum, in_sent, out_sent, gate_sum = both(input_sum, in_sent, out_sent, gate_sum)
-    in_sent, out_sent = swap(in_sent, "zh"), swap(out_sent, "zh")
+    input_sum, in_sent, gate_sum, out_sent = both(input_sum, in_sent, gate_sum, out_sent)
+    in_sent = swap(in_sent, "zh")
     gate_mine, gate_other = cross_zl(gate_sum)
+    out_mine, out_other = finish(branch_whole, mixed_low, out_far, out_sent)
     gate_term = joined(gate_mine, gate_other)
-    in_sent, gate_term, input_sum = both(in_sent, gate_term, input_sum)
+    out_term = joined(out_mine, out_other, True)
+    input_grad = from_sequence_direct(hidden_grad + input_sum)
+    up_sum, input_grad, out_term, gate_term = both(up_sum, input_grad, out_term, gate_term)
+    up_pair = cross_zl(up_sum)
     in_mine, in_other = finish(whole, projected_grad, in_far, in_sent)
-    out_sent, in_mine = both(out_sent, in_mine)
-    out_mine, out_other = finish(branch_whole, mixed_low, out_far, out_sent)
-    out_term = joined(out_mine, out_other, True)
-    up_pair = cross_zl(up_sum)
-    input_grad = from_sequence(hidden_grad + input_sum)
     gains = lax.dynamic_slice_in_dim(gains, s * block, block, 1)
     up_term = joined(*up_pair)
     query_term, key_term, value_term = (

time: 615 us -> 622 us (1.011)
  waiting for transfers between devices: 266 us -> 276 us
    reduce_scatter x3, waiting for transfers between devices: 40 us -> 0.02 us  [whole_sum(): return lax.psum_scatter(v, ('zh', 'x'), scatter_dimension=0, tiled=True)]
    ppermute x67 -> x69, waiting for transfers between devices: 173 us -> 211 us  [swap(): return lax.ppermute(v, name, ((0, 1), (1, 0)))]
    ppermute x3, waiting for transfers between devices: 40.9 us -> 53 us  [swap_zy(): return lax.ppermute(v, ('zl', 'y'), ((0, 3), (3, 0), (1, 2), (2, 1)))]
    unnamed x127 -> x137, local copies, waits for them, and re-layouts: 17 us -> 19.6 us
    ppermute x67 -> x69, starting transfers between devices: 47.8 us -> 45.6 us  [swap(): return lax.ppermute(v, name, ((0, 1), (1, 0)))]
  transfers between devices with their start and end apart: 77 -> 79, of which waited for: 47 -> 46; matrix products, arithmetic and copies ran while one was open for 12% -> 12% of each run, Pallas kernels for 16% -> 15%
where the time goes in v4:
time: 622 us; the launch traced here: 617 us
  waiting for transfers between devices  276 us (44%)
  Pallas kernels  130 us (21%)
  starting transfers between devices  72.5 us (12%)
  other arithmetic  54.9 us (9%)
  local copies, waits for them, and re-layouts  36.2 us (6%)
  matrix products  32.4 us (5%)
  between operations  15.4 us (2%)
    ppermute x69, waiting for transfers between devices, swap(): return lax.ppermute(v, name, ((0, 1), (1, 0)))  211 us
    pallas_call x9, Pallas kernels, grads(): pl.pallas_call(lambda *refs: grads_kernel(len(terms), *refs), grid_spec=p...  60.2 us
    ppermute x3, waiting for transfers between devices, swap_zy(): return lax.ppermute(v, ('zl', 'y'), ((0, 3), (3, 0), (1, 2), (2, 1)))  53 us
    ppermute x69, starting transfers between devices, swap(): return lax.ppermute(v, name, ((0, 1), (1, 0)))  45.6 us
    pallas_call x1, Pallas kernels, grouped(): pl.pallas_call(feed_back_kernel, grid_spec=pltpu.PrefetchScalarGridSpec(n...  25 us
    unnamed x137, local copies, waits for them, and re-layouts  19.6 us
    pallas_call x4, Pallas kernels, assemble(): pl.pallas_call(lambda *refs: assemble_kernel(moves, *refs), in_specs=[pl....  17.5 us
    pallas_call x1, Pallas kernels, grouped(): pl.pallas_call(lambda *refs: attend_kernel(heads, *refs), out_shape=[rows...  12.9 us
  transfers between devices with their start and end apart: 79, of which 46 were waited for; matrix products, arithmetic and copies ran while one was open for 12% of the time, Pallas kernels for 15%

profile of v4, /device:TPU:0, one launch (start us, length us, event | category | flops | bytes accessed | tf_op | source)
XLA Modules:
  0.0 617.3 jit_solution(13906923494620351217)
XLA Ops:
  9.5 6.2 %all-to-all-start = ((bf16[4,32,2048]{2,1,0:T(8,128)(2,1)}), bf16[4,32,2048]{2,1,0:T(8,128)(2,1)S(1)}, u32[]{:S(2)}, u32[]{:S(2)}) async-start(bf16[4,32,2048]{2,1,0:T(8,128)(2,1)} %bitcast.140), calls=%async_computation | async-start | bytes 1048576 | tf_op jit(solution)/shard_map/all_to_all | solution.py:600
  18.6 11.6 %all-to-all-done = bf16[4,32,2048]{2,1,0:T(8,128)(2,1)S(1)} async-done(((bf16[4,32,2048]{2,1,0:T(8,128)(2,1)}), bf16[4,32,2048]{2,1,0:T(8,128)(2,1)S(1)}, u32[]{:S(2)}, u32[]{:S(2)}) %all-to-all-start) | async-done | bytes 524320 | tf_op jit(solution)/shard_map/all_to_all | solution.py:600
  32.0 5.5 collective-permute-done
  45.7 5.0 all-to-all-start.1
  59.2 4.3 assemble.4.refs_1_
  63.7 6.1 fusion.51
  84.1 12.9 %attend.1 = (bf16[2,2,256,256]{3,2,1,0:T(8,128)(2,1)}, f32[2,2,256,256]{3,2,1,0:T(8,128)}, f32[2,2,256,2]{3,2,1,0:T(8,128)}, bf16[2,2,256,256]{3,2,1,0:T(8,128)(...) custom-call(f32[2,2,256,768]{3,2,1,0:T(8,128)} %bitcast.141, f32[2,2,256,2]{3,2,1,0:T(8,128)} %bitcast.160, ...), custom_call_target="tpu_custom_call" | custom-call | tf_op jit(solution)/shard_map/attend/pallas_call | solution.py:793
  106.0 12.3 %collective-permute-done.13 = bf16[128,2048]{1,0:T(8,128)(2,1)S(1)} collective-permute-done((bf16[128,2048]{1,0:T(8,128)(2,1)S(1)}, bf16[128,2048]{1,0:T(8,128)(2,1)S(1)}, u32[]{:S(2)}, u32[]{:S(2)}) %collective-permute-start.13) | collective-permute-done | bytes 524320 | tf_op jit(solution)/shard_map/ppermute | solution.py:597
  122.0 4.1 collective-permute-done.16
  131.0 4.5 collective-permute-done.17
  138.6 9.6 %collective-permute-done.19.refs_1_ = bf16[128,2048]{1,0:T(8,128)(2,1)S(1)} collective-permute-done((bf16[128,2048]{1,0:T(8,128)(2,1)S(1)}, bf16[128,2048]{1,0:T(8,128)(2,1)S(1)}, u32[]{:S(2)}, u32[]{:S(2)}) %collective-permute-start.19) | collective-permute-done | bytes 524320 | tf_op jit(solution)/shard_map/ppermute | solution.py:597
  152.5 4.5 assemble.5.refs_1_
  157.0 8.1 %fusion.19.gate_ref = bf16[1024,1024]{1,0:T(8,128)(2,1)S(1)} fusion(bf16[1024,2048]{1,0:T(8,128)(2,1)} %assemble.5.refs_1_, bf16[2048,2048]{1,0:T(8,128)(2,1)} %wg_ref, s32[]{:T(128)S(6)} %select_n.134), kind=kOutput, calls=%fused_computation.34 | convolution fusion | flops 4296015872 | bytes 10485764 | tf_op jit(solution)/shard_map/rd,df->rf/dot_general | solution.py:811
  165.2 6.6 %fusion.54 = (bf16[1024,1024]{1,0:T(8,128)(2,1)}, bf16[1024,1024]{1,0:T(8,128)(2,1)S(1)}) fusion(bf16[1024,1024]{1,0:T(8,128)(2,1)S(1)} %fusion.19.gate_ref, bf16[1024,2048]{1,0:T(8,128)(2,1)S(1)} %copy-done.2, bf16[2048,2048]{1,0:T(8,128)(2,1)S(1)} %bitcast.145, s32[]{:T(128)S(6)} %select_n.134), kind=kOutput, calls=%fused_computation.194 | convolution fusion | flops 4303355904 | bytes 14680068 | tf_op jit(solution)/shard_map/rd,df->rf/dot_general | solution.py:813
  181.2 12.2 %collective-permute-done.27 = bf16[128,2048]{1,0:T(8,128)(2,1)S(1)} collective-permute-done((bf16[128,2048]{1,0:T(8,128)(2,1)S(1)}, bf16[128,2048]{1,0:T(8,128)(2,1)S(1)}, u32[]{:S(2)}, u32[]{:S(2)}) %collective-permute-start.27) | collective-permute-done | bytes 524320 | tf_op jit(solution)/shard_map/ppermute | solution.py:597
  196.4 5.5 collective-permute-done.30
  205.4 4.7 collective-permute-done.31
  214.1 8.1 %collective-permute-done.33.refs_1_ = bf16[128,2048]{1,0:T(8,128)(2,1)} collective-permute-done((bf16[128,2048]{1,0:T(8,128)(2,1)S(1)}, bf16[128,2048]{1,0:T(8,128)(2,1)}, u32[]{:S(2)}, u32[]{:S(2)}) %collective-permute-start.33) | collective-permute-done | bytes 524320 | tf_op jit(solution)/shard_map/ppermute | solution.py:597
  226.4 4.3 assemble.6.refs_1_.rows_ref
  230.8 10.9 %grads.9 = bf16[2048,1024]{1,0:T(8,128)(2,1)} custom-call(s32[8]{0:T(128)} %add_xor_fusion.refs_0_, bf16[1024,2048]{1,0:T(8,128)(2,1)} %assemble.6.refs_1_.rows_ref, bf16[1024,1024]{1,0:T(8,128)(2,1)} %copy-done.23), custom_call_target="tpu_custom_call" | custom-call | tf_op jit(solution)/shard_map/grads/pallas_call | solution.py:514
  241.7 25.0 %feed_back.1 = (bf16[1024,1024]{1,0:T(8,128)(2,1)}, bf16[1024,1024]{1,0:T(8,128)(2,1)}, bf16[512,2048]{1,0:T(8,128)(2,1)}, bf16[256,2048]{1,0:T(8,128)(2,1)}, bf16[256,2048]{1,0:T(8,128)(2,1)}) custom-call(s32[1]{0:T(128)} %bitcast.5.zl_ref, bf16[1024,2048]{1,0:T(8,128)(2,1)} %assemble.6.refs_1_.rows_ref, bf16[2048,2048]{1,0:T(8,128)(2,1)} %wg_ref, ...), custom_call_target="tpu_custom_call" | custom-call | tf_op jit(solution)/shard_map/feed_back/pallas_call | solution.py:831
  281.4 5.7 all-to-all-start.2
  287.0 11.0 %grads.10 = bf16[2048,1024]{1,0:T(8,128)(2,1)} custom-call(s32[8]{0:T(128)} %add_xor_fusion.refs_0_, bf16[1024,2048]{1,0:T(8,128)(2,1)} %assemble.5.refs_1_, bf16[1024,1024]{1,0:T(8,128)(2,1)} %get-tuple-element.183.refs_2_), custom_call_target="tpu_custom_call" | custom-call | tf_op jit(solution)/shard_map/grads/pallas_call | solution.py:514
  298.0 11.4 %collective-permute-done.43 = bf16[128,2048]{1,0:T(8,128)(2,1)S(1)} collective-permute-done((bf16[128,2048]{1,0:T(8,128)(2,1)}, bf16[128,2048]{1,0:T(8,128)(2,1)S(1)}, u32[]{:S(2)}, u32[]{:S(2)}) %collective-permute-start.43) | collective-permute-done | bytes 524320 | tf_op jit(solution)/shard_map/ppermute | solution.py:648
  309.4 10.6 %collective-permute-done.42 = bf16[128,2048]{1,0:T(8,128)(2,1)S(1)} collective-permute-done((bf16[128,2048]{1,0:T(8,128)(2,1)}, bf16[128,2048]{1,0:T(8,128)(2,1)S(1)}, u32[]{:S(2)}, u32[]{:S(2)}) %collective-permute-start.42) | collective-permute-done | bytes 524320 | tf_op jit(solution)/shard_map/ppermute | solution.py:597
  327.9 10.0 %collective-permute-done.44.refs_1_ = bf16[128,2048]{1,0:T(8,128)(2,1)S(1)} collective-permute-done((bf16[128,2048]{1,0:T(8,128)(2,1)S(1)}, bf16[128,2048]{1,0:T(8,128)(2,1)S(1)}, u32[]{:S(2)}, u32[]{:S(2)}) %collective-permute-start.44) | collective-permute-done | bytes 524320 | tf_op jit(solution)/shard_map/ppermute | solution.py:597
  337.9 8.6 %collective-permute-done.45.refs_2_ = bf16[128,2048]{1,0:T(8,128)(2,1)S(1)} collective-permute-done((bf16[128,2048]{1,0:T(8,128)(2,1)S(1)}, bf16[128,2048]{1,0:T(8,128)(2,1)S(1)}, u32[]{:S(2)}, u32[]{:S(2)}) %collective-permute-start.45) | collective-permute-done | bytes 524320 | tf_op jit(solution)/shard_map/ppermute | solution.py:597
  346.5 14.7 %collective-permute-done.46.refs_3_ = bf16[128,2048]{1,0:T(8,128)(2,1)S(1)} collective-permute-done((bf16[128,2048]{1,0:T(8,128)(2,1)S(1)}, bf16[128,2048]{1,0:T(8,128)(2,1)S(1)}, u32[]{:S(2)}, u32[]{:S(2)}) %collective-permute-start.46) | collective-permute-done | bytes 524320 | tf_op jit(solution)/shard_map/ppermute | solution.py:648
  362.6 11.1 %grads.11 = bf16[2048,1024]{1,0:T(8,128)(2,1)} custom-call(s32[8]{0:T(128)} %add_xor_fusion.refs_0_, bf16[1024,2048]{1,0:T(8,128)(2,1)} %assemble.5.refs_1_, bf16[1024,1024]{1,0:T(8,128)(2,1)} %get-tuple-element.194.refs_2_), custom_call_target="tpu_custom_call" | custom-call | tf_op jit(solution)/shard_map/grads/pallas_call | solution.py:514
  373.7 4.4 assemble.7.rows_ref.refs_1_
  378.1 4.3 mixed_back.1
  382.4 10.1 %attend_back.1 = (f32[2,2,256,256]{3,2,1,0:T(8,128)}, f32[2,2,256,256]{3,2,1,0:T(8,128)}, bf16[2,2,256,256]{3,2,1,0:T(8,128)(2,1)}) custom-call(bf16[2,2,256,256]{3,2,1,0:T(8,128)(2,1)} %get-tuple-element.196.refs_0_, bf16[2,2,256,256]{3,2,1,0:T(8,128)(2,1)} %get-tuple-element.197.refs_1_, bf16[2,2,256,256]{3,2,1,0:T(8,128)(2,1)} %get-tuple-element.198.refs_2_, ...), custom_call_target="tpu_custom_call" | custom-call | tf_op jit(solution)/shard_map/attend_back/pallas_call | solution.py:889
  397.2 3.7 collective-permute-done.52
  401.8 5.0 grads.12
  422.2 3.0 copy.109
  425.3 3.0 convolution_convert_fusion.3
  428.3 8.8 %collective-permute-done.56 = bf16[256,1024]{1,0:T(8,128)(2,1)} collective-permute-done((bf16[256,1024]{1,0:T(8,128)(2,1)}, bf16[256,1024]{1,0:T(8,128)(2,1)}, u32[]{:S(2)}, u32[]{:S(2)}) %collective-permute-start.56) | collective-permute-done | bytes 524320 | tf_op jit(solution)/shard_map/ppermute | solution.py:597
  437.2 6.1 grads.13
  452.8 3.3 grads.14
  459.6 27.0 %collective-permute-done.61 = bf16[128,2048]{1,0:T(8,128)(2,1)S(1)} collective-permute-done((bf16[128,2048]{1,0:T(8,128)(2,1)S(1)}, bf16[128,2048]{1,0:T(8,128)(2,1)S(1)}, u32[]{:S(2)}, u32[]{:S(2)}) %collective-permute-start.61) | collective-permute-done | bytes 524320 | tf_op jit(solution)/shard_map/ppermute | solution.py:648
  486.6 15.5 %collective-permute-done.60 = bf16[128,2048]{1,0:T(8,128)(2,1)S(1)} collective-permute-done((bf16[128,2048]{1,0:T(8,128)(2,1)S(1)}, bf16[128,2048]{1,0:T(8,128)(2,1)S(1)}, u32[]{:S(2)}, u32[]{:S(2)}) %collective-permute-start.60) | collective-permute-done | bytes 524320 | tf_op jit(solution)/shard_map/ppermute | solution.py:597
  503.4 4.6 grads.15
  509.3 3.6 grads.16
  523.4 18.5 %collective-permute-done.67 = bf16[256,256]{1,0:T(8,128)(2,1)S(1)} collective-permute-done((bf16[256,256]{1,0:T(8,128)(2,1)}, bf16[256,256]{1,0:T(8,128)(2,1)S(1)}, u32[]{:S(2)}, u32[]{:S(2)}) %collective-permute-start.67) | collective-permute-done | bytes 131104 | tf_op jit(solution)/shard_map/ppermute | solution.py:597
  548.8 29.9 %collective-permute-done.69.refs_4_ = bf16[512,768]{1,0:T(8,128)(2,1)} collective-permute-done((bf16[512,768]{1,0:T(8,128)(2,1)S(1)}, bf16[512,768]{1,0:T(8,128)(2,1)}, u32[]{:S(2)}, u32[]{:S(2)}) %collective-permute-start.69) | collective-permute-done | bytes 786464 | tf_op jit(solution)/shard_map/ppermute | solution.py:597
  578.7 4.7 grads.17
  591.3 5.4 collective-permute-done.70
  600.3 6.7 %collective-permute-done.71 = bf16[256,1024]{1,0:T(8,128)(2,1)} collective-permute-done((bf16[256,1024]{1,0:T(8,128)(2,1)}, bf16[256,1024]{1,0:T(8,128)(2,1)}, u32[]{:S(2)}, u32[]{:S(2)}) %collective-permute-start.71) | collective-permute-done | bytes 524320 | tf_op jit(solution)/shard_map/ppermute | solution.py:597
  (446 shorter events, 179.6 us)
Async XLA Ops:
  9.5 20.7 %all-to-all-start = ((bf16[4,32,2048]{2,1,0:T(8,128)(2,1)}), bf16[4,32,2048]{2,1,0:T(8,128)(2,1)S(1)}, u32[]{:S(2)}, u32[]{:S(2)}) async-start(bf16[4,32,2048]{2,1,0:T(8,128)(2,1)} %bitcast.140), calls=%async_computation | async-start | bytes 1048576 | tf_op jit(solution)/shard_map/all_to_all | solution.py:600
  30.2 7.2 %collective-permute-start = (bf16[64,2048]{1,0:T(8,128)(2,1)S(1)}, bf16[64,2048]{1,0:T(8,128)(2,1)S(1)}, u32[]{:S(2)}, u32[]{:S(2)}) collective-permute-start(bf16[64,2048]{1,0:T(8,128)(2,1)S(1)} %bitcast.165), channel_id=1, source_target_pairs={{0,2},{2,0},{1,3},{3,1},{4,6},{6,4},{5,7},{7,5},{8,10},{10,8},{9,1... | collective-permute-start | bytes 786440 | tf_op jit(solution)/shard_map/ppermute | solution.py:597
  40.8 12.8 %collective-permute-start.2 = (bf16[128,2048]{1,0:T(8,128)(2,1)}, bf16[128,2048]{1,0:T(8,128)(2,1)}, u32[]{:S(2)}, u32[]{:S(2)}) collective-permute-start(bf16[128,2048]{1,0:T(8,128)(2,1)} %get-tuple-element.126.refs_0_), channel_id=1, source_target_pairs={{0,8},{8,0},{1,9},{9,1},{2,10},{10,2},{3,11},{11,3},{4,12},{12,4},... | collective-permute-start | bytes 1572872 | tf_op jit(solution)/shard_map/ppermute | solution.py:597
  41.1 12.5 %collective-permute-start.3 = (bf16[128,2048]{1,0:T(8,128)(2,1)}, bf16[128,2048]{1,0:T(8,128)(2,1)}, u32[]{:S(2)}, u32[]{:S(2)}) collective-permute-start(bf16[128,2048]{1,0:T(8,128)(2,1)} %get-tuple-element.127.refs_2_), channel_id=1, source_target_pairs={{0,2},{2,0},{1,3},{3,1},{4,6},{6,4},{5,7},{7,5},{8,10},{10,8},{9,1... | collective-permute-start | bytes 1572872 | tf_op jit(solution)/shard_map/ppermute | solution.py:597
  45.7 18.0 %all-to-all-start.1 = ((bf16[4,32,2048]{2,1,0:T(8,128)(2,1)}), bf16[4,32,2048]{2,1,0:T(8,128)(2,1)S(1)}, u32[]{:S(2)}, u32[]{:S(2)}) async-start(bf16[4,32,2048]{2,1,0:T(8,128)(2,1)} %bitcast.158), calls=%async_computation.1 | async-start | bytes 1048576 | tf_op jit(solution)/shard_map/all_to_all | solution.py:600
  50.7 357.9 %reduce-scatter.6.cloned.1.call-start = ((), (), s32[]{:S(2)}) async-start(), calls=%async_computation.7 | async-start | bytes 5242880 | tf_op jit(solution)/shard_map/reduce_scatter | solution.py:720
  104.2 14.0 %collective-permute-start.13 = (bf16[128,2048]{1,0:T(8,128)(2,1)S(1)}, bf16[128,2048]{1,0:T(8,128)(2,1)S(1)}, u32[]{:S(2)}, u32[]{:S(2)}) collective-permute-start(bf16[128,2048]{1,0:T(8,128)(2,1)S(1)} %slice.337), channel_id=1, source_target_pairs={{0,8},{8,0},{1,9},{9,1},{2,10},{10,2},{3,11},{11,3},{4,12},{12,4},... | collective-permute-start | bytes 1572872 | tf_op jit(solution)/shard_map/ppermute | solution.py:597
  104.4 14.0 %collective-permute-start.14 = (bf16[2,64,2048]{2,1,0:T(8,128)(2,1)S(1)}, bf16[2,64,2048]{2,1,0:T(8,128)(2,1)S(1)}, u32[]{:S(2)}, u32[]{:S(2)}) collective-permute-start(bf16[2,64,2048]{2,1,0:T(8,128)(2,1)S(1)} %slice_bitcast_fusion.3), channel_id=1, source_target_pairs={{0,2},{2,0},{1,3},{3,1},{4,6},{6,4},{5,7},{7,5},{8,10},{10,8},{9,1... | collective-permute-start | bytes 1572872 | tf_op jit(solution)/shard_map/ppermute | solution.py:597
  118.5 7.5 %collective-permute-start.16 = (bf16[64,2048]{1,0:T(8,128)(2,1)S(1)}, bf16[64,2048]{1,0:T(8,128)(2,1)S(1)}, u32[]{:S(2)}, u32[]{:S(2)}) collective-permute-start(bf16[64,2048]{1,0:T(8,128)(2,1)S(1)} %slice_bitcast_fusion.7), channel_id=1, source_target_pairs={{0,8},{8,0},{1,9},{9,1},{2,10},{10,2},{3,11},{11,3},{4,12},{12,4},... | collective-permute-start | bytes 786440 | tf_op jit(solution)/shard_map/ppermute | solution.py:597
  137.5 10.6 %collective-permute-start.19 = (bf16[128,2048]{1,0:T(8,128)(2,1)S(1)}, bf16[128,2048]{1,0:T(8,128)(2,1)S(1)}, u32[]{:S(2)}, u32[]{:S(2)}) collective-permute-start(bf16[128,2048]{1,0:T(8,128)(2,1)S(1)} %pad_maximum_fusion.7.refs_0_), channel_id=1, source_target_pairs={{0,8},{8,0},{1,9},{9,1},{2,10},{10,2},{3,11},{11,3},{4,12},{12,4},... | collective-permute-start | bytes 1572872 | tf_op jit(solution)/shard_map/ppermute | solution.py:597
  137.9 10.3 %collective-permute-start.20 = (bf16[128,2048]{1,0:T(8,128)(2,1)S(1)}, bf16[128,2048]{1,0:T(8,128)(2,1)}, u32[]{:S(2)}, u32[]{:S(2)}) collective-permute-start(bf16[128,2048]{1,0:T(8,128)(2,1)S(1)} %pad_maximum_fusion.8.refs_2_), channel_id=1, source_target_pairs={{0,2},{2,0},{1,3},{3,1},{4,6},{6,4},{5,7},{7,5},{8,10},{10,8},{9,1... | collective-permute-start | bytes 1572872 | tf_op jit(solution)/shard_map/ppermute | solution.py:597
  179.4 14.0 %collective-permute-start.27 = (bf16[128,2048]{1,0:T(8,128)(2,1)S(1)}, bf16[128,2048]{1,0:T(8,128)(2,1)S(1)}, u32[]{:S(2)}, u32[]{:S(2)}) collective-permute-start(bf16[128,2048]{1,0:T(8,128)(2,1)S(1)} %slice.349), channel_id=1, source_target_pairs={{0,8},{8,0},{1,9},{9,1},{2,10},{10,2},{3,11},{11,3},{4,12},{12,4},... | collective-permute-start | bytes 1572872 | tf_op jit(solution)/shard_map/ppermute | solution.py:597
  180.8 13.8 %collective-permute-start.28 = (bf16[2,64,2048]{2,1,0:T(8,128)(2,1)S(1)}, bf16[2,64,2048]{2,1,0:T(8,128)(2,1)S(1)}, u32[]{:S(2)}, u32[]{:S(2)}) collective-permute-start(bf16[2,64,2048]{2,1,0:T(8,128)(2,1)S(1)} %slice_bitcast_fusion.1), channel_id=1, source_target_pairs={{0,2},{2,0},{1,3},{3,1},{4,6},{6,4},{5,7},{7,5},{8,10},{10,8},{9,1... | collective-permute-start | bytes 1572872 | tf_op jit(solution)/shard_map/ppermute | solution.py:597
  194.7 7.3 %collective-permute-start.30 = (bf16[64,2048]{1,0:T(8,128)(2,1)S(1)}, bf16[64,2048]{1,0:T(8,128)(2,1)S(1)}, u32[]{:S(2)}, u32[]{:S(2)}) collective-permute-start(bf16[64,2048]{1,0:T(8,128)(2,1)S(1)} %slice_bitcast_fusion.5), channel_id=1, source_target_pairs={{0,8},{8,0},{1,9},{9,1},{2,10},{10,2},{3,11},{11,3},{4,12},{12,4},... | collective-permute-start | bytes 786440 | tf_op jit(solution)/shard_map/ppermute | solution.py:597
  211.4 10.7 %collective-permute-start.33 = (bf16[128,2048]{1,0:T(8,128)(2,1)S(1)}, bf16[128,2048]{1,0:T(8,128)(2,1)}, u32[]{:S(2)}, u32[]{:S(2)}) collective-permute-start(bf16[128,2048]{1,0:T(8,128)(2,1)S(1)} %pad_maximum_fusion.9.refs_0_), channel_id=1, source_target_pairs={{0,8},{8,0},{1,9},{9,1},{2,10},{10,2},{3,11},{11,3},{4,12},{12,4},... | collective-permute-start | bytes 1572872 | tf_op jit(solution)/shard_map/ppermute | solution.py:597
  212.8 9.4 %collective-permute-start.34 = (bf16[128,2048]{1,0:T(8,128)(2,1)S(1)}, bf16[128,2048]{1,0:T(8,128)(2,1)}, u32[]{:S(2)}, u32[]{:S(2)}) collective-permute-start(bf16[128,2048]{1,0:T(8,128)(2,1)S(1)} %pad_maximum_fusion.10.refs_2_), channel_id=1, source_target_pairs={{0,2},{2,0},{1,3},{3,1},{4,6},{6,4},{5,7},{7,5},{8,10},{10,8},{9,1... | collective-permute-start | bytes 1572872 | tf_op jit(solution)/shard_map/ppermute | solution.py:597
  275.2 34.2 %collective-permute-start.43 = (bf16[128,2048]{1,0:T(8,128)(2,1)}, bf16[128,2048]{1,0:T(8,128)(2,1)S(1)}, u32[]{:S(2)}, u32[]{:S(2)}) collective-permute-start(bf16[128,2048]{1,0:T(8,128)(2,1)} %pad_maximum_fusion.13), channel_id=1, source_target_pairs={{0,10},{10,0},{2,8},{8,2},{1,11},{11,1},{3,9},{9,3},{4,14},{14,4},... | collective-permute-start | bytes 1572872 | tf_op jit(solution)/shard_map/ppermute | solution.py:648
  278.1 41.9 %collective-permute-start.42 = (bf16[128,2048]{1,0:T(8,128)(2,1)}, bf16[128,2048]{1,0:T(8,128)(2,1)S(1)}, u32[]{:S(2)}, u32[]{:S(2)}) collective-permute-start(bf16[128,2048]{1,0:T(8,128)(2,1)} %pad_maximum_fusion.12), channel_id=1, source_target_pairs={{0,8},{8,0},{1,9},{9,1},{2,10},{10,2},{3,11},{11,3},{4,12},{12,4},... | collective-permute-start | bytes 1572872 | tf_op jit(solution)/shard_map/ppermute | solution.py:597
  280.1 39.9 %collective-permute-start.41 = (bf16[128,2048]{1,0:T(8,128)(2,1)}, bf16[128,2048]{1,0:T(8,128)(2,1)}, u32[]{:S(2)}, u32[]{:S(2)}) collective-permute-start(bf16[128,2048]{1,0:T(8,128)(2,1)} %pad_maximum_fusion.11), channel_id=1, source_target_pairs={{0,2},{2,0},{1,3},{3,1},{4,6},{6,4},{5,7},{7,5},{8,10},{10,8},{9,1... | collective-permute-start | bytes 1572872 | tf_op jit(solution)/shard_map/ppermute | solution.py:597
  281.4 41.3 %all-to-all-start.2 = ((bf16[4,32,2048]{2,1,0:T(8,128)(2,1)}), bf16[4,32,2048]{2,1,0:T(8,128)(2,1)S(1)}, u32[]{:S(2)}, u32[]{:S(2)}) async-start(bf16[4,32,2048]{2,1,0:T(8,128)(2,1)} %bitcast.30), calls=%async_computation.2 | async-start | bytes 1048576 | tf_op jit(solution)/shard_map/all_to_all | solution.py:605
  287.0 216.3 %reduce-scatter.8.cloned.1.call-start = ((), (), s32[]{:S(2)}) async-start(), calls=%async_computation.8 | async-start | bytes 5242880 | tf_op jit(solution)/shard_map/reduce_scatter | solution.py:720
  323.7 225.1 %reduce-scatter.4.cloned.1.call-start = ((), (), s32[]{:S(2)}) async-start(), calls=%async_computation.6 | async-start | bytes 5242880 | tf_op jit(solution)/shard_map/reduce_scatter | solution.py:720
  324.4 13.6 %collective-permute-start.44 = (bf16[128,2048]{1,0:T(8,128)(2,1)S(1)}, bf16[128,2048]{1,0:T(8,128)(2,1)S(1)}, u32[]{:S(2)}, u32[]{:S(2)}) collective-permute-start(bf16[128,2048]{1,0:T(8,128)(2,1)S(1)} %subtract_convert_fusion.1.refs_0_), channel_id=1, source_target_pairs={{0,2},{2,0},{1,3},{3,1},{4,6},{6,4},{5,7},{7,5},{8,10},{10,8},{9,1... | collective-permute-start | bytes 1572872 | tf_op jit(solution)/shard_map/ppermute | solution.py:597
  325.7 20.8 %collective-permute-start.45 = (bf16[128,2048]{1,0:T(8,128)(2,1)S(1)}, bf16[128,2048]{1,0:T(8,128)(2,1)S(1)}, u32[]{:S(2)}, u32[]{:S(2)}) collective-permute-start(bf16[128,2048]{1,0:T(8,128)(2,1)S(1)} %subtract_convert_fusion.1.refs_0_), channel_id=1, source_target_pairs={{0,8},{8,0},{1,9},{9,1},{2,10},{10,2},{3,11},{11,3},{4,12},{12,4},... | collective-permute-start | bytes 1572872 | tf_op jit(solution)/shard_map/ppermute | solution.py:597
  325.7 35.5 %collective-permute-start.46 = (bf16[128,2048]{1,0:T(8,128)(2,1)S(1)}, bf16[128,2048]{1,0:T(8,128)(2,1)S(1)}, u32[]{:S(2)}, u32[]{:S(2)}) collective-permute-start(bf16[128,2048]{1,0:T(8,128)(2,1)S(1)} %subtract_convert_fusion.1.refs_0_), channel_id=1, source_target_pairs={{0,10},{10,0},{2,8},{8,2},{1,11},{11,1},{3,9},{9,3},{4,14},{14,4},... | collective-permute-start | bytes 1572872 | tf_op jit(solution)/shard_map/ppermute | solution.py:648
  327.9 33.3 %collective-permute-start.47 = (bf16[128,2048]{1,0:T(8,128)(2,1)S(1)}, bf16[128,2048]{1,0:T(8,128)(2,1)S(1)}, u32[]{:S(2)}, u32[]{:S(2)}) collective-permute-start(bf16[128,2048]{1,0:T(8,128)(2,1)S(1)} %subtract_convert_fusion.1.refs_0_), channel_id=1, source_target_pairs={{0,1},{1,0},{2,3},{3,2},{4,5},{5,4},{6,7},{7,6},{8,9},{9,8},{10,11... | collective-permute-start | bytes 1572872 | tf_op jit(solution)/shard_map/ppermute | solution.py:597
  361.2 12.5 %collective-permute-start.48 = (bf16[128,2048]{1,0:T(8,128)(2,1)S(1)}, bf16[128,2048]{1,0:T(8,128)(2,1)}, u32[]{:S(2)}, u32[]{:S(2)}) collective-permute-start(bf16[128,2048]{1,0:T(8,128)(2,1)S(1)} %collective-permute-done.44.refs_1_), channel_id=1, source_target_pairs={{0,1},{1,0},{2,3},{3,2},{4,5},{5,4},{6,7},{7,6},{8,9},{9,8},{10,11... | collective-permute-start | bytes 1572872 | tf_op jit(solution)/shard_map/ppermute | solution.py:597
  362.1 11.6 %collective-permute-start.49 = (bf16[128,2048]{1,0:T(8,128)(2,1)S(1)}, bf16[128,2048]{1,0:T(8,128)(2,1)}, u32[]{:S(2)}, u32[]{:S(2)}) collective-permute-start(bf16[128,2048]{1,0:T(8,128)(2,1)S(1)} %collective-permute-done.45.refs_2_), channel_id=1, source_target_pairs={{0,1},{1,0},{2,3},{3,2},{4,5},{5,4},{6,7},{7,6},{8,9},{9,8},{10,11... | collective-permute-start | bytes 1572872 | tf_op jit(solution)/shard_map/ppermute | solution.py:597
  362.2 11.5 %collective-permute-start.50 = (bf16[128,2048]{1,0:T(8,128)(2,1)S(1)}, bf16[128,2048]{1,0:T(8,128)(2,1)}, u32[]{:S(2)}, u32[]{:S(2)}) collective-permute-start(bf16[128,2048]{1,0:T(8,128)(2,1)S(1)} %collective-permute-done.46.refs_3_), channel_id=1, source_target_pairs={{0,1},{1,0},{2,3},{3,2},{4,5},{5,4},{6,7},{7,6},{8,9},{9,8},{10,11... | collective-permute-start | bytes 1572872 | tf_op jit(solution)/shard_map/ppermute | solution.py:597
  406.9 18.4 %collective-permute-start.55 = (f32[4,2048]{1,0:T(4,128)S(1)}, f32[4,2048]{1,0:T(4,128)S(1)}, u32[]{:S(2)}, u32[]{:S(2)}) collective-permute-start(f32[4,2048]{1,0:T(4,128)S(1)} %reshape.363), channel_id=1, source_target_pairs={{0,4},{4,0},{1,5},{5,1},{2,6},{6,2},{3,7},{7,3},{8,12},{12,8},{9,1... | collective-permute-start | bytes 98312 | tf_op jit(solution)/shard_map/ppermute | solution.py:597
  416.7 29.3 %collective-permute-start.57 = (bf16[256,2048]{1,0:T(8,128)(2,1)}, bf16[256,2048]{1,0:T(8,128)(2,1)}, u32[]{:S(2)}, u32[]{:S(2)}) collective-permute-start(bf16[256,2048]{1,0:T(8,128)(2,1)} %get-tuple-element.323), channel_id=1, source_target_pairs={{0,1},{1,0},{2,3},{3,2},{4,5},{5,4},{6,7},{7,6},{8,9},{9,8},{10,11... | collective-permute-start | bytes 3145736 | tf_op jit(solution)/shard_map/ppermute | solution.py:597
  416.7 29.3 %collective-permute-start.58 = (bf16[256,2048]{1,0:T(8,128)(2,1)}, bf16[256,2048]{1,0:T(8,128)(2,1)}, u32[]{:S(2)}, u32[]{:S(2)}) collective-permute-start(bf16[256,2048]{1,0:T(8,128)(2,1)} %get-tuple-element.322), channel_id=1, source_target_pairs={{0,1},{1,0},{2,3},{3,2},{4,5},{5,4},{6,7},{7,6},{8,9},{9,8},{10,11... | collective-permute-start | bytes 3145736 | tf_op jit(solution)/shard_map/ppermute | solution.py:597
  418.5 18.7 %collective-permute-start.56 = (bf16[256,1024]{1,0:T(8,128)(2,1)}, bf16[256,1024]{1,0:T(8,128)(2,1)}, u32[]{:S(2)}, u32[]{:S(2)}) collective-permute-start(bf16[256,1024]{1,0:T(8,128)(2,1)} %get-tuple-element.339), channel_id=1, source_target_pairs={{0,8},{8,0},{1,9},{9,1},{2,10},{10,2},{3,11},{11,3},{4,12},{12,4},... | collective-permute-start | bytes 1572872 | tf_op jit(solution)/shard_map/ppermute | solution.py:597
  420.5 16.7 %collective-permute-start.54 = (bf16[1024,256]{1,0:T(8,128)(2,1)}, bf16[1024,256]{1,0:T(8,128)(2,1)S(1)}, u32[]{:S(2)}, u32[]{:S(2)}) collective-permute-start(bf16[1024,256]{1,0:T(8,128)(2,1)} %grads.12), channel_id=1, source_target_pairs={{0,4},{4,0},{1,5},{5,1},{2,6},{6,2},{3,7},{7,3},{8,12},{12,8},{9,1... | collective-permute-start | bytes 1572872 | tf_op jit(solution)/shard_map/ppermute | solution.py:597
  437.2 18.9 %collective-permute-start.72 = (f32[4,2048]{1,0:T(4,128)S(1)}, f32[4,2048]{1,0:T(4,128)S(1)}, u32[]{:S(2)}, u32[]{:S(2)}) collective-permute-start(f32[4,2048]{1,0:T(4,128)S(1)} %add.257), channel_id=1, source_target_pairs={{0,16},{16,0},{1,17},{17,1},{2,18},{18,2},{3,19},{19,3},{4,20},{20... | collective-permute-start | bytes 98312 | tf_op jit(solution)/shard_map/ppermute | solution.py:597
  443.3 60.1 %collective-permute-start.62 = (bf16[1024,768]{1,0:T(8,128)(2,1)}, bf16[1024,768]{1,0:T(8,128)(2,1)}, u32[]{:S(2)}, u32[]{:S(2)}) collective-permute-start(bf16[1024,768]{1,0:T(8,128)(2,1)} %grads.13), channel_id=1, source_target_pairs={{0,4},{4,0},{1,5},{5,1},{2,6},{6,2},{3,7},{7,3},{8,12},{12,8},{9,1... | collective-permute-start | bytes 4718600 | tf_op jit(solution)/shard_map/ppermute | solution.py:597
  448.7 37.9 %collective-permute-start.61 = (bf16[128,2048]{1,0:T(8,128)(2,1)S(1)}, bf16[128,2048]{1,0:T(8,128)(2,1)S(1)}, u32[]{:S(2)}, u32[]{:S(2)}) collective-permute-start(bf16[128,2048]{1,0:T(8,128)(2,1)S(1)} %pad_maximum_fusion.16), channel_id=1, source_target_pairs={{0,10},{10,0},{2,8},{8,2},{1,11},{11,1},{3,9},{9,3},{4,14},{14,4},... | collective-permute-start | bytes 1572872 | tf_op jit(solution)/shard_map/ppermute | solution.py:648
  451.7 50.3 %collective-permute-start.60 = (bf16[128,2048]{1,0:T(8,128)(2,1)S(1)}, bf16[128,2048]{1,0:T(8,128)(2,1)S(1)}, u32[]{:S(2)}, u32[]{:S(2)}) collective-permute-start(bf16[128,2048]{1,0:T(8,128)(2,1)S(1)} %pad_maximum_fusion.15), channel_id=1, source_target_pairs={{0,8},{8,0},{1,9},{9,1},{2,10},{10,2},{3,11},{11,3},{4,12},{12,4},... | collective-permute-start | bytes 1572872 | tf_op jit(solution)/shard_map/ppermute | solution.py:597
  451.9 50.2 %collective-permute-start.59 = (bf16[128,2048]{1,0:T(8,128)(2,1)S(1)}, bf16[128,2048]{1,0:T(8,128)(2,1)S(1)}, u32[]{:S(2)}, u32[]{:S(2)}) collective-permute-start(bf16[128,2048]{1,0:T(8,128)(2,1)S(1)} %pad_maximum_fusion.14), channel_id=1, source_target_pairs={{0,2},{2,0},{1,3},{3,1},{4,6},{6,4},{5,7},{7,5},{8,10},{10,8},{9,1... | collective-permute-start | bytes 1572872 | tf_op jit(solution)/shard_map/ppermute | solution.py:597
  456.1 47.3 %collective-permute-start.63 = (bf16[512,256]{1,0:T(8,128)(2,1)}, bf16[512,256]{1,0:T(8,128)(2,1)S(1)}, u32[]{:S(2)}, u32[]{:S(2)}) collective-permute-start(bf16[512,256]{1,0:T(8,128)(2,1)} %grads.14), channel_id=1, source_target_pairs={{0,16},{16,0},{1,17},{17,1},{2,18},{18,2},{3,19},{19,3},{4,20},{20... | collective-permute-start | bytes 786440 | tf_op jit(solution)/shard_map/ppermute | solution.py:597
  509.3 36.7 %collective-permute-start.68 = (bf16[256,1024]{1,0:T(8,128)(2,1)}, bf16[256,1024]{1,0:T(8,128)(2,1)}, u32[]{:S(2)}, u32[]{:S(2)}) collective-permute-start(bf16[256,1024]{1,0:T(8,128)(2,1)} %get-tuple-element.337), channel_id=1, source_target_pairs={{0,8},{8,0},{1,9},{9,1},{2,10},{10,2},{3,11},{11,3},{4,12},{12,4},... | collective-permute-start | bytes 1572872 | tf_op jit(solution)/shard_map/ppermute | solution.py:597
  514.5 27.5 %collective-permute-start.67 = (bf16[256,256]{1,0:T(8,128)(2,1)}, bf16[256,256]{1,0:T(8,128)(2,1)S(1)}, u32[]{:S(2)}, u32[]{:S(2)}) collective-permute-start(bf16[256,256]{1,0:T(8,128)(2,1)} %get-tuple-element.379), channel_id=1, source_target_pairs={{0,8},{8,0},{1,9},{9,1},{2,10},{10,2},{3,11},{11,3},{4,12},{12,4},... | collective-permute-start | bytes 393224 | tf_op jit(solution)/shard_map/ppermute | solution.py:597
  517.2 25.6 %collective-permute-start.64 = (bf16[32,2048]{1,0:T(8,128)(2,1)}, bf16[32,2048]{1,0:T(8,128)(2,1)}, u32[]{:S(2)}, u32[]{:S(2)}) collective-permute-start(bf16[32,2048]{1,0:T(8,128)(2,1)} %get-tuple-element.366), channel_id=1, source_target_pairs={{0,4},{4,0},{1,5},{5,1},{2,6},{6,2},{3,7},{7,3},{8,12},{12,8},{9,1... | collective-permute-start | bytes 393224 | tf_op jit(solution)/shard_map/ppermute | solution.py:597
  518.1 24.8 %collective-permute-start.65 = (bf16[32,2048]{1,0:T(8,128)(2,1)}, bf16[32,2048]{1,0:T(8,128)(2,1)}, u32[]{:S(2)}, u32[]{:S(2)}) collective-permute-start(bf16[32,2048]{1,0:T(8,128)(2,1)} %get-tuple-element.365), channel_id=1, source_target_pairs={{0,16},{16,0},{1,17},{17,1},{2,18},{18,2},{3,19},{19,3},{4,20},{20... | collective-permute-start | bytes 393224 | tf_op jit(solution)/shard_map/ppermute | solution.py:597
  519.1 23.8 %collective-permute-start.66 = (bf16[32,2048]{1,0:T(8,128)(2,1)S(1)}, bf16[32,2048]{1,0:T(8,128)(2,1)}, u32[]{:S(2)}, u32[]{:S(2)}) collective-permute-start(bf16[32,2048]{1,0:T(8,128)(2,1)S(1)} %get-tuple-element.364), channel_id=1, source_target_pairs={{0,20},{20,0},{4,16},{16,4},{1,21},{21,1},{5,17},{17,5},{2,22},{22... | collective-permute-start | bytes 393224 | tf_op jit(solution)/shard_map/ppermute | solution.py:609
  542.0 36.8 %collective-permute-start.69 = (bf16[512,768]{1,0:T(8,128)(2,1)S(1)}, bf16[512,768]{1,0:T(8,128)(2,1)}, u32[]{:S(2)}, u32[]{:S(2)}) collective-permute-start(bf16[512,768]{1,0:T(8,128)(2,1)S(1)} %copy-done.37), channel_id=1, source_target_pairs={{0,16},{16,0},{1,17},{17,1},{2,18},{18,2},{3,19},{19,3},{4,20},{20... | collective-permute-start | bytes 2359304 | tf_op jit(solution)/shard_map/ppermute | solution.py:597
  584.5 12.2 %collective-permute-start.70 = (bf16[256,768]{1,0:T(8,128)(2,1)S(1)}, bf16[256,768]{1,0:T(8,128)(2,1)}, u32[]{:S(2)}, u32[]{:S(2)}) collective-permute-start(bf16[256,768]{1,0:T(8,128)(2,1)S(1)} %slice.389), channel_id=1, source_target_pairs={{0,8},{8,0},{1,9},{9,1},{2,10},{10,2},{3,11},{11,3},{4,12},{12,4},... | collective-permute-start | bytes 1179656 | tf_op jit(solution)/shard_map/ppermute | solution.py:597
  585.6 21.4 %collective-permute-start.71 = (bf16[256,1024]{1,0:T(8,128)(2,1)}, bf16[256,1024]{1,0:T(8,128)(2,1)}, u32[]{:S(2)}, u32[]{:S(2)}) collective-permute-start(bf16[256,1024]{1,0:T(8,128)(2,1)} %get-tuple-element.335), channel_id=1, source_target_pairs={{0,8},{8,0},{1,9},{9,1},{2,10},{10,2},{3,11},{11,3},{4,12},{12,4},... | collective-permute-start | bytes 1572872 | tf_op jit(solution)/shard_map/ppermute | solution.py:597
  (97 other events, 890.4 us)
Sparse Core Ops, SparseCore 0:
  241.8 94.9 reduce-scatter.5
  340.0 87.3 reduce-scatter.7
  430.4 110.1 reduce-scatter.3

commit v5 on v3

--- a/solution.py
+++ b/solution.py
@@ -474,7 +474,7 @@
     for part in (1, 0):
         at = slice(part * half, (part + 1) * half)
         act_grad = dot_last(rows_ref[at, :], wd_ref[...])
-        gate, up = gate_ref[at, :], up_ref[at, :]
+        gate, up = gate_ref[at, :].astype(f32), up_ref[at, :].astype(f32)
         sig = jax.nn.sigmoid(gate)
         up_low = (act_grad * gate * sig).astype(bf16)
         gate_low = (act_grad * up * sig * (1.0 + gate * (1.0 - sig))).astype(bf16)
@@ -798,9 +798,11 @@
     hidden = rows_in.astype(f32) + branch * attn_inv * attention_gain
     hidden_whole = gather(hidden.astype(bf16))
     gate_value = jnp.einsum("rd,df->rf", hidden_whole, wg, preferred_element_type=f32)
+    gate_value = gate_value.astype(bf16)
     up_value = jnp.einsum("rd,df->rf", hidden_whole, wu, preferred_element_type=f32)
-    sigmoid_value = jax.nn.sigmoid(gate_value)
-    act_low = (gate_value * sigmoid_value * up_value).astype(bf16)
+    gate_wide = gate_value.astype(f32)
+    act_low = (gate_wide * jax.nn.sigmoid(gate_wide) * up_value).astype(bf16)
+    up_value = up_value.astype(bf16)
     down_value = scatter(*times(act_low, wd, "rf,fd->rd"))
     feed_inv = rms_scale(down_value)
     down_low = norm_back(down_value, feed_inv, feed_gain, grad_top).astype(bf16)

time: 615 us -> 611 us (level)
    unnamed x127 -> x131, local copies, waits for them, and re-layouts: 17 us -> 17 us
where the time goes in v5:
time: 611 us; the launch traced here: 607 us
  waiting for transfers between devices  268 us (44%)
  Pallas kernels  130 us (21%)
  starting transfers between devices  72.7 us (12%)
  other arithmetic  54.5 us (9%)
  local copies, waits for them, and re-layouts  33.6 us (5%)
  matrix products  32.3 us (5%)
  between operations  15.4 us (3%)
    ppermute x67, waiting for transfers between devices, swap(): return lax.ppermute(v, name, ((0, 1), (1, 0)))  175 us
    pallas_call x9, Pallas kernels, grads(): pl.pallas_call(lambda *refs: grads_kernel(len(terms), *refs), grid_spec=p...  60.3 us
    ppermute x67, starting transfers between devices, swap(): return lax.ppermute(v, name, ((0, 1), (1, 0)))  46.3 us
    ppermute x3, waiting for transfers between devices, swap_zy(): return lax.ppermute(v, ('zl', 'y'), ((0, 3), (3, 0), (1, 2), (2, 1)))  41.6 us
    reduce_scatter x3, waiting for transfers between devices, whole_sum(): return lax.psum_scatter(v, ('zh', 'x'), scatter_dimension=0, tiled=True)  40 us
    pallas_call x1, Pallas kernels, grouped(): pl.pallas_call(feed_back_kernel, grid_spec=pltpu.PrefetchScalarGridSpec(n...  25 us
    pallas_call x4, Pallas kernels, assemble(): pl.pallas_call(lambda *refs: assemble_kernel(moves, *refs), in_specs=[pl....  17.4 us
    unnamed x131, local copies, waits for them, and re-layouts  17 us
  transfers between devices with their start and end apart: 77, of which 47 were waited for; matrix products, arithmetic and copies ran while one was open for 12% of the time, Pallas kernels for 16%

profile of v5, /device:TPU:0, one launch (start us, length us, event | category | flops | bytes accessed | tf_op | source)
XLA Modules:
  0.0 606.5 jit_solution(8454769767158205880)
XLA Ops:
  9.5 6.2 %all-to-all-start = ((bf16[4,32,2048]{2,1,0:T(8,128)(2,1)}), bf16[4,32,2048]{2,1,0:T(8,128)(2,1)S(1)}, u32[]{:S(2)}, u32[]{:S(2)}) async-start(bf16[4,32,2048]{2,1,0:T(8,128)(2,1)} %bitcast.125), calls=%async_computation | async-start | bytes 1048576 | tf_op jit(solution)/shard_map/all_to_all | solution.py:600
  18.6 11.6 %all-to-all-done = bf16[4,32,2048]{2,1,0:T(8,128)(2,1)S(1)} async-done(((bf16[4,32,2048]{2,1,0:T(8,128)(2,1)}), bf16[4,32,2048]{2,1,0:T(8,128)(2,1)S(1)}, u32[]{:S(2)}, u32[]{:S(2)}) %all-to-all-start) | async-done | bytes 524320 | tf_op jit(solution)/shard_map/all_to_all | solution.py:600
  32.0 5.5 collective-permute-done
  45.7 5.1 all-to-all-start.1
  59.2 4.3 assemble.4.refs_1_
  63.7 6.1 %fusion.50 = f32[1024,768]{1,0:T(8,128)S(1)} fusion(bf16[1024,2048]{1,0:T(8,128)(2,1)} %assemble.4.refs_1_, bf16[2048,256]{1,0:T(8,128)(2,1)S(1)} %copy-done.26, bf16[2048,256]{1,0:T(8,128)(2,1)S(1)} %constant_dynamic-slice_fusion.2, bf16[2048,256]{1,0:T(8,128)(2,1)} %constant_dynamic-slice_fusion.3), kind=kOutput, calls=%fused_computation.180 | convolution fusion | flops 3230662656 | bytes 10485760 | tf_op jit(solution)/shard_map/rd,dh->rh/dot_general | solution.py:772
  84.1 12.9 %attend.1 = (bf16[2,2,256,256]{3,2,1,0:T(8,128)(2,1)}, f32[2,2,256,256]{3,2,1,0:T(8,128)}, f32[2,2,256,2]{3,2,1,0:T(8,128)}, bf16[2,2,256,256]{3,2,1,0:T(8,128)(...) custom-call(f32[2,2,256,768]{3,2,1,0:T(8,128)} %bitcast.126, f32[2,2,256,2]{3,2,1,0:T(8,128)} %bitcast.146, ...), custom_call_target="tpu_custom_call" | custom-call | tf_op jit(solution)/shard_map/attend/pallas_call | solution.py:782
  106.0 12.3 %collective-permute-done.13 = bf16[128,2048]{1,0:T(8,128)(2,1)S(1)} collective-permute-done((bf16[128,2048]{1,0:T(8,128)(2,1)S(1)}, bf16[128,2048]{1,0:T(8,128)(2,1)S(1)}, u32[]{:S(2)}, u32[]{:S(2)}) %collective-permute-start.13) | collective-permute-done | bytes 524320 | tf_op jit(solution)/shard_map/ppermute | solution.py:597
  122.0 4.1 collective-permute-done.15
  131.1 4.2 collective-permute-done.17
  139.6 7.7 %collective-permute-done.19.refs_1_ = bf16[128,2048]{1,0:T(8,128)(2,1)S(1)} collective-permute-done((bf16[128,2048]{1,0:T(8,128)(2,1)S(1)}, bf16[128,2048]{1,0:T(8,128)(2,1)S(1)}, u32[]{:S(2)}, u32[]{:S(2)}) %collective-permute-start.19) | collective-permute-done | bytes 524320 | tf_op jit(solution)/shard_map/ppermute | solution.py:597
  152.1 4.4 assemble.5.refs_1_
  156.6 8.1 %fusion.19.gate_ref = bf16[1024,1024]{1,0:T(8,128)(2,1)S(1)} fusion(bf16[1024,2048]{1,0:T(8,128)(2,1)} %assemble.5.refs_1_, bf16[2048,2048]{1,0:T(8,128)(2,1)} %wg_ref, s32[]{:T(128)S(6)} %select_n.119), kind=kOutput, calls=%fused_computation.34 | convolution fusion | flops 4296015872 | bytes 10485764 | tf_op jit(solution)/shard_map/rd,df->rf/dot_general | solution.py:800
  164.7 6.6 %fusion.53 = (bf16[1024,1024]{1,0:T(8,128)(2,1)}, bf16[1024,1024]{1,0:T(8,128)(2,1)S(1)}) fusion(bf16[1024,1024]{1,0:T(8,128)(2,1)S(1)} %fusion.19.gate_ref, bf16[1024,2048]{1,0:T(8,128)(2,1)S(1)} %copy-done.2, bf16[2048,2048]{1,0:T(8,128)(2,1)S(1)} %bitcast.130, s32[]{:T(128)S(6)} %select_n.119), kind=kOutput, calls=%fused_computation.183 | convolution fusion | flops 4303355904 | bytes 14680068 | tf_op jit(solution)/shard_map/rd,df->rf/dot_general | solution.py:802
  181.5 11.5 %collective-permute-done.27 = bf16[128,2048]{1,0:T(8,128)(2,1)S(1)} collective-permute-done((bf16[128,2048]{1,0:T(8,128)(2,1)S(1)}, bf16[128,2048]{1,0:T(8,128)(2,1)S(1)}, u32[]{:S(2)}, u32[]{:S(2)}) %collective-permute-start.27) | collective-permute-done | bytes 524320 | tf_op jit(solution)/shard_map/ppermute | solution.py:597
  197.0 4.4 collective-permute-done.29
  205.3 4.7 collective-permute-done.31
  211.9 5.6 all-to-all-start.2
  220.0 13.4 %collective-permute-done.33.refs_1_ = bf16[128,2048]{1,0:T(8,128)(2,1)S(1)} collective-permute-done((bf16[128,2048]{1,0:T(8,128)(2,1)S(1)}, bf16[128,2048]{1,0:T(8,128)(2,1)S(1)}, u32[]{:S(2)}, u32[]{:S(2)}) %collective-permute-start.33) | collective-permute-done | bytes 524320 | tf_op jit(solution)/shard_map/ppermute | solution.py:597
  236.4 4.3 assemble.6.refs_1_.rows_ref
  240.7 10.9 %grads.9 = bf16[2048,1024]{1,0:T(8,128)(2,1)} custom-call(s32[8]{0:T(128)} %add_xor_fusion.refs_0_, bf16[1024,2048]{1,0:T(8,128)(2,1)} %assemble.6.refs_1_.rows_ref, bf16[1024,1024]{1,0:T(8,128)(2,1)} %copy-done.21), custom_call_target="tpu_custom_call" | custom-call | tf_op jit(solution)/shard_map/grads/pallas_call | solution.py:514
  251.7 25.0 %feed_back.1 = (bf16[1024,1024]{1,0:T(8,128)(2,1)}, bf16[1024,1024]{1,0:T(8,128)(2,1)}, bf16[512,2048]{1,0:T(8,128)(2,1)}, bf16[256,2048]{1,0:T(8,128)(2,1)}, bf16[256,2048]{1,0:T(8,128)(2,1)}) custom-call(s32[1]{0:T(128)} %bitcast.31.zl_ref, bf16[1024,2048]{1,0:T(8,128)(2,1)} %assemble.6.refs_1_.rows_ref, bf16[2048,2048]{1,0:T(8,128)(2,1)} %wg_ref, ...), custom_call_target="tpu_custom_call" | custom-call | tf_op jit(solution)/shard_map/feed_back/pallas_call | solution.py:822
  290.3 11.0 %grads.10 = bf16[2048,1024]{1,0:T(8,128)(2,1)} custom-call(s32[8]{0:T(128)} %add_xor_fusion.refs_0_, bf16[1024,2048]{1,0:T(8,128)(2,1)} %assemble.5.refs_1_, bf16[1024,1024]{1,0:T(8,128)(2,1)} %get-tuple-element.184.refs_2_), custom_call_target="tpu_custom_call" | custom-call | tf_op jit(solution)/shard_map/grads/pallas_call | solution.py:514
  301.3 12.9 %collective-permute-done.42 = bf16[128,2048]{1,0:T(8,128)(2,1)S(1)} collective-permute-done((bf16[128,2048]{1,0:T(8,128)(2,1)}, bf16[128,2048]{1,0:T(8,128)(2,1)S(1)}, u32[]{:S(2)}, u32[]{:S(2)}) %collective-permute-start.42) | collective-permute-done | bytes 524320 | tf_op jit(solution)/shard_map/ppermute | solution.py:597
  314.2 12.5 %collective-permute-done.43 = bf16[128,2048]{1,0:T(8,128)(2,1)} collective-permute-done((bf16[128,2048]{1,0:T(8,128)(2,1)}, bf16[128,2048]{1,0:T(8,128)(2,1)}, u32[]{:S(2)}, u32[]{:S(2)}) %collective-permute-start.43) | collective-permute-done | bytes 524320 | tf_op jit(solution)/shard_map/ppermute | solution.py:638
  329.5 3.2 collective-permute-start.46
  332.7 9.7 %collective-permute-done.44.refs_1_ = bf16[128,2048]{1,0:T(8,128)(2,1)S(1)} collective-permute-done((bf16[128,2048]{1,0:T(8,128)(2,1)S(1)}, bf16[128,2048]{1,0:T(8,128)(2,1)S(1)}, u32[]{:S(2)}, u32[]{:S(2)}) %collective-permute-start.44) | collective-permute-done | bytes 524320 | tf_op jit(solution)/shard_map/ppermute | solution.py:597
  342.4 6.3 %collective-permute-done.45.refs_2_ = bf16[128,2048]{1,0:T(8,128)(2,1)S(1)} collective-permute-done((bf16[128,2048]{1,0:T(8,128)(2,1)S(1)}, bf16[128,2048]{1,0:T(8,128)(2,1)S(1)}, u32[]{:S(2)}, u32[]{:S(2)}) %collective-permute-start.45) | collective-permute-done | bytes 524320 | tf_op jit(solution)/shard_map/ppermute | solution.py:597
  348.6 16.0 %collective-permute-done.46.refs_3_ = bf16[128,2048]{1,0:T(8,128)(2,1)S(1)} collective-permute-done((bf16[128,2048]{1,0:T(8,128)(2,1)S(1)}, bf16[128,2048]{1,0:T(8,128)(2,1)S(1)}, u32[]{:S(2)}, u32[]{:S(2)}) %collective-permute-start.46) | collective-permute-done | bytes 524320 | tf_op jit(solution)/shard_map/ppermute | solution.py:638
  366.0 11.2 %grads.11 = bf16[2048,1024]{1,0:T(8,128)(2,1)} custom-call(s32[8]{0:T(128)} %add_xor_fusion.refs_0_, bf16[1024,2048]{1,0:T(8,128)(2,1)} %assemble.5.refs_1_, bf16[1024,1024]{1,0:T(8,128)(2,1)} %get-tuple-element.200.refs_2_), custom_call_target="tpu_custom_call" | custom-call | tf_op jit(solution)/shard_map/grads/pallas_call | solution.py:514
  377.3 4.3 assemble.7.rows_ref.refs_1_
  381.6 4.3 mixed_back.1
  385.9 10.1 %attend_back.1 = (f32[2,2,256,256]{3,2,1,0:T(8,128)}, f32[2,2,256,256]{3,2,1,0:T(8,128)}, bf16[2,2,256,256]{3,2,1,0:T(8,128)(2,1)}) custom-call(bf16[2,2,256,256]{3,2,1,0:T(8,128)(2,1)} %get-tuple-element.186.refs_0_, bf16[2,2,256,256]{3,2,1,0:T(8,128)(2,1)} %get-tuple-element.187.refs_1_, bf16[2,2,256,256]{3,2,1,0:T(8,128)(2,1)} %get-tuple-element.188.refs_2_, ...), custom_call_target="tpu_custom_call" | custom-call | tf_op jit(solution)/shard_map/attend_back/pallas_call | solution.py:878
  400.9 3.4 collective-permute-done.52
  405.2 5.1 grads.12
  429.3 3.0 convolution_convert_fusion.3
  434.6 3.5 collective-permute-done.56
  438.1 6.1 %grads.13 = bf16[1024,768]{1,0:T(8,128)(2,1)} custom-call(s32[4]{0:T(128)} %broadcast_xor_fusion.1.refs_0_, bf16[1024,2048]{1,0:T(8,128)(2,1)} %assemble.4.refs_1_, bf16[1024,768]{1,0:T(8,128)(2,1)} %copy-done.5), custom_call_target="tpu_custom_call" | custom-call | tf_op jit(solution)/shard_map/grads/pallas_call | solution.py:514
  446.6 3.3 grads.14
  457.9 7.2 %collective-permute-done.59 = bf16[128,2048]{1,0:T(8,128)(2,1)S(1)} collective-permute-done((bf16[128,2048]{1,0:T(8,128)(2,1)S(1)}, bf16[128,2048]{1,0:T(8,128)(2,1)S(1)}, u32[]{:S(2)}, u32[]{:S(2)}) %collective-permute-start.59) | collective-permute-done | bytes 524320 | tf_op jit(solution)/shard_map/ppermute | solution.py:597
  465.1 21.2 %collective-permute-done.60 = bf16[128,2048]{1,0:T(8,128)(2,1)S(1)} collective-permute-done((bf16[128,2048]{1,0:T(8,128)(2,1)S(1)}, bf16[128,2048]{1,0:T(8,128)(2,1)S(1)}, u32[]{:S(2)}, u32[]{:S(2)}) %collective-permute-start.60) | collective-permute-done | bytes 524320 | tf_op jit(solution)/shard_map/ppermute | solution.py:597
  486.3 13.1 %collective-permute-done.61 = bf16[128,2048]{1,0:T(8,128)(2,1)S(1)} collective-permute-done((bf16[128,2048]{1,0:T(8,128)(2,1)S(1)}, bf16[128,2048]{1,0:T(8,128)(2,1)S(1)}, u32[]{:S(2)}, u32[]{:S(2)}) %collective-permute-start.61) | collective-permute-done | bytes 524320 | tf_op jit(solution)/shard_map/ppermute | solution.py:638
  500.6 4.6 grads.15
  511.8 40.0 %reduce-scatter.8.cloned.1.call-done = bf16[512,1024]{1,0:T(8,128)(2,1)} async-done(((bf16[2048,1024]{1,0:T(8,128)(2,1)}), bf16[512,1024]{1,0:T(8,128)(2,1)}) %reduce-scatter.8.cloned.1.call-update) | async-done | bytes 1048592 | tf_op jit(solution)/shard_map/reduce_scatter | solution.py:709
  557.8 3.5 all-to-all-start.3
  561.3 4.7 grads.16
  569.8 3.4 grads.17
  574.4 16.0 %collective-permute-done.67 = bf16[256,256]{1,0:T(8,128)(2,1)S(1)} collective-permute-done((bf16[256,256]{1,0:T(8,128)(2,1)S(1)}, bf16[256,256]{1,0:T(8,128)(2,1)S(1)}, u32[]{:S(2)}, u32[]{:S(2)}) %collective-permute-start.67) | collective-permute-done | bytes 131104 | tf_op jit(solution)/shard_map/ppermute | solution.py:597
  (433 shorter events, 172.8 us)
Async XLA Ops:
  9.5 20.7 %all-to-all-start = ((bf16[4,32,2048]{2,1,0:T(8,128)(2,1)}), bf16[4,32,2048]{2,1,0:T(8,128)(2,1)S(1)}, u32[]{:S(2)}, u32[]{:S(2)}) async-start(bf16[4,32,2048]{2,1,0:T(8,128)(2,1)} %bitcast.125), calls=%async_computation | async-start | bytes 1048576 | tf_op jit(solution)/shard_map/all_to_all | solution.py:600
  30.2 7.2 %collective-permute-start = (bf16[64,2048]{1,0:T(8,128)(2,1)S(1)}, bf16[64,2048]{1,0:T(8,128)(2,1)S(1)}, u32[]{:S(2)}, u32[]{:S(2)}) collective-permute-start(bf16[64,2048]{1,0:T(8,128)(2,1)S(1)} %bitcast.151), channel_id=1, source_target_pairs={{0,2},{2,0},{1,3},{3,1},{4,6},{6,4},{5,7},{7,5},{8,10},{10,8},{9,1... | collective-permute-start | bytes 786440 | tf_op jit(solution)/shard_map/ppermute | solution.py:597
  40.8 12.8 %collective-permute-start.2 = (bf16[128,2048]{1,0:T(8,128)(2,1)}, bf16[128,2048]{1,0:T(8,128)(2,1)}, u32[]{:S(2)}, u32[]{:S(2)}) collective-permute-start(bf16[128,2048]{1,0:T(8,128)(2,1)} %get-tuple-element.127.refs_0_), channel_id=1, source_target_pairs={{0,8},{8,0},{1,9},{9,1},{2,10},{10,2},{3,11},{11,3},{4,12},{12,4},... | collective-permute-start | bytes 1572872 | tf_op jit(solution)/shard_map/ppermute | solution.py:597
  41.1 12.5 %collective-permute-start.3 = (bf16[128,2048]{1,0:T(8,128)(2,1)}, bf16[128,2048]{1,0:T(8,128)(2,1)}, u32[]{:S(2)}, u32[]{:S(2)}) collective-permute-start(bf16[128,2048]{1,0:T(8,128)(2,1)} %get-tuple-element.128.refs_2_), channel_id=1, source_target_pairs={{0,2},{2,0},{1,3},{3,1},{4,6},{6,4},{5,7},{7,5},{8,10},{10,8},{9,1... | collective-permute-start | bytes 1572872 | tf_op jit(solution)/shard_map/ppermute | solution.py:597
  45.7 18.0 %all-to-all-start.1 = ((bf16[4,32,2048]{2,1,0:T(8,128)(2,1)}), bf16[4,32,2048]{2,1,0:T(8,128)(2,1)S(1)}, u32[]{:S(2)}, u32[]{:S(2)}) async-start(bf16[4,32,2048]{2,1,0:T(8,128)(2,1)} %bitcast.143), calls=%async_computation.1 | async-start | bytes 1048576 | tf_op jit(solution)/shard_map/all_to_all | solution.py:600
  104.2 14.0 %collective-permute-start.13 = (bf16[128,2048]{1,0:T(8,128)(2,1)S(1)}, bf16[128,2048]{1,0:T(8,128)(2,1)S(1)}, u32[]{:S(2)}, u32[]{:S(2)}) collective-permute-start(bf16[128,2048]{1,0:T(8,128)(2,1)S(1)} %slice.337), channel_id=1, source_target_pairs={{0,8},{8,0},{1,9},{9,1},{2,10},{10,2},{3,11},{11,3},{4,12},{12,4},... | collective-permute-start | bytes 1572872 | tf_op jit(solution)/shard_map/ppermute | solution.py:597
  104.4 14.0 %collective-permute-start.14 = (bf16[2,64,2048]{2,1,0:T(8,128)(2,1)S(1)}, bf16[2,64,2048]{2,1,0:T(8,128)(2,1)S(1)}, u32[]{:S(2)}, u32[]{:S(2)}) collective-permute-start(bf16[2,64,2048]{2,1,0:T(8,128)(2,1)S(1)} %slice_bitcast_fusion.3), channel_id=1, source_target_pairs={{0,2},{2,0},{1,3},{3,1},{4,6},{6,4},{5,7},{7,5},{8,10},{10,8},{9,1... | collective-permute-start | bytes 1572872 | tf_op jit(solution)/shard_map/ppermute | solution.py:597
  118.5 7.5 %collective-permute-start.15 = (bf16[64,2048]{1,0:T(8,128)(2,1)S(1)}, bf16[64,2048]{1,0:T(8,128)(2,1)S(1)}, u32[]{:S(2)}, u32[]{:S(2)}) collective-permute-start(bf16[64,2048]{1,0:T(8,128)(2,1)S(1)} %slice.340), channel_id=1, source_target_pairs={{0,2},{2,0},{1,3},{3,1},{4,6},{6,4},{5,7},{7,5},{8,10},{10,8},{9,1... | collective-permute-start | bytes 786440 | tf_op jit(solution)/shard_map/ppermute | solution.py:597
  136.4 10.9 %collective-permute-start.19 = (bf16[128,2048]{1,0:T(8,128)(2,1)S(1)}, bf16[128,2048]{1,0:T(8,128)(2,1)S(1)}, u32[]{:S(2)}, u32[]{:S(2)}) collective-permute-start(bf16[128,2048]{1,0:T(8,128)(2,1)S(1)} %pad_maximum_fusion.7.refs_0_), channel_id=1, source_target_pairs={{0,8},{8,0},{1,9},{9,1},{2,10},{10,2},{3,11},{11,3},{4,12},{12,4},... | collective-permute-start | bytes 1572872 | tf_op jit(solution)/shard_map/ppermute | solution.py:597
  138.5 9.3 %collective-permute-start.20 = (bf16[128,2048]{1,0:T(8,128)(2,1)S(1)}, bf16[128,2048]{1,0:T(8,128)(2,1)}, u32[]{:S(2)}, u32[]{:S(2)}) collective-permute-start(bf16[128,2048]{1,0:T(8,128)(2,1)S(1)} %pad_maximum_fusion.8.refs_2_), channel_id=1, source_target_pairs={{0,2},{2,0},{1,3},{3,1},{4,6},{6,4},{5,7},{7,5},{8,10},{10,8},{9,1... | collective-permute-start | bytes 1572872 | tf_op jit(solution)/shard_map/ppermute | solution.py:597
  179.0 14.0 %collective-permute-start.27 = (bf16[128,2048]{1,0:T(8,128)(2,1)S(1)}, bf16[128,2048]{1,0:T(8,128)(2,1)S(1)}, u32[]{:S(2)}, u32[]{:S(2)}) collective-permute-start(bf16[128,2048]{1,0:T(8,128)(2,1)S(1)} %slice.349), channel_id=1, source_target_pairs={{0,8},{8,0},{1,9},{9,1},{2,10},{10,2},{3,11},{11,3},{4,12},{12,4},... | collective-permute-start | bytes 1572872 | tf_op jit(solution)/shard_map/ppermute | solution.py:597
  180.2 13.8 %collective-permute-start.28 = (bf16[2,64,2048]{2,1,0:T(8,128)(2,1)S(1)}, bf16[2,64,2048]{2,1,0:T(8,128)(2,1)S(1)}, u32[]{:S(2)}, u32[]{:S(2)}) collective-permute-start(bf16[2,64,2048]{2,1,0:T(8,128)(2,1)S(1)} %slice_bitcast_fusion.1), channel_id=1, source_target_pairs={{0,2},{2,0},{1,3},{3,1},{4,6},{6,4},{5,7},{7,5},{8,10},{10,8},{9,1... | collective-permute-start | bytes 1572872 | tf_op jit(solution)/shard_map/ppermute | solution.py:597
  194.1 7.3 %collective-permute-start.29 = (bf16[64,2048]{1,0:T(8,128)(2,1)S(1)}, bf16[64,2048]{1,0:T(8,128)(2,1)S(1)}, u32[]{:S(2)}, u32[]{:S(2)}) collective-permute-start(bf16[64,2048]{1,0:T(8,128)(2,1)S(1)} %slice.352), channel_id=1, source_target_pairs={{0,2},{2,0},{1,3},{3,1},{4,6},{6,4},{5,7},{7,5},{8,10},{10,8},{9,1... | collective-permute-start | bytes 786440 | tf_op jit(solution)/shard_map/ppermute | solution.py:597
  211.9 22.5 %all-to-all-start.2 = ((bf16[4,32,2048]{2,1,0:T(8,128)(2,1)}), bf16[4,32,2048]{2,1,0:T(8,128)(2,1)S(1)}, u32[]{:S(2)}, u32[]{:S(2)}) async-start(bf16[4,32,2048]{2,1,0:T(8,128)(2,1)} %bitcast.144), calls=%async_computation.2 | async-start | bytes 1048576 | tf_op jit(solution)/shard_map/all_to_all | solution.py:605
  217.5 193.1 %reduce-scatter.4.cloned.1.call-start = ((), (), s32[]{:S(2)}) async-start(), calls=%async_computation.7 | async-start | bytes 5242880 | tf_op jit(solution)/shard_map/reduce_scatter | solution.py:709
  217.5 15.8 %collective-permute-start.33 = (bf16[128,2048]{1,0:T(8,128)(2,1)S(1)}, bf16[128,2048]{1,0:T(8,128)(2,1)S(1)}, u32[]{:S(2)}, u32[]{:S(2)}) collective-permute-start(bf16[128,2048]{1,0:T(8,128)(2,1)S(1)} %pad_maximum_fusion.9.refs_0_), channel_id=1, source_target_pairs={{0,8},{8,0},{1,9},{9,1},{2,10},{10,2},{3,11},{11,3},{4,12},{12,4},... | collective-permute-start | bytes 1572872 | tf_op jit(solution)/shard_map/ppermute | solution.py:597
  218.3 15.1 %collective-permute-start.34 = (bf16[128,2048]{1,0:T(8,128)(2,1)S(1)}, bf16[128,2048]{1,0:T(8,128)(2,1)}, u32[]{:S(2)}, u32[]{:S(2)}) collective-permute-start(bf16[128,2048]{1,0:T(8,128)(2,1)S(1)} %pad_maximum_fusion.10.refs_2_), channel_id=1, source_target_pairs={{0,2},{2,0},{1,3},{3,1},{4,6},{6,4},{5,7},{7,5},{8,10},{10,8},{9,1... | collective-permute-start | bytes 1572872 | tf_op jit(solution)/shard_map/ppermute | solution.py:597
  219.5 16.9 %collective-permute-start.35 = (bf16[128,2048]{1,0:T(8,128)(2,1)S(1)}, bf16[128,2048]{1,0:T(8,128)(2,1)}, u32[]{:S(2)}, u32[]{:S(2)}) collective-permute-start(bf16[128,2048]{1,0:T(8,128)(2,1)S(1)} %pad_maximum_fusion.9.refs_0_), channel_id=1, source_target_pairs={{0,1},{1,0},{2,3},{3,2},{4,5},{5,4},{6,7},{7,6},{8,9},{9,8},{10,11... | collective-permute-start | bytes 1572872 | tf_op jit(solution)/shard_map/ppermute | solution.py:597
  219.5 16.9 %collective-permute-start.38 = (bf16[128,2048]{1,0:T(8,128)(2,1)S(1)}, bf16[128,2048]{1,0:T(8,128)(2,1)}, u32[]{:S(2)}, u32[]{:S(2)}) collective-permute-start(bf16[128,2048]{1,0:T(8,128)(2,1)S(1)} %pad_maximum_fusion.10.refs_2_), channel_id=1, source_target_pairs={{0,1},{1,0},{2,3},{3,2},{4,5},{5,4},{6,7},{7,6},{8,9},{9,8},{10,11... | collective-permute-start | bytes 1572872 | tf_op jit(solution)/shard_map/ppermute | solution.py:597
  251.6 249.0 %reduce-scatter.6.cloned.1.call-start = ((), (), s32[]{:S(2)}) async-start(), calls=%async_computation.8 | async-start | bytes 5242880 | tf_op jit(solution)/shard_map/reduce_scatter | solution.py:709
  285.1 16.2 %collective-permute-start.41 = (bf16[128,2048]{1,0:T(8,128)(2,1)}, bf16[128,2048]{1,0:T(8,128)(2,1)S(1)}, u32[]{:S(2)}, u32[]{:S(2)}) collective-permute-start(bf16[128,2048]{1,0:T(8,128)(2,1)} %pad_maximum_fusion.11), channel_id=1, source_target_pairs={{0,2},{2,0},{1,3},{3,1},{4,6},{6,4},{5,7},{7,5},{8,10},{10,8},{9,1... | collective-permute-start | bytes 1572872 | tf_op jit(solution)/shard_map/ppermute | solution.py:597
  286.7 27.5 %collective-permute-start.42 = (bf16[128,2048]{1,0:T(8,128)(2,1)}, bf16[128,2048]{1,0:T(8,128)(2,1)S(1)}, u32[]{:S(2)}, u32[]{:S(2)}) collective-permute-start(bf16[128,2048]{1,0:T(8,128)(2,1)} %pad_maximum_fusion.12), channel_id=1, source_target_pairs={{0,8},{8,0},{1,9},{9,1},{2,10},{10,2},{3,11},{11,3},{4,12},{12,4},... | collective-permute-start | bytes 1572872 | tf_op jit(solution)/shard_map/ppermute | solution.py:597
  288.0 38.6 %collective-permute-start.43 = (bf16[128,2048]{1,0:T(8,128)(2,1)}, bf16[128,2048]{1,0:T(8,128)(2,1)}, u32[]{:S(2)}, u32[]{:S(2)}) collective-permute-start(bf16[128,2048]{1,0:T(8,128)(2,1)} %pad_maximum_fusion.13), channel_id=1, source_target_pairs={{0,10},{10,0},{2,8},{8,2},{1,11},{11,1},{3,9},{9,3},{4,14},{14,4},... | collective-permute-start | bytes 1572872 | tf_op jit(solution)/shard_map/ppermute | solution.py:638
  328.5 223.3 %reduce-scatter.8.cloned.1.call-start = ((), (), s32[]{:S(2)}) async-start(), calls=%async_computation.9 | async-start | bytes 5242880 | tf_op jit(solution)/shard_map/reduce_scatter | solution.py:709
  329.1 13.3 %collective-permute-start.44 = (bf16[128,2048]{1,0:T(8,128)(2,1)S(1)}, bf16[128,2048]{1,0:T(8,128)(2,1)S(1)}, u32[]{:S(2)}, u32[]{:S(2)}) collective-permute-start(bf16[128,2048]{1,0:T(8,128)(2,1)S(1)} %subtract_convert_fusion.1.refs_0_), channel_id=1, source_target_pairs={{0,2},{2,0},{1,3},{3,1},{4,6},{6,4},{5,7},{7,5},{8,10},{10,8},{9,1... | collective-permute-start | bytes 1572872 | tf_op jit(solution)/shard_map/ppermute | solution.py:597
  329.5 19.2 %collective-permute-start.45 = (bf16[128,2048]{1,0:T(8,128)(2,1)S(1)}, bf16[128,2048]{1,0:T(8,128)(2,1)S(1)}, u32[]{:S(2)}, u32[]{:S(2)}) collective-permute-start(bf16[128,2048]{1,0:T(8,128)(2,1)S(1)} %subtract_convert_fusion.1.refs_0_), channel_id=1, source_target_pairs={{0,8},{8,0},{1,9},{9,1},{2,10},{10,2},{3,11},{11,3},{4,12},{12,4},... | collective-permute-start | bytes 1572872 | tf_op jit(solution)/shard_map/ppermute | solution.py:597
  329.5 35.2 %collective-permute-start.46 = (bf16[128,2048]{1,0:T(8,128)(2,1)S(1)}, bf16[128,2048]{1,0:T(8,128)(2,1)S(1)}, u32[]{:S(2)}, u32[]{:S(2)}) collective-permute-start(bf16[128,2048]{1,0:T(8,128)(2,1)S(1)} %subtract_convert_fusion.1.refs_0_), channel_id=1, source_target_pairs={{0,10},{10,0},{2,8},{8,2},{1,11},{11,1},{3,9},{9,3},{4,14},{14,4},... | collective-permute-start | bytes 1572872 | tf_op jit(solution)/shard_map/ppermute | solution.py:638
  332.7 32.0 %collective-permute-start.47 = (bf16[128,2048]{1,0:T(8,128)(2,1)S(1)}, bf16[128,2048]{1,0:T(8,128)(2,1)S(1)}, u32[]{:S(2)}, u32[]{:S(2)}) collective-permute-start(bf16[128,2048]{1,0:T(8,128)(2,1)S(1)} %subtract_convert_fusion.1.refs_0_), channel_id=1, source_target_pairs={{0,1},{1,0},{2,3},{3,2},{4,5},{5,4},{6,7},{7,6},{8,9},{9,8},{10,11... | collective-permute-start | bytes 1572872 | tf_op jit(solution)/shard_map/ppermute | solution.py:597
  364.7 12.5 %collective-permute-start.48 = (bf16[128,2048]{1,0:T(8,128)(2,1)S(1)}, bf16[128,2048]{1,0:T(8,128)(2,1)}, u32[]{:S(2)}, u32[]{:S(2)}) collective-permute-start(bf16[128,2048]{1,0:T(8,128)(2,1)S(1)} %collective-permute-done.44.refs_1_), channel_id=1, source_target_pairs={{0,1},{1,0},{2,3},{3,2},{4,5},{5,4},{6,7},{7,6},{8,9},{9,8},{10,11... | collective-permute-start | bytes 1572872 | tf_op jit(solution)/shard_map/ppermute | solution.py:597
  365.5 11.7 %collective-permute-start.49 = (bf16[128,2048]{1,0:T(8,128)(2,1)S(1)}, bf16[128,2048]{1,0:T(8,128)(2,1)}, u32[]{:S(2)}, u32[]{:S(2)}) collective-permute-start(bf16[128,2048]{1,0:T(8,128)(2,1)S(1)} %collective-permute-done.45.refs_2_), channel_id=1, source_target_pairs={{0,1},{1,0},{2,3},{3,2},{4,5},{5,4},{6,7},{7,6},{8,9},{9,8},{10,11... | collective-permute-start | bytes 1572872 | tf_op jit(solution)/shard_map/ppermute | solution.py:597
  365.6 11.6 %collective-permute-start.50 = (bf16[128,2048]{1,0:T(8,128)(2,1)S(1)}, bf16[128,2048]{1,0:T(8,128)(2,1)}, u32[]{:S(2)}, u32[]{:S(2)}) collective-permute-start(bf16[128,2048]{1,0:T(8,128)(2,1)S(1)} %collective-permute-done.46.refs_3_), channel_id=1, source_target_pairs={{0,1},{1,0},{2,3},{3,2},{4,5},{5,4},{6,7},{7,6},{8,9},{9,8},{10,11... | collective-permute-start | bytes 1572872 | tf_op jit(solution)/shard_map/ppermute | solution.py:597
  418.7 31.3 %collective-permute-start.57 = (bf16[256,2048]{1,0:T(8,128)(2,1)}, bf16[256,2048]{1,0:T(8,128)(2,1)}, u32[]{:S(2)}, u32[]{:S(2)}) collective-permute-start(bf16[256,2048]{1,0:T(8,128)(2,1)} %get-tuple-element.325), channel_id=1, source_target_pairs={{0,1},{1,0},{2,3},{3,2},{4,5},{5,4},{6,7},{7,6},{8,9},{9,8},{10,11... | collective-permute-start | bytes 3145736 | tf_op jit(solution)/shard_map/ppermute | solution.py:597
  418.7 31.3 %collective-permute-start.58 = (bf16[256,2048]{1,0:T(8,128)(2,1)}, bf16[256,2048]{1,0:T(8,128)(2,1)}, u32[]{:S(2)}, u32[]{:S(2)}) collective-permute-start(bf16[256,2048]{1,0:T(8,128)(2,1)} %get-tuple-element.324), channel_id=1, source_target_pairs={{0,1},{1,0},{2,3},{3,2},{4,5},{5,4},{6,7},{7,6},{8,9},{9,8},{10,11... | collective-permute-start | bytes 3145736 | tf_op jit(solution)/shard_map/ppermute | solution.py:597
  419.2 10.1 %collective-permute-start.55 = (f32[4,2048]{1,0:T(4,128)S(1)}, f32[4,2048]{1,0:T(4,128)S(1)}, u32[]{:S(2)}, u32[]{:S(2)}) collective-permute-start(f32[4,2048]{1,0:T(4,128)S(1)} %reshape.359), channel_id=1, source_target_pairs={{0,4},{4,0},{1,5},{5,1},{2,6},{6,2},{3,7},{7,3},{8,12},{12,8},{9,1... | collective-permute-start | bytes 98312 | tf_op jit(solution)/shard_map/ppermute | solution.py:597
  420.8 13.8 %collective-permute-start.54 = (bf16[1024,256]{1,0:T(8,128)(2,1)}, bf16[1024,256]{1,0:T(8,128)(2,1)S(1)}, u32[]{:S(2)}, u32[]{:S(2)}) collective-permute-start(bf16[1024,256]{1,0:T(8,128)(2,1)} %grads.12), channel_id=1, source_target_pairs={{0,4},{4,0},{1,5},{5,1},{2,6},{6,2},{3,7},{7,3},{8,12},{12,8},{9,1... | collective-permute-start | bytes 1572872 | tf_op jit(solution)/shard_map/ppermute | solution.py:597
  423.8 14.3 %collective-permute-start.56 = (bf16[256,1024]{1,0:T(8,128)(2,1)}, bf16[256,1024]{1,0:T(8,128)(2,1)}, u32[]{:S(2)}, u32[]{:S(2)}) collective-permute-start(bf16[256,1024]{1,0:T(8,128)(2,1)} %get-tuple-element.341), channel_id=1, source_target_pairs={{0,8},{8,0},{1,9},{9,1},{2,10},{10,2},{3,11},{11,3},{4,12},{12,4},... | collective-permute-start | bytes 1572872 | tf_op jit(solution)/shard_map/ppermute | solution.py:597
  444.2 56.4 %collective-permute-start.62 = (bf16[1024,768]{1,0:T(8,128)(2,1)}, bf16[1024,768]{1,0:T(8,128)(2,1)}, u32[]{:S(2)}, u32[]{:S(2)}) collective-permute-start(bf16[1024,768]{1,0:T(8,128)(2,1)} %grads.13), channel_id=1, source_target_pairs={{0,4},{4,0},{1,5},{5,1},{2,6},{6,2},{3,7},{7,3},{8,12},{12,8},{9,1... | collective-permute-start | bytes 4718600 | tf_op jit(solution)/shard_map/ppermute | solution.py:597
  445.7 61.8 %collective-permute-start.69 = (f32[4,2048]{1,0:T(4,128)S(1)}, f32[4,2048]{1,0:T(4,128)S(1)}, u32[]{:S(2)}, u32[]{:S(2)}) collective-permute-start(f32[4,2048]{1,0:T(4,128)S(1)} %add.242), channel_id=1, source_target_pairs={{0,16},{16,0},{1,17},{17,1},{2,18},{18,2},{3,19},{19,3},{4,20},{20... | collective-permute-start | bytes 98312 | tf_op jit(solution)/shard_map/ppermute | solution.py:597
  452.6 12.5 %collective-permute-start.59 = (bf16[128,2048]{1,0:T(8,128)(2,1)S(1)}, bf16[128,2048]{1,0:T(8,128)(2,1)S(1)}, u32[]{:S(2)}, u32[]{:S(2)}) collective-permute-start(bf16[128,2048]{1,0:T(8,128)(2,1)S(1)} %pad_maximum_fusion.14), channel_id=1, source_target_pairs={{0,2},{2,0},{1,3},{3,1},{4,6},{6,4},{5,7},{7,5},{8,10},{10,8},{9,1... | collective-permute-start | bytes 1572872 | tf_op jit(solution)/shard_map/ppermute | solution.py:597
  453.4 32.9 %collective-permute-start.60 = (bf16[128,2048]{1,0:T(8,128)(2,1)S(1)}, bf16[128,2048]{1,0:T(8,128)(2,1)S(1)}, u32[]{:S(2)}, u32[]{:S(2)}) collective-permute-start(bf16[128,2048]{1,0:T(8,128)(2,1)S(1)} %pad_maximum_fusion.15), channel_id=1, source_target_pairs={{0,8},{8,0},{1,9},{9,1},{2,10},{10,2},{3,11},{11,3},{4,12},{12,4},... | collective-permute-start | bytes 1572872 | tf_op jit(solution)/shard_map/ppermute | solution.py:597
  455.9 43.4 %collective-permute-start.61 = (bf16[128,2048]{1,0:T(8,128)(2,1)S(1)}, bf16[128,2048]{1,0:T(8,128)(2,1)S(1)}, u32[]{:S(2)}, u32[]{:S(2)}) collective-permute-start(bf16[128,2048]{1,0:T(8,128)(2,1)S(1)} %pad_maximum_fusion.16), channel_id=1, source_target_pairs={{0,10},{10,0},{2,8},{8,2},{1,11},{11,1},{3,9},{9,3},{4,14},{14,4},... | collective-permute-start | bytes 1572872 | tf_op jit(solution)/shard_map/ppermute | solution.py:638
  505.2 51.7 %collective-permute-start.63 = (bf16[512,768]{1,0:T(8,128)(2,1)}, bf16[512,768]{1,0:T(8,128)(2,1)}, u32[]{:S(2)}, u32[]{:S(2)}) collective-permute-start(bf16[512,768]{1,0:T(8,128)(2,1)} %grads.15), channel_id=1, source_target_pairs={{0,16},{16,0},{1,17},{17,1},{2,18},{18,2},{3,19},{19,3},{4,20},{20... | collective-permute-start | bytes 2359304 | tf_op jit(solution)/shard_map/ppermute | solution.py:597
  506.5 47.5 %collective-permute-start.64 = (bf16[256,1024]{1,0:T(8,128)(2,1)}, bf16[256,1024]{1,0:T(8,128)(2,1)}, u32[]{:S(2)}, u32[]{:S(2)}) collective-permute-start(bf16[256,1024]{1,0:T(8,128)(2,1)} %get-tuple-element.339), channel_id=1, source_target_pairs={{0,8},{8,0},{1,9},{9,1},{2,10},{10,2},{3,11},{11,3},{4,12},{12,4},... | collective-permute-start | bytes 1572872 | tf_op jit(solution)/shard_map/ppermute | solution.py:597
  508.1 61.7 %collective-permute-start.65 = (bf16[512,256]{1,0:T(8,128)(2,1)S(1)}, bf16[512,256]{1,0:T(8,128)(2,1)}, u32[]{:S(2)}, u32[]{:S(2)}) collective-permute-start(bf16[512,256]{1,0:T(8,128)(2,1)S(1)} %copy-done.50), channel_id=1, source_target_pairs={{0,16},{16,0},{1,17},{17,1},{2,18},{18,2},{3,19},{19,3},{4,20},{20... | collective-permute-start | bytes 786440 | tf_op jit(solution)/shard_map/ppermute | solution.py:597
  554.0 37.5 %collective-permute-start.68 = (bf16[256,1024]{1,0:T(8,128)(2,1)}, bf16[256,1024]{1,0:T(8,128)(2,1)}, u32[]{:S(2)}, u32[]{:S(2)}) collective-permute-start(bf16[256,1024]{1,0:T(8,128)(2,1)} %get-tuple-element.337), channel_id=1, source_target_pairs={{0,8},{8,0},{1,9},{9,1},{2,10},{10,2},{3,11},{11,3},{4,12},{12,4},... | collective-permute-start | bytes 1572872 | tf_op jit(solution)/shard_map/ppermute | solution.py:597
  557.8 40.2 %all-to-all-start.3 = ((bf16[4,32,2048]{2,1,0:T(8,128)(2,1)}), bf16[4,32,2048]{2,1,0:T(8,128)(2,1)S(1)}, u32[]{:S(2)}, u32[]{:S(2)}) async-start(bf16[4,32,2048]{2,1,0:T(8,128)(2,1)} %bitcast.142), calls=%async_computation.5 | async-start | bytes 1048576 | tf_op jit(solution)/shard_map/all_to_all | solution.py:605
  567.8 26.5 %collective-permute-start.66 = (bf16[256,768]{1,0:T(8,128)(2,1)}, bf16[256,768]{1,0:T(8,128)(2,1)}, u32[]{:S(2)}, u32[]{:S(2)}) collective-permute-start(bf16[256,768]{1,0:T(8,128)(2,1)} %get-tuple-element.359), channel_id=1, source_target_pairs={{0,8},{8,0},{1,9},{9,1},{2,10},{10,2},{3,11},{11,3},{4,12},{12,4},... | collective-permute-start | bytes 1179656 | tf_op jit(solution)/shard_map/ppermute | solution.py:597
  574.2 16.2 %collective-permute-start.67 = (bf16[256,256]{1,0:T(8,128)(2,1)S(1)}, bf16[256,256]{1,0:T(8,128)(2,1)S(1)}, u32[]{:S(2)}, u32[]{:S(2)}) collective-permute-start(bf16[256,256]{1,0:T(8,128)(2,1)S(1)} %get-tuple-element.375), channel_id=1, source_target_pairs={{0,8},{8,0},{1,9},{9,1},{2,10},{10,2},{3,11},{11,3},{4,12},{12,4},... | collective-permute-start | bytes 393224 | tf_op jit(solution)/shard_map/ppermute | solution.py:597
  (92 other events, 896.6 us)
Sparse Core Ops, SparseCore 0:
  251.7 87.1 reduce-scatter.3
  342.1 86.0 reduce-scatter.5
  431.2 120.5 reduce-scatter.7
